TPU v7x, 32 devices: a whole 2x2x4 slice. The times are simulated.
32 devices in a mesh: dp: 8 (over z, x), th: 2 (over core), tw: 2 (over y).
Axes of the slice: x: 2, y: 2, z: 4, core: 2. Of those that a mesh axis runs over, the one named last changes fastest.
Arguments:
- tokens: bfloat16 [16, 1536, 768], P('dp', ('th', 'tw')), may hold values from -6 to 6
- segment_ids: int32 [16, 1536], P('dp'), may hold values from 0 to 7, never falling along the last dimension, each value on 1 to 768 neighbouring positions
- norm1_gain: float32 [768], replicated, may hold values from 0.5 to 1.5
- norm1_shift: float32 [768], replicated, may hold values from -3 to 3
- w_qkv: bfloat16 [3, 768, 768], P(None, None, ('th', 'tw')), may hold values from -0.21875 to 0.21875
- b_qv: float32 [2, 768], P(None, ('th', 'tw')), may hold values from -3 to 3
- w_out: bfloat16 [768, 768], P(('th', 'tw')), may hold values from -0.875 to 0.875
- b_out: float32 [768], replicated, may hold values from -3 to 3
- norm2_gain: float32 [768], replicated, may hold values from 0.5 to 1.5
- norm2_shift: float32 [768], replicated, may hold values from -3 to 3
- w_up: bfloat16 [768, 3072], replicated, may hold values from -0.21875 to 0.21875
- b_up: float32 [3072], replicated, may hold values from -3 to 3
- w_down: bfloat16 [3072, 768], replicated, may hold values from -0.109375 to 0.109375
- b_down: float32 [768], replicated, may hold values from -3 to 3
- cotangent: bfloat16 [16, 1536, 768], P('dp', ('th', 'tw')), may hold values from -6 to 6
Outputs:
- block_out: bfloat16 [16, 1536, 768], P('dp', ('th', 'tw'))
- grad_tokens: bfloat16 [16, 1536, 768], P('dp', ('th', 'tw'))
- grad_norm1_gain: float32 [768], replicated
- grad_norm1_shift: float32 [768], replicated
- grad_w_qkv: float32 [3, 768, 768], P(None, None, ('th', 'tw'))
- grad_b_qv: float32 [2, 768], P(None, ('th', 'tw'))
- grad_w_out: float32 [768, 768], P(('th', 'tw'))
- grad_b_out: float32 [768], replicated
- grad_norm2_gain: float32 [768], replicated
- grad_norm2_shift: float32 [768], replicated
- grad_w_up: float32 [768, 3072], replicated
- grad_b_up: float32 [3072], replicated
- grad_w_down: float32 [3072, 768], replicated
- grad_b_down: float32 [768], replicated
Inputs may be any that keep to these rules, and one draw needn't show every extreme that they name: `segment_ids`: within each row the ids never fall, and one image holds 1 to 768 tokens.
All inputs are finite; a program needn't handle non-finite values.
Results may differ from a plain program's by a relative error of at most 0.015.
Values may be sent and summed in bfloat16 or wider, within the bound.
A program may use at most 192 MiB of HBM per device.

v0:
```python
import functools

import jax
import jax.numpy as jnp
from jax import lax
from jax.experimental import pallas as pl
from jax.experimental.pallas import tpu as pltpu
from jax.sharding import PartitionSpec as P

NT=(((1,),(1,)),((),())); NN=(((1,),(0,)),((),())); TN=(((0,),(0,)),((),()))
F32=jnp.float32; BF=jnp.bfloat16
BQ=256; BK=256; HD=64
def dot(a,b,d): return lax.dot_general(a,b,d,preferred_element_type=F32)

def fwd_kernel(lo_ref, hi_ref, q_ref, k_ref, v_ref, mq_ref, mk_ref, o_ref, lse_ref, m_ref, l_ref, acc_ref):
    i=pl.program_id(0)
    pairs=q_ref.shape[1]//128
    lane=lax.broadcasted_iota(jnp.int32,(1,128),1)
    halves=(lane<HD, lane>=HD)
    m_ref[...]=jnp.full(m_ref.shape,-1e30,F32)
    l_ref[...]=jnp.zeros_like(l_ref)
    acc_ref[...]=jnp.zeros_like(acc_ref)
    def body(j,_):
        ks=pl.ds(pl.multiple_of(j*BK,BK),BK)
        mk=mk_ref[ks,:]
        for p in range(pairs):
            cols=slice(p*128,(p+1)*128)
            qx=jnp.concatenate([q_ref[:,cols],mq_ref[...]],1)
            k2=k_ref[ks,cols]; v2=v_ref[ks,cols]
            ps=[]
            for e in range(2):
                h=2*p+e
                kx=jnp.concatenate([jnp.where(halves[e],k2,jnp.zeros_like(k2)),mk],1)
                s=dot(kx,qx,NT)
                m_old=m_ref[h:h+1,:]
                m_new=jnp.maximum(m_old,jnp.max(s,axis=0,keepdims=True))
                alpha=jnp.exp(m_old-m_new)
                pe=jnp.exp(s-m_new)
                l_ref[h:h+1,:]=l_ref[h:h+1,:]*alpha+jnp.sum(pe,axis=0,keepdims=True)
                m_ref[h:h+1,:]=m_new
                acc_ref[h*HD:(h+1)*HD,:]=acc_ref[h*HD:(h+1)*HD,:]*alpha
                ps.append(pe.astype(BF))
            vcat=jnp.concatenate([jnp.where(halves[0],v2,jnp.zeros_like(v2)),jnp.where(halves[1],v2,jnp.zeros_like(v2))],0)
            acc_ref[cols,:]+=dot(vcat,jnp.concatenate(ps,0),TN)
        return 0
    lax.fori_loop(lo_ref[i],hi_ref[i],body,0)
    for p in range(pairs):
        parts=[]
        for e in range(2):
            h=2*p+e
            parts.append(acc_ref[h*HD:(h+1)*HD,:]*(1.0/l_ref[h:h+1,:]))
        o_ref[:,p*128:(p+1)*128]=jnp.concatenate(parts,0).T.astype(BF)
    lse_ref[...]=m_ref[...]+jnp.log(jnp.maximum(l_ref[...],1e-37))

def attn_fwd(q,k,v,mq,mk,lo,hi):
    L,C=q.shape
    return pl.pallas_call(fwd_kernel,
        grid_spec=pltpu.PrefetchScalarGridSpec(num_scalar_prefetch=2,grid=(L//BQ,),
          in_specs=[pl.BlockSpec((BQ,C),lambda i,*_:(i,0)),pl.BlockSpec((L,C),lambda i,*_:(0,0)),pl.BlockSpec((L,C),lambda i,*_:(0,0)),
                    pl.BlockSpec((BQ,128),lambda i,*_:(i,0)),pl.BlockSpec((L,128),lambda i,*_:(0,0))],
          out_specs=[pl.BlockSpec((BQ,C),lambda i,*_:(i,0)),pl.BlockSpec((8,BQ),lambda i,*_:(0,i))],
          scratch_shapes=[pltpu.VMEM((8,BQ),F32),pltpu.VMEM((8,BQ),F32),pltpu.VMEM((C,BQ),F32)]),
        out_shape=[jax.ShapeDtypeStruct((L,C),BF),jax.ShapeDtypeStruct((8,L),F32)],
        name="attention_forward",
    )(lo,hi,q,k,v,mq,mk)

def bwd_kernel(lo_ref, hi_ref, q_ref, k_ref, v_ref, do_ref, o_ref, lse_ref, mq_ref, mk_ref, dq_ref, dk_ref, dv_ref, dk_acc, dv_acc, dq_acc, qcat, docat):
    i=pl.program_id(0); n=pl.num_programs(0)
    C=q_ref.shape[1]; pairs=C//128
    lane=lax.broadcasted_iota(jnp.int32,(1,128),1)
    halves=(lane<HD, lane>=HD)
    @pl.when(i==0)
    def _():
        dk_acc[...]=jnp.zeros_like(dk_acc); dv_acc[...]=jnp.zeros_like(dv_acc)
    dq_acc[...]=jnp.zeros_like(dq_acc)
    sel=(lax.broadcasted_iota(jnp.int32,(8,C),1)//HD==lax.broadcasted_iota(jnp.int32,(8,C),0)).astype(F32)
    delta=lax.dot_general(sel,do_ref[...].astype(F32)*o_ref[...].astype(F32),NT,precision=lax.Precision.HIGHEST,preferred_element_type=F32)
    for p in range(pairs):
        cols=slice(p*128,(p+1)*128)
        for e in range(2):
            q2=q_ref[:,cols]; d2=do_ref[:,cols]
            qcat[p,e*BQ:(e+1)*BQ,:]=jnp.where(halves[e],q2,jnp.zeros_like(q2))
            docat[p,e*BQ:(e+1)*BQ,:]=jnp.where(halves[e],d2,jnp.zeros_like(d2))
    lse=lse_ref[...]
    def body(j,_):
        ks=pl.ds(pl.multiple_of(j*BK,BK),BK)
        mk=mk_ref[ks,:]
        for p in range(pairs):
            cols=slice(p*128,(p+1)*128)
            qx=jnp.concatenate([q_ref[:,cols],mq_ref[...]],1)
            k2=k_ref[ks,cols]; v2=v_ref[ks,cols]; d2=do_ref[:,cols]
            ps=[]; dss=[]; kms=[]
            for e in range(2):
                h=2*p+e
                km=jnp.where(halves[e],k2,jnp.zeros_like(k2)); vm=jnp.where(halves[e],v2,jnp.zeros_like(v2))
                s=dot(jnp.concatenate([km,mk],1),qx,NT)
                pr=jnp.exp(s-lse[h:h+1,:])
                dp=dot(vm,d2,NT)
                ds=pr*(dp-delta[h:h+1,:])
                ps.append(pr.astype(BF)); dss.append(ds.astype(BF)); kms.append(km)
            dv_acc[ks,cols]+=dot(jnp.concatenate(ps,1),docat[p],NN)
            dk_acc[ks,cols]+=dot(jnp.concatenate(dss,1),qcat[p],NN)
            dq_acc[cols,:]+=dot(jnp.concatenate(kms,0),jnp.concatenate(dss,0),TN)
        return 0
    lax.fori_loop(lo_ref[i],hi_ref[i],body,0)
    dq_ref[...]=(dq_acc[...]*0.125).T.astype(BF)
    @pl.when(i==n-1)
    def _():
        dk_ref[...]=dk_acc[...].astype(BF); dv_ref[...]=dv_acc[...].astype(BF)

def attn_bwd(q,k,v,do,o,lse,mq,mk,lo,hi):
    L,C=q.shape
    blk=pl.BlockSpec((BQ,C),lambda i,*_:(i,0)); full=pl.BlockSpec((L,C),lambda i,*_:(0,0))
    return pl.pallas_call(bwd_kernel,
        grid_spec=pltpu.PrefetchScalarGridSpec(num_scalar_prefetch=2,grid=(L//BQ,),
          in_specs=[blk,full,full,blk,blk,pl.BlockSpec((8,BQ),lambda i,*_:(0,i)),pl.BlockSpec((BQ,128),lambda i,*_:(i,0)),pl.BlockSpec((L,128),lambda i,*_:(0,0))],
          out_specs=[blk,full,full],
          scratch_shapes=[pltpu.VMEM((L,C),F32),pltpu.VMEM((L,C),F32),pltpu.VMEM((C,BQ),F32),pltpu.VMEM((C//128,2*BQ,128),BF),pltpu.VMEM((C//128,2*BQ,128),BF)]),
        out_shape=[jax.ShapeDtypeStruct((L,C),BF)]*3,
        name="attention_backward",
    )(lo,hi,q,k,v,do,o,lse,mq,mk)

def block_ranges(seg):
    first=seg[::BQ]; last=seg[BQ-1::BQ]
    lo=jnp.sum(seg[None,:]<first[:,None],axis=1,dtype=jnp.int32)//BK
    hi=(jnp.sum(seg[None,:]<=last[:,None],axis=1,dtype=jnp.int32)+BK-1)//BK
    return lo,hi


TT=256; FC=512
LAG=2; GLAG=2; HLAG=2; HC=3; HSP=2

def bits_of(dp): return dp.bit_length()-1

def big_plan(dp,rows):
    n=bits_of(dp)
    orders=(["tw"]+list(range(n)),[0,"tw"]+list(range(1,n)),[1,2,0,"tw"]+list(range(3,n)))
    unit=16<<(n+1)
    units=rows//unit
    third=max(1,units//4)
    shares=[units-units//3-third,units//3,third]
    return streams(orders,shares,unit)

def head_plan(dp,rows):
    n=bits_of(dp)
    orders=(["tw"]+list(range(n)),[1,2,0,"tw"]+list(range(3,n)))
    unit=16<<n
    units=rows//unit
    low=max(1,units//6)
    return streams(orders,[units-low,low],unit)

def streams(orders,shares,unit):
    out=[]; start=0
    for order,share in zip(orders,shares):
        out.append((order,start,share*unit)); start+=share*unit
    return out

class Peers:
    def __init__(self):
        self.dp=lax.axis_index("dp"); self.th=lax.axis_index("th"); self.tw=lax.axis_index("tw")
    def bit(self,axis):
        return self.tw if axis=="tw" else (self.dp//(1<<axis))%2
    def peer(self,axis):
        if axis=="tw": return {"tw":1-self.tw}
        if axis=="th": return {"th":1-self.th}
        return {"dp":self.dp+(1-2*self.bit(axis))*(1<<axis)}

def send(src,dst,ssem,rsem,peer):
    return pltpu.make_async_remote_copy(src,dst,ssem,rsem,device_id=peer,device_id_type=pl.DeviceIdType.MESH)

def barrier(p,axes):
    sem=pltpu.get_barrier_semaphore()
    for a in axes:
        pl.semaphore_signal(sem,inc=1,device_id=p.peer(a),device_id_type=pl.DeviceIdType.MESH)
    pl.semaphore_wait(sem,len(axes))

def halves(p,order,row,rows,keep_tw=False):
    out=[]
    for axis in order:
        if keep_tw and axis=="tw": out.append((row,row,rows)); continue
        rows//=2; bit=p.bit(axis)
        out.append((row+(1-bit)*rows,row+bit*rows,rows)); row=row+bit*rows
    return out
def al(x): return x if isinstance(x,int) else pl.multiple_of(x,16)
def rows_at(row,n): return pl.ds(al(row),n)

EPS=1e-06
def norm_parts(x):
    mean=jnp.mean(x,axis=-1,keepdims=True)
    cen=x-mean
    r=lax.rsqrt(jnp.mean(cen*cen,axis=-1,keepdims=True)+EPS)
    return cen*r,r
def norm_back(e,n,r,gain):
    t=e*gain
    return r*(t-jnp.mean(t,axis=-1,keepdims=True)-n*jnp.mean(t*n,axis=-1,keepdims=True))
def colsum(x): return jnp.sum(x,axis=0,keepdims=True)

def ffn_kernel(dp,att,wo,x,vin,cot,wu,wd,bu,mine,other,gm,gb,vec,red,gheads,gwo,
               cotT,mid,n2,n2T,bo,gn,obuf,orecv,grow,act,gh,dw,chip_recv,osem,gsem,*rest):
    CH=dw.shape[0]; T,D=x.shape
    plan=big_plan(dp,dw.shape[2]); n=len(plan[0][0]); K=len(plan)
    recv=[rest[k*n:(k+1)*n] for k in range(K)]
    send_sem,recv_sem,chip_send,chip_got=rest[K*n:]
    p=Peers(); g=pl.program_id(0); last=pl.num_programs(0)-1
    tiles=[slice(t*TT,(t+1)*TT) for t in range(T//TT)]
    regs=[halves(p,*s) for s in plan]
    def copy(k,s,c):
        out,_,nr=regs[k][s]
        return send(dw.at[c,p.th,rows_at(out,nr),:],recv[k][s].at[c],send_sem.at[k,s,c],recv_sem.at[k,s,c],p.peer(plan[k][0][s]))
    def chip_copy(c):
        return send(dw.at[c,1-p.th],chip_recv.at[c],chip_send.at[c],chip_got.at[c],p.peer("th"))
    def ocopy(): return send(obuf,orecv,osem.at[0],osem.at[1],p.peer("th"))
    def gcopy(landed):
        ref=grow.at[rows_at((1-p.th if landed else p.th)*T,T),:]
        return send(ref,ref,gsem.at[0],gsem.at[1],p.peer("th"))
    @pl.when(g==0)
    def _():
        barrier(p,["th"]+plan[0][0])
        for r in tiles:
            obuf[r,:]=dot(att[rows_at((1-p.th)*T+r.start,TT),:],wo[...],NN).astype(BF)
        for t,r in enumerate(tiles):
            mid[r,:]=x[r,:].astype(F32)+dot(att[rows_at(p.th*T+r.start,TT),:],wo[...],NN)+vin[0:1,:]
            if t==0: ocopy().start()
            cotT[:,r]=cot[r,:].T
        ocopy().wait_recv()
        for r in tiles:
            m=mid[r,:]+orecv[r,:].astype(F32)
            mid[r,:]=m
            nn,_=norm_parts(m)
            y=(nn*vin[1:2,:]+vin[2:3,:]).astype(BF)
            n2[r,:]=y; n2T[:,r]=y.T
        bo[...]=jnp.zeros_like(bo); gn[...]=jnp.zeros_like(gn)
    for s in reversed(range(n)):
        c=g-1-LAG*(s+1)
        @pl.when((c>=0)&(c<CH))
        def _():
            out=0
            for k in range(K):
                copy(k,s,c).wait_recv()
                _,kr,nr=regs[k][s]
                at=(c,p.th,rows_at(kr,nr),slice(None))
                new=dw[at].astype(F32)+recv[k][s][c].astype(F32)
                if s<n-1: dw[at]=new.astype(BF)
                else:
                    red[c,out:out+nr,:]=new.astype(BF); out+=nr
    for s in reversed(range(n)):
        c=g-1-LAG*s
        @pl.when((c>=0)&(c<CH))
        def _():
            for k in range(K): copy(k,s,c).start()
    @pl.when(g<CH)
    def _():
        gsum=jnp.zeros((1,FC),F32)
        for r in tiles:
            h=dot(n2[r,:],wu[...],NN)+bu[...]
            ga=dot(cot[r,:],wd[...],NT)
            cdf=0.5*(1.0+lax.erf(h*(0.5**0.5)))
            a=(h*cdf).astype(BF)
            gr=(ga*(cdf+h*(jnp.exp(h*h*-0.5)*0.3989422804014327))).astype(BF)
            act[r,:]=a; gh[r,:]=gr
            gsum+=colsum(gr.astype(F32))
        gb[...]=gsum
        for t in range(D//TT):
            r=slice(t*TT,(t+1)*TT)
            for m,(lhs,rhs) in enumerate(((n2T,gh),(cotT,act))):
                y=dot(lhs[r,:],rhs[...],NN).astype(BF)
                for q in range(FC//128): dw[g,m,q*D+t*TT:q*D+(t+1)*TT,:]=y[:,q*128:(q+1)*128]
        for t,r in enumerate(tiles):
            bo[r,:]+=dot(act[r,:],wd[...],NN)
            if t==0: chip_copy(g).start()
            gn[r,:]+=dot(gh[r,:],wu[...],NT)
        chip_copy(g).wait_recv()
        def add(q,_):
            r=rows_at(q*TT,TT)
            dw[g,p.th,r,:]=(dw[g,p.th,r,:].astype(F32)+chip_recv[g,r,:].astype(F32)).astype(BF)
            return 0
        lax.fori_loop(0,dw.shape[2]//TT,add,0)
    @pl.when(g==CH)
    def _():
        vec[...]=jnp.zeros_like(vec)
        for r in tiles:
            m=mid[r,:]
            nn,rs=norm_parts(m)
            e=gn[r,:]; ct=cot[r,:].astype(F32)
            gmid=ct+norm_back(e,nn,rs,vin[1:2,:])
            gm[r,:]=gmid
            gbr=gmid.astype(BF)
            grow[rows_at(p.th*T+r.start,TT),:]=gbr
            vec[0:1,:]+=colsum(gbr.astype(F32)); vec[1:2,:]+=colsum(e*nn); vec[2:3,:]+=colsum(e); vec[3:4,:]+=colsum(ct)
            n2[r,:]=(m+bo[r,:]+vin[3:4,:]).astype(BF)
        gcopy(False).start()
        mine[...]=n2[rows_at(p.tw*(T//2),T//2),:]
        other[...]=n2[rows_at((1-p.tw)*(T//2),T//2),:]
    @pl.when(g==CH+1)
    def _():
        gcopy(True).wait_recv()
        for t in range(2*T//TT):
            r=slice(t*TT,(t+1)*TT)
            gheads[r,:]=dot(grow[r,:],wo[...],NT).astype(BF)
        for t in range(D//TT):
            r=slice(t*TT,(t+1)*TT)
            gwo[r,:]=dot(grow[:,r],att[...],TN).astype(BF)
    @pl.when(g==last)
    def _():
        ocopy().wait_send(); gcopy(False).wait_send()
        def drain(c,_):
            chip_copy(c).wait_send()
            for k in range(K):
                for s in range(n): copy(k,s,c).wait_send()
            return 0
        lax.fori_loop(0,CH,drain,0)

def whole(shape):
    return pl.BlockSpec(shape,lambda g:(0,)*len(shape),pipeline_mode=pl.Buffered(1))

def ffn(dp,att,wo,x,vin,cot,wu,wd,bu):
    T,D=x.shape; FF=wu.shape[1]; CH=FF//FC; R=FC//128*D; C=att.shape[1]
    plan=big_plan(dp,R); n=len(plan[0][0])
    m=lambda c: jnp.minimum(c,CH-1)
    fin=R>>n
    recv=[pltpu.VMEM((CH,rows>>(s+1),128),BF) for _,_,rows in plan for s in range(n)]
    outs=[((T//2,D),BF),((T//2,D),BF),((T,D),F32),((1,FF),F32),((8,D),F32),((CH,fin,128),BF),((2*T,C),BF),((D,C),BF)]
    specs=[whole(o[0]) for o in outs]
    specs[3]=pl.BlockSpec((1,FC),lambda c:(0,m(c)))
    return pl.pallas_call(functools.partial(ffn_kernel,dp),grid=(CH+LAG*n+1,),
      in_specs=[whole(v.shape) for v in (att,wo,x,vin,cot)]+[pl.BlockSpec((D,FC),lambda c:(0,m(c))),pl.BlockSpec((FC,D),lambda c:(m(c),0)),pl.BlockSpec((1,FC),lambda c:(0,m(c)))],
      out_specs=specs,out_shape=[jax.ShapeDtypeStruct(*o) for o in outs],
      scratch_shapes=[pltpu.VMEM((D,T),BF),pltpu.VMEM((T,D),F32),pltpu.VMEM((T,D),BF),pltpu.VMEM((D,T),BF),pltpu.VMEM((T,D),F32),pltpu.VMEM((T,D),F32),
          pltpu.VMEM((T,D),BF),pltpu.VMEM((T,D),BF),pltpu.VMEM((2*T,D),BF)]
        +[pltpu.VMEM((T,FC),BF)]*2+[pltpu.VMEM((CH,2,R,128),BF),pltpu.VMEM((CH,R,128),BF),pltpu.SemaphoreType.DMA((2,)),pltpu.SemaphoreType.DMA((2,))]+recv
        +[pltpu.SemaphoreType.DMA((len(plan),n,CH))]*2+[pltpu.SemaphoreType.DMA((CH,))]*2,
      compiler_params=pltpu.CompilerParams(vmem_limit_bytes=60*2**20,collective_id=0,has_side_effects=True),name="feed_forward")(att,wo,x,vin,cot,wu,wd,bu)

def finish_kernel(dp,red,dq,dk,dv,normT,wh,gwo,x,gain,gm,vec,gbu,up,down,heads_out,vec_out,tok,full,hp,hg,vbuf,vrecv,own,obuf,orecv,tbuf,trecv,osem,tsem,*rest):
    CH=full.shape[0]; R=full.shape[2]; D=up.shape[0]; T=x.shape[0]; C=dq.shape[1]
    tiles=[slice(t*TT,(t+1)*TT) for t in range(T//TT)]
    plan=big_plan(dp,R); n=len(plan[0][0]); K=len(plan)
    HR=hp.shape[2]; hplan=head_plan(dp,HR); HK=len(hplan)
    hrecv=[rest[k*n:(k+1)*n] for k in range(HK)]
    send_sem,recv_sem,chip_send,chip_got,hs_sem,hr_sem,ha_send,ha_recv,vs_sem,vr_sem=rest[HK*n:]
    p=Peers(); g=pl.program_id(0); last=pl.num_programs(0)-1
    regs=[halves(p,*s) for s in plan]
    hregs=[halves(p,*s,keep_tw=True) for s in hplan]
    def gat(k,s,c,landed):
        other,mine,nr=regs[k][s]
        ref=full.at[c,p.th,rows_at(other if landed else mine,nr),:]
        return send(ref,ref,send_sem.at[k,s,c],recv_sem.at[k,s,c],p.peer(plan[k][0][s]))
    def chip(c,landed):
        ref=full.at[c,1-p.th if landed else p.th]
        return send(ref,ref,chip_send.at[c],chip_got.at[c],p.peer("th"))
    def hsum(k,s,c):
        order=hplan[k][0]; other,_,nr=hregs[k][s]
        if order[s]=="tw": src=hp.at[c,pl.ds(1,1),rows_at(other,nr),:]
        elif order.index("tw")>s: src=hp.at[c,:,rows_at(other,nr),:]
        else: src=hp.at[c,pl.ds(0,1),rows_at(other,nr),:]
        return send(src,hrecv[k][s].at[c],hs_sem.at[k,s,c],hr_sem.at[k,s,c],p.peer(order[s]))
    def hgat(k,s,c,landed):
        order=hplan[k][0]; other,mine,nr=hregs[k][s]
        ref=hg.at[c,rows_at(other if landed else mine,nr),:]
        return send(ref,ref,ha_send.at[k,s,c],ha_recv.at[k,s,c],p.peer(order[s]))
    backs=[[s for s in reversed(range(n)) if o[s]!="tw"] for o,_,_ in hplan]
    vaxes=["th","tw"]+list(range(n-1))
    def vcopy(i): return send(vbuf.at[i],vrecv.at[i],vs_sem.at[i],vr_sem.at[i],p.peer(vaxes[i]))
    @pl.when(g==0)
    def _():
        out=0
        for k in range(K):
            _,kr,nr=regs[k][n-1]
            for c in range(CH): full[c,p.th,rows_at(kr,nr),:]=red[c,out:out+nr,:]
            out+=nr
        barrier(p,["th"]+plan[0][0])
    def ocopy(): return send(obuf,orecv,osem.at[0],osem.at[1],p.peer("th"))
    def tcopy(): return send(tbuf.at[rows_at((1-p.tw)*(T//2),T//2),:],trecv,tsem.at[0],tsem.at[1],p.peer("tw"))
    for j in reversed(range(n+1)):
        c=g-GLAG*j
        @pl.when((c>=0)&(c<CH))
        def _():
            if j>0:
                for k in range(K): gat(k,n-j,c,True).wait_recv()
            if j<n:
                for k in range(K): gat(k,n-1-j,c,False).start()
            else: chip(c,False).start()
    @pl.when(g==0)
    def _():
        for r in tiles:
            parts=[dot(normT[r,:],d[...],NN).astype(BF) for d in (dq,dk,dv)]+[gwo[r,:]]
            for q in range(2):
                y=jnp.concatenate([z[:,q*(C//2):(q+1)*(C//2)] for z in parts],1)
                for i in range(y.shape[1]//128):
                    row=i*D+r.start
                    hp[row//HR,q,row%HR:row%HR+TT,:]=y[:,i*128:(i+1)*128]
    @pl.when(g==1)
    def _():
        for half in (1-p.th,p.th):
            for t,r in enumerate(tiles):
                rr=rows_at(half*T+r.start,TT)
                y=dot(dq[rr,:],wh[0],NT)+dot(dk[rr,:],wh[1],NT)+dot(dv[rr,:],wh[2],NT)
                if half is p.th:
                    own[r,:]=y
                    if t==0: ocopy().start()
                else: obuf[r,:]=y.astype(BF)
    @pl.when(g==2)
    def _():
        ocopy().wait_recv()
        vbuf[0]=jnp.zeros(vbuf.shape[1:],F32)
        gsum=jnp.zeros((1,D),F32); ssum=gsum
        for r in tiles:
            e=own[r,:]+orecv[r,:].astype(F32)
            nn,rs=norm_parts(x[r,:].astype(F32))
            tbuf[r,:]=(gm[r,:]+norm_back(e,nn,rs,gain[...])).astype(BF)
            gsum+=colsum(e*nn); ssum+=colsum(e)
        rows=[gsum,ssum]+[vec[i:i+1,:] for i in range(4)]+[gbu[...]]
        at=0
        for v in rows:
            for i in range(v.shape[1]//128):
                vbuf[0,at:at+1,:]=v[:,i*128:(i+1)*128]; at+=1
        for i,d in enumerate((dq,dv)):
            bs=colsum(d[...].astype(F32))
            for q in range(2):
                quarter=2*p.th+(p.tw if q==0 else 1-p.tw)
                y=jnp.concatenate([bs[:,q*(C//2):(q+1)*(C//2)],jnp.zeros((1,256-C//2),F32)],1)
                for z in range(2):
                    vbuf[0,pl.ds(at+quarter*4+i*2+z,1),:]=y[:,z*128:(z+1)*128]
    @pl.when(g==3)
    def _():
        tcopy().start()
        tok[p.tw]=tbuf[rows_at(p.tw*(T//2),T//2),:]
    steps=n+n-1
    for j in range(steps+1):
        for c in range(hp.shape[0]):
            @pl.when(g==1+HSP*c+HLAG*j)
            def _():
                for k in range(HK):
                    order=hplan[k][0]
                    if 0<j<=n:
                        s=j-1
                        hsum(k,s,c).wait_recv()
                        _,kr,nr=hregs[k][s]
                        q=slice(0,2) if order.index("tw")>s else slice(0,1)
                        at=(c,q,rows_at(kr,nr),slice(None))
                        new=(hp[at].astype(F32)+hrecv[k][s][c].astype(F32)).astype(BF)
                        if j<n: hp[at]=new
                        else: hg[c,rows_at(kr,nr),:]=new[0]
                    elif j>n: hgat(k,backs[k][j-n-1],c,True).wait_recv()
                for k in range(HK):
                    if j<n: hsum(k,j,c).start()
                    elif j<steps: hgat(k,backs[k][j-n],c,False).start()
                if j==steps: heads_out[c*HR:(c+1)*HR,:]=hg[c]
    for i in range(len(vaxes)+1):
        @pl.when(g==3+HLAG*i)
        def _():
            if i>0:
                vcopy(i-1).wait_recv()
                x=vbuf[i-1]+vrecv[i-1]
                if i<len(vaxes): vbuf[i]=x
                else: vec_out[...]=x
            if i<len(vaxes): vcopy(i).start()
    c=g-GLAG*(n+1)
    @pl.when((c>=0)&(c<CH))
    def _():
        chip(c,True).wait_recv()
        for q in range(FC//128):
            cols=slice(q*128,(q+1)*128)
            up[:,cols]=full[c,0,q*D:(q+1)*D,:]
            down[:,cols]=full[c,1,q*D:(q+1)*D,:]
    @pl.when(g==last)
    def _():
        def drain(c,_):
            chip(c,False).wait_send()
            for k in range(K):
                for s in range(n): gat(k,s,c,False).wait_send()
            return 0
        lax.fori_loop(0,CH,drain,0)
        for c in range(hp.shape[0]):
            for k in range(HK):
                for s in range(n): hsum(k,s,c).wait_send()
                for s in backs[k]: hgat(k,s,c,False).wait_send()
        for i in range(len(vaxes)): vcopy(i).wait_send()
        ocopy().wait_send(); tcopy().wait()
        tok[1-p.tw]=trecv[...]

def finish(dp,red,dq,dk,dv,normT,wh,gwo,x,gain,gm,vec,gbu):
    T,D=x.shape; CH,fin,_=red.shape; R=FC//128*D
    plan=big_plan(dp,R); n=len(plan[0][0])
    HRA=2*dq.shape[1]//128*D; HR=HRA//HC; hplan=head_plan(dp,HR)
    m=lambda g: jnp.clip(g-GLAG*(n+1),0,CH-1)
    hrecv=[]
    for order,_,rows in hplan:
        q=2
        for axis in order:
            if axis=="tw": q=1
            else: rows//=2
            hrecv.append(pltpu.VMEM((HC,q,rows,128),BF))
    V=(6*D+gbu.shape[1])//128+16; nv=n+1; args=(red,dq,dk,dv,normT,wh,gwo,x,gain,gm,vec,gbu)
    grid=max(CH+GLAG*(n+1),1+HSP*(HC-1)+HLAG*(2*n-1)+1,3+HLAG*nv+1)
    return pl.pallas_call(functools.partial(finish_kernel,dp),grid=(grid,),
      in_specs=[whole(a.shape) for a in args],
      out_specs=[pl.BlockSpec((D,FC),lambda g:(0,m(g)))]*2+[whole((HRA,128)),whole((V,128)),whole((2,T//2,D))],
      out_shape=[jax.ShapeDtypeStruct((D,CH*FC),BF)]*2+[jax.ShapeDtypeStruct((HRA,128),BF),jax.ShapeDtypeStruct((V,128),F32),jax.ShapeDtypeStruct((2,T//2,D),BF)],
      scratch_shapes=[pltpu.VMEM((CH,2,R,128),BF),pltpu.VMEM((HC,2,HR,128),BF),pltpu.VMEM((HC,HR,128),BF),pltpu.VMEM((nv,V,128),F32),pltpu.VMEM((nv,V,128),F32),pltpu.VMEM((T,D),F32)]+[pltpu.VMEM((T,D),BF)]*3+[pltpu.VMEM((T//2,D),BF)]+[pltpu.SemaphoreType.DMA((2,))]*2+hrecv
        +[pltpu.SemaphoreType.DMA((len(plan),n,CH))]*2+[pltpu.SemaphoreType.DMA((CH,))]*2+[pltpu.SemaphoreType.DMA((len(hplan),n,HC))]*4+[pltpu.SemaphoreType.DMA((nv,))]*2,
      compiler_params=pltpu.CompilerParams(vmem_limit_bytes=60*2**20,collective_id=1,has_side_effects=True),name="finish_gradients")(*args)

def widen_kernel(where,up,down,heads,mine,got,wup,wdown,wqkv,wout,blk):
    D=heads.shape[1]; q=wout.shape[0]; g=pl.program_id(0)
    wup[...]=up[...].astype(F32)
    wdown[...]=down[...].astype(F32).T
    @pl.when(g==0)
    def _():
        for r in range(D//TT):
            rr=slice(r*TT,(r+1)*TT)
            y=jnp.concatenate([heads[i,rr,:] for i in range(heads.shape[0])],1).astype(F32)
            for c in range(3): wqkv[c,rr,:]=y[:,c*q:(c+1)*q]
            wout[:,rr]=y[:,3*q:].T
        blk[where[0]]=mine[...]; blk[1-where[0]]=got[...]

def widen(tw,up,down,heads,mine,got):
    D,FF=up.shape; heads=heads.reshape(-1,D,128); q=heads.shape[0]*128//4; T2=mine.shape[0]
    outs=[(D,FF),(FF,D),(3,D,q),(q,D)]
    return pl.pallas_call(widen_kernel,grid=(FF//FC,),
      in_specs=[pl.BlockSpec(memory_space=pltpu.SMEM)]+[pl.BlockSpec((D,FC),lambda g:(0,g))]*2+[whole(a.shape) for a in (heads,mine,got)],
      out_specs=[pl.BlockSpec((D,FC),lambda g:(0,g)),pl.BlockSpec((FC,D),lambda g:(g,0)),whole(outs[2]),whole(outs[3]),whole((2,T2,D))],
      out_shape=[jax.ShapeDtypeStruct(o,F32) for o in outs]+[jax.ShapeDtypeStruct((2,T2,D),BF)],
      compiler_params=pltpu.CompilerParams(vmem_limit_bytes=50*2**20),name="widen")(tw.reshape(1),up,down,heads,mine,got)

def front_kernel(tok,w,b,gain,shift,seg,x_o,normT_o,q_o,k_o,v_o,wh_o,mq_o,mk_o,x,norm,normT,qkv,wh,wgot,bgot,mq,mk,tsem,bsem,csem,ysem,xsem,osem):
    p=Peers(); Q,D=tok.shape[1:]; T=2*Q; L=2*T; E=w.shape[2]; HALF=D//2
    barrier(p,["th","tw",0])
    def tcopy(): return send(tok.at[1-p.tw],x.at[rows_at(p.tw*Q,Q),:],tsem.at[0],tsem.at[1],p.peer("tw"))
    def bcopy(): return send(b,bgot,bsem.at[0],bsem.at[1],p.peer("tw"))
    def ycopy(c):
        r=rows_at(p.bit(0)*HALF,HALF)
        return send(w.at[c,r,:],wgot.at[c,r,:],ysem.at[0,c],ysem.at[1,c],p.peer("tw"))
    def xcopy(c,landed):
        ref=wgot.at[c,rows_at((1-p.bit(0) if landed else p.bit(0))*HALF,HALF),:]
        return send(ref,ref,xsem.at[0,c],xsem.at[1,c],p.peer(0))
    def ccopy(i,landed):
        core=1-p.th if landed else p.th
        quarter=p.tw if i==0 else 1-p.tw
        ref=norm.at[rows_at(core*T+quarter*Q,Q),:]
        return send(ref,ref,csem.at[0,i],csem.at[1,i],p.peer("th"))
    tcopy().start(); bcopy().start()
    for c in range(3): ycopy(c).start()
    def normalize(src,row):
        for t in range(Q//128):
            v=src(t)
            y=(norm_parts(v.astype(F32))[0]*gain[...]+shift[...]).astype(BF)
            norm[rows_at(row+t*128,128),:]=y
    def put(src,dst,i): return pltpu.make_async_copy(src,dst,osem.at[i])
    x[rows_at(p.tw*Q,Q),:]=tok[p.tw]
    normalize(lambda t: tok[p.tw,t*128:(t+1)*128,:],p.th*T+p.tw*Q)
    onehot=lax.broadcasted_iota(jnp.int32,(128,L),0)
    same=onehot==seg[...]
    mk[...]=jnp.where(same,1.0,0.0).T.astype(BF)
    ccopy(0,False).start()
    mq[...]=jnp.where(same|(onehot>=8),0.0,-float(2**40)).T.astype(BF)
    put(mk,mk_o,0).start(); put(mq,mq_o,1).start()
    tcopy().wait_recv()
    normalize(lambda t: x[rows_at((1-p.tw)*Q+t*128,128),:],p.th*T+(1-p.tw)*Q)
    put(x,x_o,2).start()
    bcopy().wait_recv()
    tiles=[slice(t*TT,(t+1)*TT) for t in range(L//TT)]
    def bias(c,ref): return ref[c//2:c//2+1,:] if c!=1 else None
    def project(c,wt,bs,r):
        y=dot(norm[r,:],wt,NN)
        if bs is not None: y=y+bs
        y=y.astype(BF)
        return y*BF(0.125) if c==0 else y
    ccopy(1,False).start()
    ccopy(0,True).wait_recv()
    ccopy(1,True).wait_recv()
    for c in range(3):
        for r in tiles: qkv[c,r,0:E]=project(c,w[c],bias(c,b),r)
    for r in tiles: normT[:,r]=norm[r,:].T
    put(normT,normT_o,3).start()
    for c in range(3):
        ycopy(c).wait_recv()
        xcopy(c,False).start()
    for c in range(3):
        xcopy(c,True).wait_recv()
        for r in tiles: qkv[c,r,E:2*E]=project(c,wgot[c],bias(c,bgot),r)
        put(qkv.at[c],(q_o,k_o,v_o)[c],4+c).start()
        wh[c,:,0:E]=w[c]; wh[c,:,E:2*E]=wgot[c]
    put(wh,wh_o,7).start()
    for src,dst,i in ((mk,mk_o,0),(mq,mq_o,1),(x,x_o,2),(normT,normT_o,3),(wh,wh_o,7)): put(src,dst,i).wait()
    for c in range(3):
        put(qkv.at[c],(q_o,k_o,v_o)[c],4+c).wait()
        ycopy(c).wait_send(); xcopy(c,False).wait_send()
    tcopy().wait_send(); bcopy().wait_send()
    for i in range(2): ccopy(i,False).wait_send()

def front(tok,w,b,gain,shift,seg):
    _,Q,D=tok.shape; T=2*Q; L=2*T; E=w.shape[2]
    outs=[((T,D),BF),((D,L),BF)]+[((L,2*E),BF)]*3+[((3,D,2*E),BF)]+[((L,128),BF)]*2
    sem=pltpu.SemaphoreType.DMA
    return pl.pallas_call(front_kernel,
      in_specs=[pl.BlockSpec(memory_space=pltpu.VMEM)]*6,out_specs=[pl.BlockSpec(memory_space=pl.ANY)]*len(outs),
      out_shape=[jax.ShapeDtypeStruct(*o) for o in outs],
      scratch_shapes=[pltpu.VMEM((T,D),BF),pltpu.VMEM((L,D),BF),pltpu.VMEM((D,L),BF),pltpu.VMEM((3,L,2*E),BF),pltpu.VMEM((3,D,2*E),BF),pltpu.VMEM((3,D,E),BF),
        pltpu.VMEM(b.shape,F32),pltpu.VMEM((L,128),BF),pltpu.VMEM((L,128),BF),sem((2,)),sem((2,)),sem((2,2)),sem((2,3)),sem((2,3)),sem((8,))],
      compiler_params=pltpu.CompilerParams(vmem_limit_bytes=60*2**20,collective_id=2,has_side_effects=True),name="front")(tok,w,b,gain,shift,seg)


SWAP = [(0, 1), (1, 0)]


def swap(value, axis):
    return lax.ppermute(value, axis, SWAP)


def in_order(mine, other, index, axis):
    return jnp.where(
        index == 0, jnp.concatenate([mine, other], axis), jnp.concatenate([other, mine], axis)
    )


def own_row(rows, tw):
    mine = lax.dynamic_index_in_dim(rows, tw, 0, keepdims=False)
    other = lax.dynamic_index_in_dim(rows, 1 - tw, 0, keepdims=False)
    return in_order(mine, swap(other, "tw"), tw, 0)


def body(
    dp_size,
    tokens,
    segment_ids,
    norm1_gain,
    norm1_shift,
    w_qkv,
    b_qv,
    w_out,
    b_out,
    norm2_gain,
    norm2_shift,
    w_up,
    b_up,
    w_down,
    b_down,
    cotangent,
):
    th, tw = lax.axis_index("th"), lax.axis_index("tw")
    d = tokens.shape[-1]
    mine = w_qkv.shape[2]
    seg = lax.dynamic_index_in_dim(segment_ids, tw, 0)
    x, normed_t, query, key, value, w_heads, mq, mk = front(tokens, w_qkv, b_qv, norm1_gain[None], norm1_shift[None], seg)
    tables = (mq, mk, *block_ranges(seg[0]))
    later = lax.optimization_barrier((cotangent, w_out, query))
    cot = own_row(later[0], tw)
    w_out_heads = jnp.concatenate([w_out, swap(later[1], "tw")], 0)
    attended, totals = attn_fwd(query, key, value, *tables)
    vectors = jnp.stack([b_out, norm2_gain, norm2_shift, b_down] + [jnp.zeros_like(b_out)] * 4)
    out_mine, out_other, grad_middle, grad_b_up, sums, red, grad_heads, grad_w_out = ffn(
        dp_size, attended, w_out_heads, x, vectors, cot, w_up, w_down, b_up[None]
    )
    out_got = swap(out_other, "tw")
    dq, dk, dv = attn_bwd(query, key, value, grad_heads, attended, totals, *tables)
    up, down, heads, small, grad_tokens = finish(
        dp_size, red, dq, dk, dv, normed_t, w_heads, grad_w_out, x, norm1_gain[None], grad_middle, sums, grad_b_up
    )
    up, down, w_qkv_grad, w_out_grad, block_out = widen(tw, up, down, heads, out_mine, out_got)
    parts = small.reshape(-1)
    b_qv_grad = lax.dynamic_slice_in_dim(small[-16:].reshape(4, 2, 256), 2 * th + tw, 1, 0)[0, :, :mine]
    return (
        block_out,
        grad_tokens,
        parts[:d],
        parts[d : 2 * d],
        w_qkv_grad,
        b_qv_grad,
        w_out_grad,
        parts[2 * d : 3 * d],
        parts[3 * d : 4 * d],
        parts[4 * d : 5 * d],
        up,
        parts[6 * d : -16 * 128],
        down,
        parts[5 * d : 6 * d],
    )


def solution(mesh):
    return jax.shard_map(
        functools.partial(body, mesh.shape["dp"]),
        mesh=mesh,
        in_specs=(
            P("dp", ("th", "tw"), None),
            P("dp", None),
            P(),
            P(),
            P(None, None, ("th", "tw")),
            P(None, ("th", "tw")),
            P(("th", "tw"), None),
            P(),
            P(),
            P(),
            P(),
            P(),
            P(),
            P(),
            P("dp", ("th", "tw"), None),
        ),
        out_specs=(
            P("dp", ("th", "tw"), None),
            P("dp", ("th", "tw"), None),
            P(),
            P(),
            P(None, None, ("th", "tw")),
            P(None, ("th", "tw")),
            P(("th", "tw"), None),
            P(),
            P(),
            P(),
            P(),
            P(),
            P(),
            P(),
        ),
        check_vma=False,
    )
```

profile of v0, /device:TPU:0, one launch (start us, length us, event | category | flops | bytes accessed | tf_op | source)
XLA Modules:
  0.0 310.3 jit_solution(10486082601514123460)
XLA Ops:
  0.7 1.3 broadcast_in_dim.12.gain
  1.9 1.3 broadcast_in_dim.13.shift
  3.2 2.3 copy.31.w
  5.5 0.6 fusion
  6.1 41.5 %front.1 = (bf16[768,768]{1,0:T(8,128)(2,1)}, bf16[768,1536]{1,0:T(8,128)(2,1)}, bf16[1536,384]{1,0:T(8,128)(2,1)}, bf16[1536,384]{1,0:T(8,128)(2,1)}, bf16[1536...) custom-call(bf16[2,384,768]{2,1,0:T(8,128)(2,1)} %tok.1, ...), custom_call_target="tpu_custom_call" | custom-call | tf_op jit(solution)/shard_map/front/pallas_call | solution.py:596
  47.8 1.6 collective-permute-start.1
  49.4 0.7 collective-permute-start
  50.4 0.6 stack.23.vin
  51.3 0.5 and_select_fusion
  51.8 20.7 %attention_forward.1 = (bf16[1536,384]{1,0:T(8,128)(2,1)}, f32[8,1536]{1,0:T(8,128)}) custom-call(s32[6]{0:T(128)} %get-tuple-element.121.lo_ref, s32[6]{0:T(128)} %get-tuple-element.120.hi_ref, bf16[1536,384]{1,0:T(8,128)(2,1)} %get-tuple-element.47.q_ref, bf16[1536,384]{1,0:T(8,128)(2,1)} %get-tuple-element.48.k_ref, ...), custom_call_target="tpu_custom_call" | custom-call | tf_op jit(solution)/shard_map/attention_forward/pallas_call | solution.py:57
  72.5 0.9 pad_maximum_fusion.wo
  73.4 1.5 maximum_select_fusion.cot
  74.8 79.1 %feed_forward.1 = (bf16[384,768]{1,0:T(8,128)(2,1)}, bf16[384,768]{1,0:T(8,128)(2,1)}, f32[768,768]{1,0:T(8,128)}, f32[1,3072]{1,0:T(1,128)}, f32[8,768]{1,0:T(8...) custom-call(bf16[1536,384]{1,0:T(8,128)(2,1)} %get-tuple-element.52.att.o_ref, ...), custom_call_target="tpu_custom_call" | custom-call | tf_op jit(solution)/shard_map/feed_forward/pallas_call | solution.py:325
  153.9 1.1 collective-permute-start.2
  155.0 27.7 %attention_backward.1 = (bf16[1536,384]{1,0:T(8,128)(2,1)}, bf16[1536,384]{1,0:T(8,128)(2,1)}, bf16[1536,384]{1,0:T(8,128)(2,1)}) custom-call(s32[6]{0:T(128)} %get-tuple-element.121.lo_ref, s32[6]{0:T(128)} %get-tuple-element.120.hi_ref, bf16[1536,384]{1,0:T(8,128)(2,1)} %get-tuple-element.47.q_ref, bf16[1536,384]{1,0:T(8,128)(2,1)} %get-tuple-element.48.k_ref, ...), custom_call_target="tpu_custom_call" | custom-call | tf_op jit(solution)/shard_map/attention_backward/pallas_call | solution.py:114
  182.8 105.1 %finish_gradients.1 = (bf16[768,3072]{1,0:T(8,128)(2,1)}, bf16[768,3072]{1,0:T(8,128)(2,1)}, bf16[4608,128]{1,0:T(8,128)(2,1)}, f32[76,128]{1,0:T(8,128)}, bf16[2,384,768]{2,1,0:T(8,128)(2,1)}) custom-call(bf16[6,192,128]{2,1,0:T(8,128)(2,1)} %get-tuple-element.56.red, bf16[1536,384]{1,0:T(8,128)(2,1)} %get-tuple-element.59.dq, ...), custom_call_target="tpu_custom_call" | custom-call | tf_op jit(solution)/shard_map/finish_gradients/pallas_call | solution.py:496
  287.9 0.7 slice.60
  288.6 0.6 dynamic-slice_bitcast_fusion.2
  289.2 1.3 slice_bitcast_fusion
  290.5 1.4 slice_bitcast_fusion.1
  291.9 1.3 copy-done
  293.2 13.0 %widen.1 = (f32[768,3072]{1,0:T(8,128)}, f32[3072,768]{1,0:T(8,128)}, f32[3,768,192]{2,1,0:T(8,128)}, f32[192,768]{1,0:T(8,128)}, bf16[2,384,768]{2,1,0:T(8,128)(2,1)}) custom-call(s32[1]{0:T(128)} %bitcast.where, bf16[768,3072]{1,0:T(8,128)(2,1)} %get-tuple-element.68.up, bf16[768,3072]{1,0:T(8,128)(2,1)} %get-tuple-element.69.down, ...), custom_call_target="tpu_custom_call" | custom-call | tf_op jit(solution)/shard_map/widen/pallas_call | solution.py:520
  306.2 3.0 copy.32
  309.3 1.0 copy.34
  (32 shorter events, 0.6 us)
Async XLA Ops:
  0.6 4.9 %copy-start.9 = (s32[2,1536]{1,0:T(2,128)S(1)}, s32[2,1536]{1,0:T(2,128)}, u32[]{:S(2)}) copy-start(s32[2,1536]{1,0:T(2,128)} %param.16) | copy-start | bytes 36868
  6.1 41.5 %copy-start.2 = (bf16[2,384,768]{2,1,0:T(8,128)(2,1)S(1)}, bf16[2,384,768]{2,1,0:T(8,128)(2,1)}, u32[]{:S(2)}) copy-start(bf16[2,384,768]{2,1,0:T(8,128)(2,1)} %param.29) | copy-start | bytes 3538948
  47.6 1.8 copy-start.4
  47.7 2.7 copy-start.5
  47.7 2.7 copy-start.6
  47.7 2.7 copy-start.7
  47.7 2.7 copy-start.8
  47.8 25.6 %collective-permute-start.1 = (bf16[384,768]{1,0:T(8,128)(2,1)S(1)}, bf16[384,768]{1,0:T(8,128)(2,1)S(1)}, u32[]{:S(2)}, u32[]{:S(2)}) collective-permute-start(bf16[384,768]{1,0:T(8,128)(2,1)S(1)} %get-tuple-element.113), channel_id=1, source_target_pairs={{0,1},{1,0},{2,3},{3,2},{4,5},{5,4},{6,7},{7,6},{8,9},{9,8},{10,11... | collective-permute-start | bytes 1769480 | tf_op jit(solution)/shard_map/ppermute | solution.py:608
  49.4 23.1 %collective-permute-start = (bf16[192,768]{1,0:T(8,128)(2,1)S(1)}, bf16[192,768]{1,0:T(8,128)(2,1)S(1)}, u32[]{:S(2)}, u32[]{:S(2)}) collective-permute-start(bf16[192,768]{1,0:T(8,128)(2,1)S(1)} %copy-done.4), channel_id=1, source_target_pairs={{0,1},{1,0},{2,3},{3,2},{4,5},{5,4},{6,7},{7,6},{8,9},{9,8},{10,11... | collective-permute-start | bytes 884744 | tf_op jit(solution)/shard_map/ppermute | solution.py:608
  153.9 138.0 %collective-permute-start.2 = (bf16[384,768]{1,0:T(8,128)(2,1)}, bf16[384,768]{1,0:T(8,128)(2,1)S(1)}, u32[]{:S(2)}, u32[]{:S(2)}) collective-permute-start(bf16[384,768]{1,0:T(8,128)(2,1)} %get-tuple-element.72), channel_id=1, source_target_pairs={{0,1},{1,0},{2,3},{3,2},{4,5},{5,4},{6,7},{7,6},{8,9},{9,8},{10,11... | collective-permute-start | bytes 1769480 | tf_op jit(solution)/shard_map/ppermute | solution.py:608
  182.8 109.2 %copy-start.1 = (bf16[384,768]{1,0:T(8,128)(2,1)S(1)}, bf16[384,768]{1,0:T(8,128)(2,1)}, u32[]{:S(2)}) copy-start(bf16[384,768]{1,0:T(8,128)(2,1)} %get-tuple-element.71.mine) | copy-start | bytes 1769476
  291.9 1.3 copy-start
  306.2 3.0 copy-start.3
where the time goes:
time: 311 us; the launch traced here: 310 us
  Pallas kernels  287 us (92%)
  local copies, waits for them, and re-layouts  15.7 us (5%)
  starting transfers between devices  3.48 us (1%)
    pallas_call x1, Pallas kernels, finish(): pl.pallas_call(functools.partial(finish_kernel, dp), grid=(grid,), in_spe...  105 us
    pallas_call x1, Pallas kernels, ffn(): pl.pallas_call(functools.partial(ffn_kernel, dp), grid=(CH + LAG * n + 1,...  79.1 us
    pallas_call x1, Pallas kernels, front(): pl.pallas_call(front_kernel, in_specs=[pl.BlockSpec(memory_space=pltpu.VM...  41.5 us
    pallas_call x1, Pallas kernels, attn_bwd(): pl.pallas_call(bwd_kernel, grid_spec=pltpu.PrefetchScalarGridSpec(num_sca...  27.7 us
    pallas_call x1, Pallas kernels, attn_fwd(): pl.pallas_call(fwd_kernel, grid_spec=pltpu.PrefetchScalarGridSpec(num_sca...  20.7 us
    pallas_call x1, Pallas kernels, widen(): pl.pallas_call(widen_kernel, grid=(FF // FC,), in_specs=[pl.BlockSpec(mem...  13 us
    unnamed x23, local copies, waits for them, and re-layouts  7.65 us
  transfers between devices with their start and end apart: 3, of which 0 were waited for; matrix products, arithmetic and copies ran while one was open for 2% of the time, Pallas kernels for 49%

commit v1 on v0

v1 whole, which is shorter than its diff:
```python
import functools

import jax
import jax.numpy as jnp
from jax import lax
from jax.experimental import pallas as pl
from jax.experimental.pallas import tpu as pltpu
from jax.sharding import PartitionSpec as P

NT=(((1,),(1,)),((),())); NN=(((1,),(0,)),((),())); TN=(((0,),(0,)),((),()))
F32=jnp.float32; BF=jnp.bfloat16
BQ=256; BK=256; HD=64
def dot(a,b,d): return lax.dot_general(a,b,d,preferred_element_type=F32)

def fwd_kernel(lo_ref, hi_ref, q_ref, k_ref, v_ref, mq_ref, mk_ref, o_ref, lse_ref, m_ref, l_ref, acc_ref):
    i=pl.program_id(0)
    pairs=q_ref.shape[1]//128
    lane=lax.broadcasted_iota(jnp.int32,(1,128),1)
    halves=(lane<HD, lane>=HD)
    m_ref[...]=jnp.full(m_ref.shape,-1e30,F32)
    l_ref[...]=jnp.zeros_like(l_ref)
    acc_ref[...]=jnp.zeros_like(acc_ref)
    def body(j,_):
        ks=pl.ds(pl.multiple_of(j*BK,BK),BK)
        mk=mk_ref[ks,:]
        for p in range(pairs):
            cols=slice(p*128,(p+1)*128)
            qx=jnp.concatenate([q_ref[:,cols],mq_ref[...]],1)
            k2=k_ref[ks,cols]; v2=v_ref[ks,cols]
            ps=[]
            for e in range(2):
                h=2*p+e
                kx=jnp.concatenate([jnp.where(halves[e],k2,jnp.zeros_like(k2)),mk],1)
                s=dot(kx,qx,NT)
                m_old=m_ref[h:h+1,:]
                m_new=jnp.maximum(m_old,jnp.max(s,axis=0,keepdims=True))
                alpha=jnp.exp(m_old-m_new)
                pe=jnp.exp(s-m_new)
                l_ref[h:h+1,:]=l_ref[h:h+1,:]*alpha+jnp.sum(pe,axis=0,keepdims=True)
                m_ref[h:h+1,:]=m_new
                acc_ref[h*HD:(h+1)*HD,:]=acc_ref[h*HD:(h+1)*HD,:]*alpha
                ps.append(pe.astype(BF))
            vcat=jnp.concatenate([jnp.where(halves[0],v2,jnp.zeros_like(v2)),jnp.where(halves[1],v2,jnp.zeros_like(v2))],0)
            acc_ref[cols,:]+=dot(vcat,jnp.concatenate(ps,0),TN)
        return 0
    lax.fori_loop(lo_ref[i],hi_ref[i],body,0)
    for p in range(pairs):
        parts=[]
        for e in range(2):
            h=2*p+e
            parts.append(acc_ref[h*HD:(h+1)*HD,:]*(1.0/l_ref[h:h+1,:]))
        o_ref[:,p*128:(p+1)*128]=jnp.concatenate(parts,0).T.astype(BF)
    lse_ref[...]=m_ref[...]+jnp.log(jnp.maximum(l_ref[...],1e-37))

def attn_fwd(q,k,v,mq,mk,lo,hi):
    L,C=q.shape
    return pl.pallas_call(fwd_kernel,
        grid_spec=pltpu.PrefetchScalarGridSpec(num_scalar_prefetch=2,grid=(L//BQ,),
          in_specs=[pl.BlockSpec((BQ,C),lambda i,*_:(i,0)),pl.BlockSpec((L,C),lambda i,*_:(0,0)),pl.BlockSpec((L,C),lambda i,*_:(0,0)),
                    pl.BlockSpec((BQ,128),lambda i,*_:(i,0)),pl.BlockSpec((L,128),lambda i,*_:(0,0))],
          out_specs=[pl.BlockSpec((BQ,C),lambda i,*_:(i,0)),pl.BlockSpec((8,BQ),lambda i,*_:(0,i))],
          scratch_shapes=[pltpu.VMEM((8,BQ),F32),pltpu.VMEM((8,BQ),F32),pltpu.VMEM((C,BQ),F32)]),
        out_shape=[jax.ShapeDtypeStruct((L,C),BF),jax.ShapeDtypeStruct((8,L),F32)],
        name="attention_forward",
    )(lo,hi,q,k,v,mq,mk)

def bwd_kernel(lo_ref, hi_ref, q_ref, k_ref, v_ref, do_ref, o_ref, lse_ref, mq_ref, mk_ref, dq_ref, dk_ref, dv_ref, dk_acc, dv_acc, dq_acc, qcat, docat):
    i=pl.program_id(0); n=pl.num_programs(0)
    C=q_ref.shape[1]; pairs=C//128
    lane=lax.broadcasted_iota(jnp.int32,(1,128),1)
    halves=(lane<HD, lane>=HD)
    @pl.when(i==0)
    def _():
        dk_acc[...]=jnp.zeros_like(dk_acc); dv_acc[...]=jnp.zeros_like(dv_acc)
    dq_acc[...]=jnp.zeros_like(dq_acc)
    sel=(lax.broadcasted_iota(jnp.int32,(8,C),1)//HD==lax.broadcasted_iota(jnp.int32,(8,C),0)).astype(F32)
    delta=lax.dot_general(sel,do_ref[...].astype(F32)*o_ref[...].astype(F32),NT,precision=lax.Precision.HIGHEST,preferred_element_type=F32)
    for p in range(pairs):
        cols=slice(p*128,(p+1)*128)
        for e in range(2):
            q2=q_ref[:,cols]; d2=do_ref[:,cols]
            qcat[p,e*BQ:(e+1)*BQ,:]=jnp.where(halves[e],q2,jnp.zeros_like(q2))
            docat[p,e*BQ:(e+1)*BQ,:]=jnp.where(halves[e],d2,jnp.zeros_like(d2))
    lse=lse_ref[...]
    def body(j,_):
        ks=pl.ds(pl.multiple_of(j*BK,BK),BK)
        mk=mk_ref[ks,:]
        for p in range(pairs):
            cols=slice(p*128,(p+1)*128)
            qx=jnp.concatenate([q_ref[:,cols],mq_ref[...]],1)
            k2=k_ref[ks,cols]; v2=v_ref[ks,cols]; d2=do_ref[:,cols]
            ps=[]; dss=[]; kms=[]
            for e in range(2):
                h=2*p+e
                km=jnp.where(halves[e],k2,jnp.zeros_like(k2)); vm=jnp.where(halves[e],v2,jnp.zeros_like(v2))
                s=dot(jnp.concatenate([km,mk],1),qx,NT)
                pr=jnp.exp(s-lse[h:h+1,:])
                dp=dot(vm,d2,NT)
                ds=pr*(dp-delta[h:h+1,:])
                ps.append(pr.astype(BF)); dss.append(ds.astype(BF)); kms.append(km)
            dv_acc[ks,cols]+=dot(jnp.concatenate(ps,1),docat[p],NN)
            dk_acc[ks,cols]+=dot(jnp.concatenate(dss,1),qcat[p],NN)
            dq_acc[cols,:]+=dot(jnp.concatenate(kms,0),jnp.concatenate(dss,0),TN)
        return 0
    lax.fori_loop(lo_ref[i],hi_ref[i],body,0)
    dq_ref[...]=(dq_acc[...]*0.125).T.astype(BF)
    @pl.when(i==n-1)
    def _():
        dk_ref[...]=dk_acc[...].astype(BF); dv_ref[...]=dv_acc[...].astype(BF)

def attn_bwd(q,k,v,do,o,lse,mq,mk,lo,hi):
    L,C=q.shape
    blk=pl.BlockSpec((BQ,C),lambda i,*_:(i,0)); full=pl.BlockSpec((L,C),lambda i,*_:(0,0))
    return pl.pallas_call(bwd_kernel,
        grid_spec=pltpu.PrefetchScalarGridSpec(num_scalar_prefetch=2,grid=(L//BQ,),
          in_specs=[blk,full,full,blk,blk,pl.BlockSpec((8,BQ),lambda i,*_:(0,i)),pl.BlockSpec((BQ,128),lambda i,*_:(i,0)),pl.BlockSpec((L,128),lambda i,*_:(0,0))],
          out_specs=[blk,full,full],
          scratch_shapes=[pltpu.VMEM((L,C),F32),pltpu.VMEM((L,C),F32),pltpu.VMEM((C,BQ),F32),pltpu.VMEM((C//128,2*BQ,128),BF),pltpu.VMEM((C//128,2*BQ,128),BF)]),
        out_shape=[jax.ShapeDtypeStruct((L,C),BF)]*3,
        name="attention_backward",
    )(lo,hi,q,k,v,do,o,lse,mq,mk)

def block_ranges(seg):
    first=seg[::BQ]; last=seg[BQ-1::BQ]
    lo=jnp.sum(seg[None,:]<first[:,None],axis=1,dtype=jnp.int32)//BK
    hi=(jnp.sum(seg[None,:]<=last[:,None],axis=1,dtype=jnp.int32)+BK-1)//BK
    return lo,hi


TT=256; FC=512
LAG=2; GLAG=3; HLAG=3; HSP=2; GSP=4; VLAG=2; FL=3

def bits_of(dp): return dp.bit_length()-1

def big_plan(dp,rows):
    n=bits_of(dp)
    orders=(["tw"]+list(range(n)),[0,"tw"]+list(range(1,n)),[1,2,0,"tw"]+list(range(3,n)))
    unit=16<<(n+1)
    units=rows//unit
    third=max(1,units//4)
    shares=[units-units//3-third,units//3,third]
    return streams(orders,shares,unit)

def head_plan(dp,rows):
    n=bits_of(dp)
    orders=(["tw"]+list(range(n)),[0,"tw"]+list(range(1,n)),[1,2,0,"tw"]+list(range(3,n)))
    unit=16<<n
    units=rows//unit
    low=max(1,units//6)
    mid=max(1,units//3)
    return streams(orders,[units-mid-low,mid,low],unit)

def streams(orders,shares,unit):
    out=[]; start=0
    for order,share in zip(orders,shares):
        out.append((order,start,share*unit)); start+=share*unit
    return out

class Peers:
    def __init__(self):
        self.dp=lax.axis_index("dp"); self.th=lax.axis_index("th"); self.tw=lax.axis_index("tw")
    def bit(self,axis):
        return self.tw if axis=="tw" else (self.dp//(1<<axis))%2
    def peer(self,axis):
        if axis=="tw": return {"tw":1-self.tw}
        if axis=="th": return {"th":1-self.th}
        return {"dp":self.dp+(1-2*self.bit(axis))*(1<<axis)}

def send(src,dst,ssem,rsem,peer):
    return pltpu.make_async_remote_copy(src,dst,ssem,rsem,device_id=peer,device_id_type=pl.DeviceIdType.MESH)

def barrier(p,axes):
    sem=pltpu.get_barrier_semaphore()
    for a in axes:
        pl.semaphore_signal(sem,inc=1,device_id=p.peer(a),device_id_type=pl.DeviceIdType.MESH)
    pl.semaphore_wait(sem,len(axes))

def halves(p,order,row,rows,keep_tw=False):
    out=[]
    for axis in order:
        if keep_tw and axis=="tw": out.append((row,row,rows)); continue
        rows//=2; bit=p.bit(axis)
        out.append((row+(1-bit)*rows,row+bit*rows,rows)); row=row+bit*rows
    return out
def run_steps(steps):
    total=max(f+sp*(cnt-1) for f,sp,cnt,_ in steps)+1
    def body(i,_):
        for r in range(2):
            g=2*i+r
            for f,sp,cnt,what in steps:
                if sp==2:
                    if f%2!=r: continue
                    c=i-f//2
                else: c=g-f
                if cnt==1:
                    pl.when(c==0)(functools.partial(what,0))
                else: pl.when((c>=0)&(c<cnt))(functools.partial(what,c))
        return 0
    lax.fori_loop(0,(total+1)//2,body,0)
def al(x): return x if isinstance(x,int) else pl.multiple_of(x,16)
def rows_at(row,n): return pl.ds(al(row),n)

EPS=1e-06
def norm_parts(x):
    mean=jnp.mean(x,axis=-1,keepdims=True)
    cen=x-mean
    r=lax.rsqrt(jnp.mean(cen*cen,axis=-1,keepdims=True)+EPS)
    return cen*r,r
def norm_back(e,n,r,gain):
    t=e*gain
    return r*(t-jnp.mean(t,axis=-1,keepdims=True)-n*jnp.mean(t*n,axis=-1,keepdims=True))
def colsum(x): return jnp.sum(x,axis=0,keepdims=True)

def ffn_kernel(dp,att,wo,x,vin,cot,wu_h,wd_h,bu,mine,other,gm,gb,vec,red,gheads,gwo,
               wu,wd,cotT,mid,n2,n2T,obuf,orecv,grow,act,gh,dw,chip_recv,wsem,osem,gsem,*rest):
    CH=dw.shape[0]; T,D=x.shape; SLOTS=chip_recv.shape[0]
    plan=big_plan(dp,dw.shape[2]); n=len(plan[0][0]); K=len(plan)
    recv=[rest[k*n:(k+1)*n] for k in range(K)]
    send_sem,recv_sem,chip_send,chip_got=rest[K*n:]
    p=Peers()
    tiles=[slice(t*TT,(t+1)*TT) for t in range(T//TT)]; NT_=len(tiles)
    regs=[halves(p,*s) for s in plan]
    def copy(k,s,c):
        out,_,nr=regs[k][s]
        return send(dw.at[c,p.th,rows_at(out,nr),:],recv[k][s].at[c],send_sem.at[k,s,c],recv_sem.at[k,s,c],p.peer(plan[k][0][s]))
    def chip_copy(c):
        return send(dw.at[c,1-p.th],chip_recv.at[c%SLOTS],chip_send.at[c],chip_got.at[c],p.peer("th"))
    def ocopy(): return send(obuf,orecv,osem.at[0],osem.at[1],p.peer("th"))
    def gcopy(landed):
        ref=grow.at[rows_at((1-p.th if landed else p.th)*T,T),:]
        return send(ref,ref,gsem.at[0],gsem.at[1],p.peer("th"))
    def wload(c):
        return (pltpu.make_async_copy(wu_h.at[:,pl.ds(pl.multiple_of(c*FC,FC),FC)],wu.at[c],wsem.at[0,c]),
                pltpu.make_async_copy(wd_h.at[pl.ds(pl.multiple_of(c*FC,FC),FC),:],wd.at[c],wsem.at[1,c]))
    def load(c,_):
        for w in wload(c): w.start()
        return 0
    lax.fori_loop(0,CH,load,0)
    barrier(p,["th"]+plan[0][0])
    for r in tiles:
        obuf[r,:]=dot(att[rows_at((1-p.th)*T+r.start,TT),:],wo[...],NN).astype(BF)
    for t,r in enumerate(tiles):
        mid[r,:]=x[r,:].astype(F32)+dot(att[rows_at(p.th*T+r.start,TT),:],wo[...],NN)+vin[0:1,:]
        if t==0: ocopy().start()
        cotT[:,r]=cot[r,:].T
    ocopy().wait_recv()
    for r in tiles:
        m=mid[r,:]+orecv[r,:].astype(F32)
        mid[r,:]=m
        nn,_=norm_parts(m)
        y=(nn*vin[1:2,:]+vin[2:3,:]).astype(BF)
        n2[r,:]=y; n2T[:,r]=y.T
    vec[...]=jnp.zeros_like(vec)
    def sum_step(s,c):
        news=[]
        for k in range(K):
            copy(k,s,c).wait_recv()
            _,kr,nr=regs[k][s]
            at=(c,p.th,rows_at(kr,nr),slice(None))
            new=(dw[at].astype(F32)+recv[k][s][c].astype(F32)).astype(BF)
            if s<n-1: dw[at]=new
            else: news.append((kr,nr,new))
        if s<n-1:
            for k in range(K): copy(k,s+1,c).start()
        else:
            out=0
            for kr,nr,new in news:
                red[c,out:out+nr,:]=new; out+=nr
    def chip_sum(c):
        chip_copy(c).wait_recv()
        def add(q,_):
            r=rows_at(q*TT,TT)
            dw[c,p.th,r,:]=(dw[c,p.th,r,:].astype(F32)+chip_recv[c%SLOTS,r,:].astype(F32)).astype(BF)
            return 0
        lax.fori_loop(0,dw.shape[2]//TT,add,0)
        for k in range(K): copy(k,0,c).start()
    def hidden(c):
        for w in wload(c): w.wait()
        cols=pl.ds(pl.multiple_of(c*FC,FC),FC)
        gsum=jnp.zeros((1,FC),F32)
        for r in tiles:
            h=dot(n2[r,:],wu[c],NN)+bu[:,cols]
            ga=dot(cot[r,:],wd[c],NT)
            cdf=0.5*(1.0+lax.erf(h*(0.5**0.5)))
            a=(h*cdf).astype(BF)
            gr=(ga*(cdf+h*(jnp.exp(h*h*-0.5)*0.3989422804014327))).astype(BF)
            act[c,r,:]=a; gh[c,r,:]=gr
            gsum+=colsum(gr.astype(F32))
        gb[:,cols]=gsum
    def weight_grads(c):
        for t in range(D//TT):
            r=slice(t*TT,(t+1)*TT)
            for m,(lhs,rhs) in enumerate(((n2T,gh),(cotT,act))):
                y=dot(lhs[r,:],rhs[c],NN).astype(BF)
                for q in range(FC//128): dw[c,m,q*D+t*TT:q*D+(t+1)*TT,:]=y[:,q*128:(q+1)*128]
    def norm_two_back(t):
        r=rows_at(t*TT,TT)
        e=dot(gh[0,r,:],wu[0],NT)
        for c in range(1,CH): e+=dot(gh[c,r,:],wu[c],NT)
        nn,rs=norm_parts(mid[r,:])
        ct=cot[r,:].astype(F32)
        gmid=ct+norm_back(e,nn,rs,vin[1:2,:])
        gm[r,:]=gmid
        gbr=gmid.astype(BF)
        grow[rows_at(p.th*T+t*TT,TT),:]=gbr
        vec[0:1,:]+=colsum(gbr.astype(F32)); vec[1:2,:]+=colsum(e*nn); vec[2:3,:]+=colsum(e); vec[3:4,:]+=colsum(ct)
    def block_out(t):
        r=rows_at(t*TT,TT)
        y=mid[r,:]+vin[3:4,:]
        for c in range(CH): y+=dot(act[c,r,:],wd[c],NN)
        n2[r,:]=y.astype(BF)
    def split_out(_):
        gcopy(True).wait_recv()
        mine[...]=n2[rows_at(p.tw*(T//2),T//2),:]
        other[...]=n2[rows_at((1-p.tw)*(T//2),T//2),:]
    def grad_heads(u):
        for t in range(NT_):
            r=rows_at(u*T+t*TT,TT)
            gheads[r,:]=dot(grow[r,:],wo[...],NT).astype(BF)
    def grad_wo(_):
        for t in range(D//TT):
            r=slice(t*TT,(t+1)*TT)
            gwo[r,:]=dot(grow[:,r],att[...],TN).astype(BF)
    P2=2*CH; P3=P2+NT_; P4=P3+NT_
    part=functools.partial
    steps=[(3+FL*(s+1),2,CH,part(sum_step,s)) for s in reversed(range(n))]
    steps+=[(3,2,CH,chip_sum),(2,2,CH,lambda c: chip_copy(c).start())]
    steps+=[(0,2,CH,hidden),(1,2,CH,weight_grads),(P2,1,NT_,norm_two_back),(P3,1,1,lambda _: gcopy(False).start()),(P3,1,NT_,block_out),
            (P4,1,1,split_out),(P4,1,2,grad_heads),(P4+2,1,1,grad_wo)]
    run_steps(steps)
    ocopy().wait_send(); gcopy(False).wait_send()
    def drain(c,_):
        chip_copy(c).wait_send()
        for k in range(K):
            for s in range(n): copy(k,s,c).wait_send()
        return 0
    lax.fori_loop(0,CH,drain,0)

def whole(shape):
    return pl.BlockSpec(memory_space=pltpu.VMEM)

def ffn(dp,att,wo,x,vin,cot,wu,wd,bu):
    T,D=x.shape; FF=wu.shape[1]; CH=FF//FC; R=FC//128*D; C=att.shape[1]
    plan=big_plan(dp,R); n=len(plan[0][0])
    fin=R>>n
    recv=[pltpu.VMEM((CH,rows>>(s+1),128),BF) for _,_,rows in plan for s in range(n)]
    outs=[((T//2,D),BF),((T//2,D),BF),((T,D),F32),((1,FF),F32),((8,D),F32),((CH,fin,128),BF),((2*T,C),BF),((D,C),BF)]
    specs=[whole(o[0]) for o in outs]
    hbm=pl.BlockSpec(memory_space=pl.ANY)
    V=pltpu.VMEM; sem=pltpu.SemaphoreType.DMA
    return pl.pallas_call(functools.partial(ffn_kernel,dp),
      in_specs=[whole(v.shape) for v in (att,wo,x,vin,cot)]+[hbm,hbm,whole(bu.shape)],
      out_specs=specs,out_shape=[jax.ShapeDtypeStruct(*o) for o in outs],
      scratch_shapes=[V((CH,D,FC),BF),V((CH,FC,D),BF),V((D,T),BF),V((T,D),F32),V((T,D),BF),V((D,T),BF),V((T,D),BF),V((T,D),BF),V((2*T,D),BF),
          V((CH,T,FC),BF),V((CH,T,FC),BF),V((CH,2,R,128),BF),V((3,R,128),BF),sem((2,CH)),sem((2,)),sem((2,))]+recv
        +[sem((len(plan),n,CH))]*2+[sem((CH,))]*2,
      compiler_params=pltpu.CompilerParams(vmem_limit_bytes=63*2**20+2**19,collective_id=0,has_side_effects=True),name="feed_forward")(att,wo,x,vin,cot,wu,wd,bu)

def finish_kernel(dp,red,dq_h,dk_h,dv_h,normT_h,wh_h,gwo_h,x_h,gm_h,vin,vec,gbu,gathered,heads_out,vec_out,tok,full,fsem,dq,dk,dv,normT,wh,gwo,x,gm,isem,hp,hg,vbuf,vrecv,own,obuf,orecv,tbuf,trecv,vrow,osem,tsem,*rest):
    CH=full.shape[0]; R=full.shape[2]; T,D=x.shape; C=dq.shape[1]; Q=T//2
    plan=big_plan(dp,R); n=len(plan[0][0]); K=len(plan)
    HR=hp.shape[2]; hplan=head_plan(dp,HR); HK=len(hplan); HC=hp.shape[0]
    hrecv=[rest[k*n:(k+1)*n] for k in range(HK)]
    send_sem,recv_sem,chip_send,chip_got,hs_sem,hr_sem,ha_send,ha_recv,vs_sem,vr_sem=rest[HK*n:]
    p=Peers()
    regs=[halves(p,*s) for s in plan]
    hregs=[halves(p,*s,keep_tw=True) for s in hplan]
    def gat(k,s,c,landed):
        other,mine,nr=regs[k][s]
        ref=full.at[c,p.th,rows_at(other if landed else mine,nr),:]
        return send(ref,ref,send_sem.at[k,s,c],recv_sem.at[k,s,c],p.peer(plan[k][0][s]))
    def chip(c,landed):
        ref=full.at[c,1-p.th if landed else p.th]
        return send(ref,ref,chip_send.at[c],chip_got.at[c],p.peer("th"))
    def fput(c): return pltpu.make_async_copy(full.at[c],gathered.at[c],fsem.at[c])
    def hsum(k,s,c):
        order=hplan[k][0]; other,_,nr=hregs[k][s]
        if order[s]=="tw": src=hp.at[c,pl.ds(1,1),rows_at(other,nr),:]
        elif order.index("tw")>s: src=hp.at[c,:,rows_at(other,nr),:]
        else: src=hp.at[c,pl.ds(0,1),rows_at(other,nr),:]
        return send(src,hrecv[k][s].at[c],hs_sem.at[k,s,c],hr_sem.at[k,s,c],p.peer(order[s]))
    def hgat(k,s,c,landed):
        order=hplan[k][0]; other,mine,nr=hregs[k][s]
        ref=hg.at[c,rows_at(other if landed else mine,nr),:]
        return send(ref,ref,ha_send.at[k,s,c],ha_recv.at[k,s,c],p.peer(order[s]))
    backs=[[s for s in reversed(range(n)) if o[s]!="tw"] for o,_,_ in hplan]
    vaxes=["th","tw"]+list(range(n-1))
    def vcopy(i): return send(vbuf.at[i],vrecv.at[i],vs_sem.at[i],vr_sem.at[i],p.peer(vaxes[i]))
    def ocopy(): return send(obuf,orecv,osem.at[0],osem.at[1],p.peer("th"))
    def tcopy(): return send(tbuf.at[rows_at((1-p.tw)*Q,Q),:],trecv,tsem.at[0],tsem.at[1],p.peer("tw"))
    loads=[pltpu.make_async_copy(a,b,isem.at[i]) for i,(a,b) in enumerate(((normT_h,normT),(dq_h,dq),(dk_h,dk),(dv_h,dv),(gwo_h,gwo),(wh_h,wh),(x_h,x),(gm_h,gm)))]
    for l in loads: l.start()
    def arrived(a,b):
        for l in loads[a:b]: l.wait()
    out=0
    for k in range(K):
        _,kr,nr=regs[k][n-1]
        for c in range(CH): full[c,p.th,rows_at(kr,nr),:]=red[c,out:out+nr,:]
        out+=nr
    vbuf[0]=jnp.zeros(vbuf.shape[1:],F32)
    vrow[...]=jnp.zeros(vrow.shape,F32)
    barrier(p,["th"]+plan[0][0])
    last=n+n-1
    def head_step(j,c):
        for k in range(HK):
            order=hplan[k][0]
            if 0<j<=n:
                s=j-1
                hsum(k,s,c).wait_recv()
                _,kr,nr=hregs[k][s]
                q=slice(0,2) if order.index("tw")>s else slice(0,1)
                at=(c,q,rows_at(kr,nr),slice(None))
                new=(hp[at].astype(F32)+hrecv[k][s][c].astype(F32)).astype(BF)
                if j<n: hp[at]=new
                else: hg[c,rows_at(kr,nr),:]=new[0]
            elif j>n: hgat(k,backs[k][j-n-1],c,True).wait_recv()
        for k in range(HK):
            if j<n: hsum(k,j,c).start()
            elif j<last: hgat(k,backs[k][j-n],c,False).start()
        if j==last: heads_out[c]=hg[c]
    def gather_step(j,c):
        if 0<j<=n:
            for k in range(K): gat(k,n-j,c,True).wait_recv()
        if j<n:
            for k in range(K): gat(k,n-1-j,c,False).start()
        elif j==n: chip(c,False).start()
        else:
            chip(c,True).wait_recv()
            fput(c).start()
    HT=D//HC
    def weight_grads(t):
        r=rows_at(t*HT,HT)
        parts=[dot(normT[r,:],d[...],NN).astype(BF) for d in (dq,dk,dv)]+[gwo[r,:]]
        for q in range(2):
            y=jnp.concatenate([z[:,q*(C//2):(q+1)*(C//2)] for z in parts],1)
            for i in range(y.shape[1]//128): hp[t,q,i*HT:(i+1)*HT,:]=y[:,i*128:(i+1)*128]
    def norm_grad(core,t):
        rr=rows_at(core*T+t*TT,TT)
        return dot(dq[rr,:],wh[0],NN)+dot(dk[rr,:],wh[1],NN)+dot(dv[rr,:],wh[2],NN)
    def other_half(t): obuf[rows_at(t*TT,TT),:]=norm_grad(1-p.th,t).astype(BF)
    def own_half(t): own[rows_at(t*TT,TT),:]=norm_grad(p.th,t)
    def norm_one_back(i):
        quarter=(1-i)*(1-p.tw)+i*p.tw
        for t in range(Q//128):
            r=rows_at(quarter*Q+t*128,128)
            e=own[r,:]+orecv[r,:].astype(F32)
            nn,rs=norm_parts(x[r,:].astype(F32))
            tbuf[r,:]=(gm[r,:]+norm_back(e,nn,rs,vin[4:5,:])).astype(BF)
            vrow[0:1,:]+=colsum(e*nn); vrow[1:2,:]+=colsum(e)
    def vectors(_):
        tok[p.tw]=tbuf[rows_at(p.tw*Q,Q),:]
        rows=[vrow[0:1,:],vrow[1:2,:]]+[vec[i:i+1,:] for i in range(4)]+[gbu[...]]
        at=0
        for v in rows:
            for i in range(v.shape[1]//128):
                vbuf[0,at:at+1,:]=v[:,i*128:(i+1)*128]; at+=1
        for i,d in enumerate((dq,dv)):
            bs=colsum(d[...].astype(F32))
            for q in range(2):
                quarter=2*p.th+(p.tw if q==0 else 1-p.tw)
                y=jnp.concatenate([bs[:,q*(C//2):(q+1)*(C//2)],jnp.zeros((1,256-C//2),F32)],1)
                for z in range(2):
                    vbuf[0,pl.ds(at+quarter*4+i*2+z,1),:]=y[:,z*128:(z+1)*128]
    def vector_step(i,_):
        if i>0:
            vcopy(i-1).wait_recv()
            y=vbuf[i-1]+vrecv[i-1]
            if i<len(vaxes): vbuf[i]=y
            else: vec_out[...]=y
        if i<len(vaxes): vcopy(i).start()
    part=functools.partial
    NT_=T//TT; G1=HC; G2=G1+2*NT_
    steps=[(1+HLAG*j,HSP,HC,part(head_step,j)) for j in reversed(range(last+1))]
    steps+=[(GLAG*j,2,CH,part(gather_step,j)) for j in reversed(range(n+2))]
    steps+=[(G2+3+VLAG*i,1,1,part(vector_step,i)) for i in range(len(vaxes)+1)]
    steps+=[(0,1,1,lambda _: arrived(0,5)),(0,1,HC,weight_grads),(G1,1,1,lambda _: arrived(5,6)),(G2,1,1,lambda _: arrived(6,8)),(G1,1,NT_,other_half),(G1+NT_,1,1,lambda _: ocopy().start()),(G1+NT_,1,NT_,own_half),
            (G2,1,1,lambda _: ocopy().wait_recv()),(G2+1,1,1,lambda _: tcopy().start()),(G2,1,2,norm_one_back),(G2+2,1,1,vectors)]
    run_steps(steps)
    def drain(c,_):
        chip(c,False).wait_send(); fput(c).wait()
        for k in range(K):
            for s in range(n): gat(k,s,c,False).wait_send()
        return 0
    lax.fori_loop(0,CH,drain,0)
    def hdrain(c,_):
        for k in range(HK):
            for s in range(n): hsum(k,s,c).wait_send()
            for s in backs[k]: hgat(k,s,c,False).wait_send()
        return 0
    lax.fori_loop(0,HC,hdrain,0)
    for i in range(len(vaxes)): vcopy(i).wait_send()
    ocopy().wait_send(); tcopy().wait()
    tok[1-p.tw]=trecv[...]

def finish(dp,red,dq,dk,dv,normT,wh,gwo,x,gm,vin,vec,gbu):
    T,D=x.shape; CH,fin,_=red.shape; R=FC//128*D
    plan=big_plan(dp,R); n=len(plan[0][0])
    HC=D//TT; HR=2*dq.shape[1]//128*TT; hplan=head_plan(dp,HR)
    hrecv=[]
    for order,_,rows in hplan:
        q=2
        for axis in order:
            if axis=="tw": q=1
            else: rows//=2
            hrecv.append(pltpu.VMEM((HC,q,rows,128),BF))
    V=(6*D+gbu.shape[1])//128+16; nv=n+1; args=(red,dq,dk,dv,normT,wh,gwo,x,gm,vin,vec,gbu)
    return pl.pallas_call(functools.partial(finish_kernel,dp),
      in_specs=[pl.BlockSpec(memory_space=pl.ANY if 1<=i<=8 else pltpu.VMEM) for i in range(len(args))],
      out_specs=[pl.BlockSpec(memory_space=pl.ANY)]+[pl.BlockSpec(memory_space=pltpu.VMEM)]*3,
      out_shape=[jax.ShapeDtypeStruct((CH,2,R,128),BF),jax.ShapeDtypeStruct((HC,HR,128),BF),jax.ShapeDtypeStruct((V,128),F32),jax.ShapeDtypeStruct((2,T//2,D),BF)],
      scratch_shapes=[pltpu.VMEM((CH,2,R,128),BF),pltpu.SemaphoreType.DMA((CH,))]+[pltpu.VMEM(a.shape,a.dtype) for a in args[1:9]]+[pltpu.SemaphoreType.DMA((8,)),pltpu.VMEM((HC,2,HR,128),BF),pltpu.VMEM((HC,HR,128),BF),pltpu.VMEM((nv,V,128),F32),pltpu.VMEM((nv,V,128),F32),pltpu.VMEM((T,D),F32)]+[pltpu.VMEM((T,D),BF)]*3+[pltpu.VMEM((T//2,D),BF),pltpu.VMEM((8,D),F32)]+[pltpu.SemaphoreType.DMA((2,))]*2+hrecv
        +[pltpu.SemaphoreType.DMA((len(plan),n,CH))]*2+[pltpu.SemaphoreType.DMA((CH,))]*2+[pltpu.SemaphoreType.DMA((len(hplan),n,HC))]*4+[pltpu.SemaphoreType.DMA((nv,))]*2,
      compiler_params=pltpu.CompilerParams(vmem_limit_bytes=60*2**20,collective_id=1,has_side_effects=True),name="finish_gradients")(*args)

def widen_kernel(where,chunk,heads,mine,got,vec,wup,wdown,wqkv,wout,blk,*vectors):
    D=wup.shape[0]; q=wout.shape[0]; g=pl.program_id(0); HT=D//heads.shape[0]
    for i in range(FC//128):
        cols=slice(i*128,(i+1)*128)
        wup[:,cols]=chunk[0,i*D:(i+1)*D,:].astype(F32)
        wdown[cols,:]=chunk[1,i*D:(i+1)*D,:].T.astype(F32)
    @pl.when(g==0)
    def _():
        for t in range(heads.shape[0]):
            y=jnp.concatenate([heads[t,i*HT:(i+1)*HT,:] for i in range(heads.shape[1]//HT)],1).T.astype(F32)
            rr=slice(t*HT,(t+1)*HT)
            for c in range(3): wqkv[c,:,rr]=y[c*q:(c+1)*q,:]
            wout[:,rr]=y[3*q:,:]
        blk[where[0]]=mine[...]; blk[1-where[0]]=got[...]
        at=0
        for v in vectors:
            for i in range(v.shape[0]//128):
                v[i*128:(i+1)*128]=vec[at,:]; at+=1

def widen(tw,chunks,heads,mine,got,vec):
    CH,_,R,_=chunks.shape; D=R*128//FC; FF=CH*FC; q=heads.shape[0]*heads.shape[1]*128//(4*D); T2=mine.shape[0]
    outs=[(D,FF),(FF,D),(3,q,D),(q,D)]; sizes=[D]*6+[FF]
    res=pl.pallas_call(widen_kernel,grid=(CH,),
      in_specs=[pl.BlockSpec(memory_space=pltpu.SMEM),pl.BlockSpec((None,2,R,128),lambda g:(g,0,0,0))]+[pl.BlockSpec(memory_space=pltpu.VMEM)]*4,
      out_specs=[pl.BlockSpec((D,FC),lambda g:(0,g)),pl.BlockSpec((FC,D),lambda g:(g,0))]+[pl.BlockSpec(memory_space=pltpu.VMEM)]*(3+len(sizes)),
      out_shape=[jax.ShapeDtypeStruct(o,F32) for o in outs]+[jax.ShapeDtypeStruct((2,T2,D),BF)]+[jax.ShapeDtypeStruct((z,),F32) for z in sizes],
      compiler_params=pltpu.CompilerParams(vmem_limit_bytes=50*2**20),name="widen")(tw.reshape(1),chunks,heads,mine,got,vec)
    return res[:5],res[5:]

def front_kernel(tok,w,b,vin,seg,x_o,normT_o,q_o,k_o,v_o,wh_o,mq_o,mk_o,x,norm,normT,qkv,wh,wgot,bgot,mq,mk,tsem,bsem,csem,ysem,xsem,osem):
    p=Peers(); Q,D=tok.shape[1:]; T=2*Q; L=2*T; E=w.shape[1]; HALF=E//2
    barrier(p,["th","tw",0])
    def tcopy(): return send(tok.at[1-p.tw],x.at[rows_at(p.tw*Q,Q),:],tsem.at[0],tsem.at[1],p.peer("tw"))
    def bcopy(): return send(b,bgot,bsem.at[0],bsem.at[1],p.peer("tw"))
    def ycopy(c):
        r=rows_at(p.bit(0)*HALF,HALF)
        return send(w.at[c,r,:],wgot.at[c,r,:],ysem.at[0,c],ysem.at[1,c],p.peer("tw"))
    def xcopy(c,landed):
        ref=wgot.at[c,rows_at((1-p.bit(0) if landed else p.bit(0))*HALF,HALF),:]
        return send(ref,ref,xsem.at[0,c],xsem.at[1,c],p.peer(0))
    def ccopy(i,landed):
        core=1-p.th if landed else p.th
        quarter=p.tw if i==0 else 1-p.tw
        ref=norm.at[rows_at(core*T+quarter*Q,Q),:]
        return send(ref,ref,csem.at[0,i],csem.at[1,i],p.peer("th"))
    tcopy().start(); bcopy().start()
    for c in range(3): ycopy(c).start()
    def normalize(src,row):
        for t in range(Q//128):
            v=src(t)
            y=(norm_parts(v.astype(F32))[0]*vin[4:5,:]+vin[5:6,:]).astype(BF)
            norm[rows_at(row+t*128,128),:]=y
    def put(src,dst,i): return pltpu.make_async_copy(src,dst,osem.at[i])
    x[rows_at(p.tw*Q,Q),:]=tok[p.tw]
    normalize(lambda t: tok[p.tw,t*128:(t+1)*128,:],p.th*T+p.tw*Q)
    onehot=lax.broadcasted_iota(jnp.int32,(128,L),0)
    same=onehot==seg[...]
    mk[...]=jnp.where(same,1.0,0.0).T.astype(BF)
    ccopy(0,False).start()
    mq[...]=jnp.where(same|(onehot>=8),0.0,-float(2**40)).T.astype(BF)
    put(mk,mk_o,0).start(); put(mq,mq_o,1).start()
    tcopy().wait_recv()
    normalize(lambda t: x[rows_at((1-p.tw)*Q+t*128,128),:],p.th*T+(1-p.tw)*Q)
    put(x,x_o,2).start()
    bcopy().wait_recv()
    tiles=[slice(t*TT,(t+1)*TT) for t in range(L//TT)]
    def bias(c,ref): return ref[c//2:c//2+1,:] if c!=1 else None
    def project(c,wt,bs,r):
        y=dot(norm[r,:],wt,NT)
        if bs is not None: y=y+bs
        y=y.astype(BF)
        return y*BF(0.125) if c==0 else y
    ccopy(1,False).start()
    ccopy(0,True).wait_recv()
    ccopy(1,True).wait_recv()
    for c in range(3):
        for r in tiles: qkv[c,r,0:E]=project(c,w[c],bias(c,b),r)
    for r in tiles: normT[:,r]=norm[r,:].T
    put(normT,normT_o,3).start()
    for c in range(3):
        ycopy(c).wait_recv()
        xcopy(c,False).start()
    for c in range(3):
        xcopy(c,True).wait_recv()
        for r in tiles: qkv[c,r,E:2*E]=project(c,wgot[c],bias(c,bgot),r)
        put(qkv.at[c],(q_o,k_o,v_o)[c],4+c).start()
        wh[c,0:E,:]=w[c]; wh[c,E:2*E,:]=wgot[c]
    put(wh,wh_o,7).start()
    for src,dst,i in ((mk,mk_o,0),(mq,mq_o,1),(x,x_o,2),(normT,normT_o,3),(wh,wh_o,7)): put(src,dst,i).wait()
    for c in range(3):
        put(qkv.at[c],(q_o,k_o,v_o)[c],4+c).wait()
        ycopy(c).wait_send(); xcopy(c,False).wait_send()
    tcopy().wait_send(); bcopy().wait_send()
    for i in range(2): ccopy(i,False).wait_send()

def front(tok,w,b,vin,seg):
    _,Q,D=tok.shape; T=2*Q; L=2*T; E=w.shape[1]
    outs=[((T,D),BF),((D,L),BF)]+[((L,2*E),BF)]*3+[((3,2*E,D),BF)]+[((L,128),BF)]*2
    sem=pltpu.SemaphoreType.DMA
    return pl.pallas_call(front_kernel,
      in_specs=[pl.BlockSpec(memory_space=pltpu.VMEM)]*5,out_specs=[pl.BlockSpec(memory_space=pl.ANY)]*len(outs),
      out_shape=[jax.ShapeDtypeStruct(*o) for o in outs],
      scratch_shapes=[pltpu.VMEM((T,D),BF),pltpu.VMEM((L,D),BF),pltpu.VMEM((D,L),BF),pltpu.VMEM((3,L,2*E),BF),pltpu.VMEM((3,2*E,D),BF),pltpu.VMEM((3,E,D),BF),
        pltpu.VMEM(b.shape,F32),pltpu.VMEM((L,128),BF),pltpu.VMEM((L,128),BF),sem((2,)),sem((2,)),sem((2,2)),sem((2,3)),sem((2,3)),sem((8,))],
      compiler_params=pltpu.CompilerParams(vmem_limit_bytes=60*2**20,collective_id=2,has_side_effects=True),name="front")(tok,w,b,vin,seg)


SWAP = [(0, 1), (1, 0)]


def swap(value, axis):
    return lax.ppermute(value, axis, SWAP)


def in_order(mine, other, index, axis):
    return jnp.where(
        index == 0, jnp.concatenate([mine, other], axis), jnp.concatenate([other, mine], axis)
    )


def own_row(rows, tw):
    mine = lax.dynamic_index_in_dim(rows, tw, 0, keepdims=False)
    other = lax.dynamic_index_in_dim(rows, 1 - tw, 0, keepdims=False)
    return in_order(mine, swap(other, "tw"), tw, 0)


def body(
    dp_size,
    tokens,
    segment_ids,
    norm1_gain,
    norm1_shift,
    w_qkv,
    b_qv,
    w_out,
    b_out,
    norm2_gain,
    norm2_shift,
    w_up,
    b_up,
    w_down,
    b_down,
    cotangent,
):
    th, tw = lax.axis_index("th"), lax.axis_index("tw")
    d = tokens.shape[-1]
    mine = w_qkv.shape[2]
    vectors = jnp.stack([b_out, norm2_gain, norm2_shift, b_down, norm1_gain, norm1_shift, b_down, b_down])
    seg = lax.dynamic_index_in_dim(segment_ids, tw, 0)
    x, normed_t, query, key, value, w_heads, mq, mk = front(
        tokens, w_qkv.transpose(0, 2, 1), b_qv, vectors, seg
    )
    tables = (mq, mk, *block_ranges(seg[0]))
    later = lax.optimization_barrier((cotangent, w_out, query))
    cot = own_row(later[0], tw)
    w_out_heads = jnp.concatenate([w_out, swap(later[1], "tw")], 0)
    attended, totals = attn_fwd(query, key, value, *tables)
    out_mine, out_other, grad_middle, grad_b_up, sums, red, grad_heads, grad_w_out = ffn(
        dp_size, attended, w_out_heads, x, vectors, cot, w_up, w_down, b_up[None]
    )
    out_got = swap(out_other, "tw")
    dq, dk, dv = attn_bwd(query, key, value, grad_heads, attended, totals, *tables)
    chunks, heads, small, grad_tokens = finish(
        dp_size, red, dq, dk, dv, normed_t, w_heads, grad_w_out, x, grad_middle, vectors, sums, grad_b_up
    )
    (up, down, w_qkv_grad, w_out_grad, block_out), vecs = widen(tw, chunks, heads, out_mine, out_got, small)
    b_qv_grad = lax.dynamic_slice_in_dim(small[-16:].reshape(4, 2, 256), 2 * th + tw, 1, 0)[0, :, :mine]
    return (
        block_out,
        grad_tokens,
        vecs[0],
        vecs[1],
        w_qkv_grad.transpose(0, 2, 1),
        b_qv_grad,
        w_out_grad,
        vecs[2],
        vecs[3],
        vecs[4],
        up,
        vecs[6],
        down,
        vecs[5],
    )


def solution(mesh):
    return jax.shard_map(
        functools.partial(body, mesh.shape["dp"]),
        mesh=mesh,
        in_specs=(
            P("dp", ("th", "tw"), None),
            P("dp", None),
            P(),
            P(),
            P(None, None, ("th", "tw")),
            P(None, ("th", "tw")),
            P(("th", "tw"), None),
            P(),
            P(),
            P(),
            P(),
            P(),
            P(),
            P(),
            P("dp", ("th", "tw"), None),
        ),
        out_specs=(
            P("dp", ("th", "tw"), None),
            P("dp", ("th", "tw"), None),
            P(),
            P(),
            P(None, None, ("th", "tw")),
            P(None, ("th", "tw")),
            P(("th", "tw"), None),
            P(),
            P(),
            P(),
            P(),
            P(),
            P(),
            P(),
        ),
        check_vma=False,
    )
```

time: 311 us -> 272 us (0.87)
  Pallas kernels: 287 us -> 253 us
  local copies, waits for them, and re-layouts: 15.7 us -> 10.8 us
    pallas_call x3, Pallas kernels: 197 us -> 153 us  [the longest x1 79.3 us: finish(): pl.pallas_call(functools.partial(finish_kernel, dp), in_specs=[pl.BlockSp...]
    pallas_call x1, Pallas kernels: 27.7 us -> 34.8 us  [attn_bwd(): pl.pallas_call(bwd_kernel, grid_spec=pltpu.PrefetchScalarGridSpec(num_sca...]
    pallas_call x1, Pallas kernels: 20.7 us -> 26.8 us  [attn_fwd(): pl.pallas_call(fwd_kernel, grid_spec=pltpu.PrefetchScalarGridSpec(num_sca...]
    unnamed x23 -> x13, local copies, waits for them, and re-layouts: 7.65 us -> 3.08 us
    another operation x6 -> x7, local copies, waits for them, and re-layouts: 0.66 us -> 4.87 us  [body(): jnp.stack([b_out, norm2_gain, norm2_shift, b_down, norm1_gain, norm1_shif...]
    pallas_call x1, Pallas kernels: 41.5 us -> 37.7 us  [front(): pl.pallas_call(front_kernel, in_specs=[pl.BlockSpec(memory_space=pltpu.VM...]
  transfers between devices with their start and end apart: 3 -> 3, of which waited for: 0 -> 0; matrix products, arithmetic and copies ran while one was open for 2% -> 1% of each run, Pallas kernels for 49% -> 52%
where the time goes in v1:
time: 272 us; the launch traced here: 271 us
  Pallas kernels  253 us (93%)
  local copies, waits for them, and re-layouts  10.8 us (4%)
  starting transfers between devices  3.37 us (1%)
  other arithmetic  3.08 us (1%)
    pallas_call x1, Pallas kernels, finish(): pl.pallas_call(functools.partial(finish_kernel, dp), in_specs=[pl.BlockSp...  79.3 us
    pallas_call x1, Pallas kernels, ffn(): pl.pallas_call(functools.partial(ffn_kernel, dp), in_specs=[whole(v.shape...  60.9 us
    pallas_call x1, Pallas kernels, front(): pl.pallas_call(front_kernel, in_specs=[pl.BlockSpec(memory_space=pltpu.VM...  37.7 us
    pallas_call x1, Pallas kernels, attn_bwd(): pl.pallas_call(bwd_kernel, grid_spec=pltpu.PrefetchScalarGridSpec(num_sca...  34.8 us
    pallas_call x1, Pallas kernels, attn_fwd(): pl.pallas_call(fwd_kernel, grid_spec=pltpu.PrefetchScalarGridSpec(num_sca...  26.8 us
    pallas_call x1, Pallas kernels, widen(): pl.pallas_call(widen_kernel, grid=(CH,), in_specs=[pl.BlockSpec(memory_sp...  13.2 us
  transfers between devices with their start and end apart: 3, of which 0 were waited for; matrix products, arithmetic and copies ran while one was open for 1% of the time, Pallas kernels for 52%

profile of v1, /device:TPU:0, one launch (start us, length us, event | category | flops | bytes accessed | tf_op | source)
XLA Modules:
  0.0 270.7 jit_solution(13933450513045020460)
XLA Ops:
  0.7 0.8 stack.23
  1.4 0.7 stack.24
  2.1 0.7 stack.25
  2.8 0.7 stack.26
  3.5 0.7 stack.27
  4.2 0.7 stack.28
  4.9 1.3 fusion
  6.2 0.6 stack.29.vin
  6.8 37.7 %front.1 = (bf16[768,768]{1,0:T(8,128)(2,1)}, bf16[768,1536]{1,0:T(8,128)(2,1)}, bf16[1536,384]{1,0:T(8,128)(2,1)}, bf16[1536,384]{1,0:T(8,128)(2,1)}, bf16[1536...) custom-call(bf16[2,384,768]{2,1,0:T(8,128)(2,1)} %tok.1, ...), custom_call_target="tpu_custom_call" | custom-call | tf_op jit(solution)/shard_map/front/pallas_call | solution.py:614
  44.6 1.6 collective-permute-start.1
  46.2 0.8 collective-permute-start
  48.0 26.8 %attention_forward.1 = (bf16[1536,384]{1,0:T(8,128)(2,1)}, f32[8,1536]{1,0:T(8,128)}) custom-call(s32[6]{0:T(128)} %get-tuple-element.99.lo_ref, s32[6]{0:T(128)} %get-tuple-element.98.hi_ref, bf16[1536,384]{1,0:T(8,128)(2,1)} %get-tuple-element.53.q_ref, bf16[1536,384]{1,0:T(8,128)(2,1)} %get-tuple-element.54.k_ref, ...), custom_call_target="tpu_custom_call" | custom-call | tf_op jit(solution)/shard_map/attention_forward/pallas_call | solution.py:57
  74.8 0.9 pad_maximum_fusion.wo
  75.7 1.5 maximum_select_fusion.cot
  77.1 60.9 %feed_forward.1 = (bf16[384,768]{1,0:T(8,128)(2,1)}, bf16[384,768]{1,0:T(8,128)(2,1)}, f32[768,768]{1,0:T(8,128)}, f32[1,3072]{1,0:T(1,128)}, f32[8,768]{1,0:T(8...) custom-call(bf16[1536,384]{1,0:T(8,128)(2,1)} %get-tuple-element.58.att.o_ref, ...), custom_call_target="tpu_custom_call" | custom-call | tf_op jit(solution)/shard_map/feed_forward/pallas_call | solution.py:351
  138.0 1.0 collective-permute-start.2
  138.9 34.8 %attention_backward.1 = (bf16[1536,384]{1,0:T(8,128)(2,1)}, bf16[1536,384]{1,0:T(8,128)(2,1)}, bf16[1536,384]{1,0:T(8,128)(2,1)}) custom-call(s32[6]{0:T(128)} %get-tuple-element.99.lo_ref, s32[6]{0:T(128)} %get-tuple-element.98.hi_ref, bf16[1536,384]{1,0:T(8,128)(2,1)} %get-tuple-element.53.q_ref, bf16[1536,384]{1,0:T(8,128)(2,1)} %get-tuple-element.54.k_ref, ...), custom_call_target="tpu_custom_call" | custom-call | tf_op jit(solution)/shard_map/attention_backward/pallas_call | solution.py:114
  173.8 79.3 %finish_gradients.1 = (bf16[6,2,3072,128]{3,2,1,0:T(8,128)(2,1)}, bf16[3,1536,128]{2,1,0:T(8,128)(2,1)}, f32[76,128]{1,0:T(8,128)}, bf16[2,384,768]{2,1,0:T(8,128)(2,1)}) custom-call(bf16[6,192,128]{2,1,0:T(8,128)(2,1)} %get-tuple-element.62.red, bf16[1536,384]{1,0:T(8,128)(2,1)} %get-tuple-element.65.dq_h, bf16[1536,384]{1,0:T(8,128)(2,1)} %get-tuple-element.66.dk_h, ...), custom_call_target="tpu_custom_call" | custom-call | tf_op jit(solution)/shard_map/finish_gradients/pallas_call | solution.py:507
  253.1 0.7 slice.14
  253.8 0.6 dynamic-slice_bitcast_fusion.2
  254.4 1.3 copy-done
  255.7 0.8 copy-done.2
  256.5 13.2 %widen.1 = (f32[768,3072]{1,0:T(8,128)}, f32[3072,768]{1,0:T(8,128)}, f32[3,192,768]{2,1,0:T(8,128)}, f32[192,768]{1,0:T(8,128)}, bf16[2,384,768]{2,1,0:T(8,128)...) custom-call(s32[1]{0:T(128)} %bitcast.where, ...), custom_call_target="tpu_custom_call" | custom-call | tf_op jit(solution)/shard_map/widen/pallas_call | solution.py:537
  269.7 1.0 copy.30
  (19 shorter events, 1.1 us)
Async XLA Ops:
  0.6 43.9 %copy-start.3 = (bf16[2,384,768]{2,1,0:T(8,128)(2,1)S(1)}, bf16[2,384,768]{2,1,0:T(8,128)(2,1)}, u32[]{:S(2)}) copy-start(bf16[2,384,768]{2,1,0:T(8,128)(2,1)} %param.29) | copy-start | bytes 3538948
  44.5 1.7 copy-start.5
  44.6 31.0 %collective-permute-start.1 = (bf16[384,768]{1,0:T(8,128)(2,1)S(1)}, bf16[384,768]{1,0:T(8,128)(2,1)S(1)}, u32[]{:S(2)}, u32[]{:S(2)}) collective-permute-start(bf16[384,768]{1,0:T(8,128)(2,1)S(1)} %get-tuple-element.97), channel_id=1, source_target_pairs={{0,1},{1,0},{2,3},{3,2},{4,5},{5,4},{6,7},{7,6},{8,9},{9,8},{10,11... | collective-permute-start | bytes 1769480 | tf_op jit(solution)/shard_map/ppermute | solution.py:626
  46.2 28.6 %collective-permute-start = (bf16[192,768]{1,0:T(8,128)(2,1)S(1)}, bf16[192,768]{1,0:T(8,128)(2,1)S(1)}, u32[]{:S(2)}, u32[]{:S(2)}) collective-permute-start(bf16[192,768]{1,0:T(8,128)(2,1)S(1)} %copy-done.5), channel_id=1, source_target_pairs={{0,1},{1,0},{2,3},{3,2},{4,5},{5,4},{6,7},{7,6},{8,9},{9,8},{10,11... | collective-permute-start | bytes 884744 | tf_op jit(solution)/shard_map/ppermute | solution.py:626
  138.0 116.4 %collective-permute-start.2 = (bf16[384,768]{1,0:T(8,128)(2,1)}, bf16[384,768]{1,0:T(8,128)(2,1)S(1)}, u32[]{:S(2)}, u32[]{:S(2)}) collective-permute-start(bf16[384,768]{1,0:T(8,128)(2,1)} %get-tuple-element.77), channel_id=1, source_target_pairs={{0,1},{1,0},{2,3},{3,2},{4,5},{5,4},{6,7},{7,6},{8,9},{9,8},{10,11... | collective-permute-start | bytes 1769480 | tf_op jit(solution)/shard_map/ppermute | solution.py:626
  173.7 80.7 %copy-start.1 = (bf16[384,768]{1,0:T(8,128)(2,1)S(1)}, bf16[384,768]{1,0:T(8,128)(2,1)}, u32[]{:S(2)}) copy-start(bf16[384,768]{1,0:T(8,128)(2,1)} %get-tuple-element.76.mine) | copy-start | bytes 1769476
  254.4 1.3 copy-start
  255.7 0.8 copy-start.2
  256.5 13.2 %copy-start.4 = (bf16[2,384,768]{2,1,0:T(8,128)(2,1)S(1)}, bf16[2,384,768]{2,1,0:T(8,128)(2,1)}, u32[]{:S(2)}) copy-start(bf16[2,384,768]{2,1,0:T(8,128)(2,1)} %get-tuple-element.115) | copy-start | bytes 3538948

commit v2 on v1

--- a/solution.py
+++ b/solution.py
@@ -12,59 +12,78 @@
 BQ=256; BK=256; HD=64
 def dot(a,b,d): return lax.dot_general(a,b,d,preferred_element_type=F32)
 
-def fwd_kernel(lo_ref, hi_ref, q_ref, k_ref, v_ref, mq_ref, mk_ref, o_ref, lse_ref, m_ref, l_ref, acc_ref):
-    i=pl.program_id(0)
-    pairs=q_ref.shape[1]//128
+AL=128; VR=80
+def key_rows(lo_ref,mk_ref,i,j):
+    L=mk_ref.shape[0]
+    want=lo_ref[i]+j*BK
+    start=pl.multiple_of(jnp.minimum(want,L-BK),AL)
+    row=lax.broadcasted_iota(jnp.int32,(BK,128),0); lane=lax.broadcasted_iota(jnp.int32,(BK,128),1)
+    ks=pl.ds(start,BK)
+    return ks,jnp.where((lane==8)&(row<want-start),jnp.ones((BK,128),BF),mk_ref[ks,:])
+
+def fwd_kernel(lo_ref, n_ref, q_ref, k_ref, v_ref, mq_ref, mk_ref, o_ref, lse_ref, m_ref, acc_ref, vT_ref, *score_refs):
+    i=pl.program_id(0); H=q_ref.shape[1]//HD
     lane=lax.broadcasted_iota(jnp.int32,(1,128),1)
     halves=(lane<HD, lane>=HD)
+    @pl.when(i==0)
+    def _():
+        row=lax.broadcasted_iota(jnp.int32,(VR-HD,v_ref.shape[0]),0)
+        for p in range(H//2):
+            t=v_ref[:,p*128:(p+1)*128].T
+            for e in range(2):
+                vT_ref[2*p+e,0:HD,:]=t[e*HD:(e+1)*HD,:]
+                vT_ref[2*p+e,HD:VR,:]=jnp.where(row==0,1.0,0.0).astype(BF)
     m_ref[...]=jnp.full(m_ref.shape,-1e30,F32)
-    l_ref[...]=jnp.zeros_like(l_ref)
     acc_ref[...]=jnp.zeros_like(acc_ref)
-    def body(j,_):
-        ks=pl.ds(pl.multiple_of(j*BK,BK),BK)
-        mk=mk_ref[ks,:]
-        for p in range(pairs):
-            cols=slice(p*128,(p+1)*128)
-            qx=jnp.concatenate([q_ref[:,cols],mq_ref[...]],1)
-            k2=k_ref[ks,cols]; v2=v_ref[ks,cols]
-            ps=[]
-            for e in range(2):
-                h=2*p+e
-                kx=jnp.concatenate([jnp.where(halves[e],k2,jnp.zeros_like(k2)),mk],1)
-                s=dot(kx,qx,NT)
-                m_old=m_ref[h:h+1,:]
-                m_new=jnp.maximum(m_old,jnp.max(s,axis=0,keepdims=True))
-                alpha=jnp.exp(m_old-m_new)
-                pe=jnp.exp(s-m_new)
-                l_ref[h:h+1,:]=l_ref[h:h+1,:]*alpha+jnp.sum(pe,axis=0,keepdims=True)
-                m_ref[h:h+1,:]=m_new
-                acc_ref[h*HD:(h+1)*HD,:]=acc_ref[h*HD:(h+1)*HD,:]*alpha
-                ps.append(pe.astype(BF))
-            vcat=jnp.concatenate([jnp.where(halves[0],v2,jnp.zeros_like(v2)),jnp.where(halves[1],v2,jnp.zeros_like(v2))],0)
-            acc_ref[cols,:]+=dot(vcat,jnp.concatenate(ps,0),TN)
+    def score(h,ks,mk):
+        cols=slice(h//2*128,h//2*128+128)
+        k2=k_ref[ks,cols]
+        return dot(jnp.concatenate([jnp.where(halves[h%2],k2,jnp.zeros_like(k2)),mk],1),jnp.concatenate([q_ref[:,cols],mq_ref[...]],1),NT)
+    def soft(h,s):
+        m_old=m_ref[h:h+1,:]
+        m_new=jnp.maximum(m_old,jnp.max(s,axis=0,keepdims=True))
+        m_ref[h:h+1,:]=m_new
+        return jnp.exp(s-m_new).astype(BF),jnp.exp(m_old-m_new)
+    def weigh(h,ks,pe,alpha):
+        acc_ref[h]=acc_ref[h]*alpha+dot(vT_ref[h,:,ks],pe,NN)
+    n=n_ref[i]
+    def half(j,now,then):
+        ks,_=key_rows(lo_ref,mk_ref,i,j)
+        kn,mk=key_rows(lo_ref,mk_ref,i,j+1)
+        last=None
+        for h in range(H):
+            then[h]=score(h,kn,mk)
+            probs=soft(h,now[h])
+            if last is not None: weigh(h-1,ks,*last)
+            last=probs
+        weigh(H-1,ks,*last)
+    ks,mk=key_rows(lo_ref,mk_ref,i,0)
+    for h in range(H): score_refs[0][h]=score(h,ks,mk)
+    def body(t,_):
+        half(2*t,*score_refs)
+        @pl.when(2*t+1<n)
+        def _(): half(2*t+1,*score_refs[::-1])
         return 0
-    lax.fori_loop(lo_ref[i],hi_ref[i],body,0)
-    for p in range(pairs):
-        parts=[]
-        for e in range(2):
-            h=2*p+e
-            parts.append(acc_ref[h*HD:(h+1)*HD,:]*(1.0/l_ref[h:h+1,:]))
+    lax.fori_loop(0,(n+1)//2,body,0)
+    for p in range(H//2):
+        parts=[acc_ref[h,0:HD,:]*(1.0/acc_ref[h,HD:HD+1,:]) for h in (2*p,2*p+1)]
         o_ref[:,p*128:(p+1)*128]=jnp.concatenate(parts,0).T.astype(BF)
-    lse_ref[...]=m_ref[...]+jnp.log(jnp.maximum(l_ref[...],1e-37))
-
-def attn_fwd(q,k,v,mq,mk,lo,hi):
+    for h in range(H): lse_ref[h:h+1,:]=m_ref[h:h+1,:]+jnp.log(acc_ref[h,HD:HD+1,:])
+    lse_ref[H:,:]=jnp.zeros((lse_ref.shape[0]-H,BQ),F32)
+
+def attn_fwd(q,k,v,mq,mk,lo,n):
     L,C=q.shape
     return pl.pallas_call(fwd_kernel,
         grid_spec=pltpu.PrefetchScalarGridSpec(num_scalar_prefetch=2,grid=(L//BQ,),
           in_specs=[pl.BlockSpec((BQ,C),lambda i,*_:(i,0)),pl.BlockSpec((L,C),lambda i,*_:(0,0)),pl.BlockSpec((L,C),lambda i,*_:(0,0)),
                     pl.BlockSpec((BQ,128),lambda i,*_:(i,0)),pl.BlockSpec((L,128),lambda i,*_:(0,0))],
           out_specs=[pl.BlockSpec((BQ,C),lambda i,*_:(i,0)),pl.BlockSpec((8,BQ),lambda i,*_:(0,i))],
-          scratch_shapes=[pltpu.VMEM((8,BQ),F32),pltpu.VMEM((8,BQ),F32),pltpu.VMEM((C,BQ),F32)]),
+          scratch_shapes=[pltpu.VMEM((8,BQ),F32),pltpu.VMEM((C//HD,VR,BQ),F32),pltpu.VMEM((C//HD,VR,L),BF),pltpu.VMEM((C//HD,BK,BQ),F32),pltpu.VMEM((C//HD,BK,BQ),F32)]),
         out_shape=[jax.ShapeDtypeStruct((L,C),BF),jax.ShapeDtypeStruct((8,L),F32)],
         name="attention_forward",
-    )(lo,hi,q,k,v,mq,mk)
-
-def bwd_kernel(lo_ref, hi_ref, q_ref, k_ref, v_ref, do_ref, o_ref, lse_ref, mq_ref, mk_ref, dq_ref, dk_ref, dv_ref, dk_acc, dv_acc, dq_acc, qcat, docat):
+    )(lo,n,q,k,v,mq,mk)
+
+def bwd_kernel(lo_ref, n_ref, q_ref, k_ref, v_ref, do_ref, o_ref, lse_ref, mq_ref, mk_ref, dq_ref, dk_ref, dv_ref, dk_acc, dv_acc, dq_acc, qcat, docat):
     i=pl.program_id(0); n=pl.num_programs(0)
     C=q_ref.shape[1]; pairs=C//128
     lane=lax.broadcasted_iota(jnp.int32,(1,128),1)
@@ -73,8 +92,10 @@
     def _():
         dk_acc[...]=jnp.zeros_like(dk_acc); dv_acc[...]=jnp.zeros_like(dv_acc)
     dq_acc[...]=jnp.zeros_like(dq_acc)
-    sel=(lax.broadcasted_iota(jnp.int32,(8,C),1)//HD==lax.broadcasted_iota(jnp.int32,(8,C),0)).astype(F32)
-    delta=lax.dot_general(sel,do_ref[...].astype(F32)*o_ref[...].astype(F32),NT,precision=lax.Precision.HIGHEST,preferred_element_type=F32)
+    sel=(lax.broadcasted_iota(jnp.int32,(8,C),1)//HD==lax.broadcasted_iota(jnp.int32,(8,C),0)).astype(BF)
+    prod=do_ref[...].astype(F32)*o_ref[...].astype(F32)
+    high=prod.astype(BF)
+    delta=dot(sel,high,NT)+dot(sel,(prod-high.astype(F32)).astype(BF),NT)
     for p in range(pairs):
         cols=slice(p*128,(p+1)*128)
         for e in range(2):
@@ -83,8 +104,7 @@
             docat[p,e*BQ:(e+1)*BQ,:]=jnp.where(halves[e],d2,jnp.zeros_like(d2))
     lse=lse_ref[...]
     def body(j,_):
-        ks=pl.ds(pl.multiple_of(j*BK,BK),BK)
-        mk=mk_ref[ks,:]
+        ks,mk=key_rows(lo_ref,mk_ref,i,j)
         for p in range(pairs):
             cols=slice(p*128,(p+1)*128)
             qx=jnp.concatenate([q_ref[:,cols],mq_ref[...]],1)
@@ -102,13 +122,13 @@
             dk_acc[ks,cols]+=dot(jnp.concatenate(dss,1),qcat[p],NN)
             dq_acc[cols,:]+=dot(jnp.concatenate(kms,0),jnp.concatenate(dss,0),TN)
         return 0
-    lax.fori_loop(lo_ref[i],hi_ref[i],body,0)
+    lax.fori_loop(0,n_ref[i],body,0)
     dq_ref[...]=(dq_acc[...]*0.125).T.astype(BF)
     @pl.when(i==n-1)
     def _():
         dk_ref[...]=dk_acc[...].astype(BF); dv_ref[...]=dv_acc[...].astype(BF)
 
-def attn_bwd(q,k,v,do,o,lse,mq,mk,lo,hi):
+def attn_bwd(q,k,v,do,o,lse,mq,mk,lo,n):
     L,C=q.shape
     blk=pl.BlockSpec((BQ,C),lambda i,*_:(i,0)); full=pl.BlockSpec((L,C),lambda i,*_:(0,0))
     return pl.pallas_call(bwd_kernel,
@@ -118,17 +138,17 @@
           scratch_shapes=[pltpu.VMEM((L,C),F32),pltpu.VMEM((L,C),F32),pltpu.VMEM((C,BQ),F32),pltpu.VMEM((C//128,2*BQ,128),BF),pltpu.VMEM((C//128,2*BQ,128),BF)]),
         out_shape=[jax.ShapeDtypeStruct((L,C),BF)]*3,
         name="attention_backward",
-    )(lo,hi,q,k,v,do,o,lse,mq,mk)
+    )(lo,n,q,k,v,do,o,lse,mq,mk)
 
 def block_ranges(seg):
     first=seg[::BQ]; last=seg[BQ-1::BQ]
-    lo=jnp.sum(seg[None,:]<first[:,None],axis=1,dtype=jnp.int32)//BK
-    hi=(jnp.sum(seg[None,:]<=last[:,None],axis=1,dtype=jnp.int32)+BK-1)//BK
-    return lo,hi
+    lo=jnp.sum(seg[None,:]<first[:,None],axis=1,dtype=jnp.int32)//AL*AL
+    hi=jnp.sum(seg[None,:]<=last[:,None],axis=1,dtype=jnp.int32)
+    return lo,(hi-lo+BK-1)//BK
 
 
 TT=256; FC=512
-LAG=2; GLAG=3; HLAG=3; HSP=2; GSP=4; VLAG=2; FL=3
+LAG=2; GLAG=5; HLAG=4; HSP=2; GSP=4; VLAG=5; FL=3
 
 def bits_of(dp): return dp.bit_length()-1
 
@@ -211,13 +231,14 @@
     return r*(t-jnp.mean(t,axis=-1,keepdims=True)-n*jnp.mean(t*n,axis=-1,keepdims=True))
 def colsum(x): return jnp.sum(x,axis=0,keepdims=True)
 
-def ffn_kernel(dp,att,wo,x,vin,cot,wu_h,wd_h,bu,mine,other,gm,gb,vec,red,gheads,gwo,
+def ffn_kernel(dp,att,wo,x,vb,vg,vs,vd,cot,wu_h,wd_h,bu,mine,other,gm,gb,vec,red,gheads,gwo,
                wu,wd,cotT,mid,n2,n2T,obuf,orecv,grow,act,gh,dw,chip_recv,wsem,osem,gsem,*rest):
     CH=dw.shape[0]; T,D=x.shape; SLOTS=chip_recv.shape[0]
     plan=big_plan(dp,dw.shape[2]); n=len(plan[0][0]); K=len(plan)
     recv=[rest[k*n:(k+1)*n] for k in range(K)]
     send_sem,recv_sem,chip_send,chip_got=rest[K*n:]
     p=Peers()
+    b_row,g_row,s_row,d_row=[v[...].reshape(1,D) for v in (vb,vg,vs,vd)]
     tiles=[slice(t*TT,(t+1)*TT) for t in range(T//TT)]; NT_=len(tiles)
     regs=[halves(p,*s) for s in plan]
     def copy(k,s,c):
@@ -240,7 +261,7 @@
     for r in tiles:
         obuf[r,:]=dot(att[rows_at((1-p.th)*T+r.start,TT),:],wo[...],NN).astype(BF)
     for t,r in enumerate(tiles):
-        mid[r,:]=x[r,:].astype(F32)+dot(att[rows_at(p.th*T+r.start,TT),:],wo[...],NN)+vin[0:1,:]
+        mid[r,:]=x[r,:].astype(F32)+dot(att[rows_at(p.th*T+r.start,TT),:],wo[...],NN)+b_row
         if t==0: ocopy().start()
         cotT[:,r]=cot[r,:].T
     ocopy().wait_recv()
@@ -248,7 +269,7 @@
         m=mid[r,:]+orecv[r,:].astype(F32)
         mid[r,:]=m
         nn,_=norm_parts(m)
-        y=(nn*vin[1:2,:]+vin[2:3,:]).astype(BF)
+        y=(nn*g_row+s_row).astype(BF)
         n2[r,:]=y; n2T[:,r]=y.T
     vec[...]=jnp.zeros_like(vec)
     def sum_step(s,c):
@@ -299,14 +320,14 @@
         for c in range(1,CH): e+=dot(gh[c,r,:],wu[c],NT)
         nn,rs=norm_parts(mid[r,:])
         ct=cot[r,:].astype(F32)
-        gmid=ct+norm_back(e,nn,rs,vin[1:2,:])
+        gmid=ct+norm_back(e,nn,rs,g_row)
         gm[r,:]=gmid
         gbr=gmid.astype(BF)
         grow[rows_at(p.th*T+t*TT,TT),:]=gbr
         vec[0:1,:]+=colsum(gbr.astype(F32)); vec[1:2,:]+=colsum(e*nn); vec[2:3,:]+=colsum(e); vec[3:4,:]+=colsum(ct)
     def block_out(t):
         r=rows_at(t*TT,TT)
-        y=mid[r,:]+vin[3:4,:]
+        y=mid[r,:]+d_row
         for c in range(CH): y+=dot(act[c,r,:],wd[c],NN)
         n2[r,:]=y.astype(BF)
     def split_out(_):
@@ -339,7 +360,7 @@
 def whole(shape):
     return pl.BlockSpec(memory_space=pltpu.VMEM)
 
-def ffn(dp,att,wo,x,vin,cot,wu,wd,bu):
+def ffn(dp,att,wo,x,vb,vg,vs,vd,cot,wu,wd,bu):
     T,D=x.shape; FF=wu.shape[1]; CH=FF//FC; R=FC//128*D; C=att.shape[1]
     plan=big_plan(dp,R); n=len(plan[0][0])
     fin=R>>n
@@ -349,14 +370,14 @@
     hbm=pl.BlockSpec(memory_space=pl.ANY)
     V=pltpu.VMEM; sem=pltpu.SemaphoreType.DMA
     return pl.pallas_call(functools.partial(ffn_kernel,dp),
-      in_specs=[whole(v.shape) for v in (att,wo,x,vin,cot)]+[hbm,hbm,whole(bu.shape)],
+      in_specs=[whole(v.shape) for v in (att,wo,x,vb,vg,vs,vd,cot)]+[hbm,hbm,whole(bu.shape)],
       out_specs=specs,out_shape=[jax.ShapeDtypeStruct(*o) for o in outs],
       scratch_shapes=[V((CH,D,FC),BF),V((CH,FC,D),BF),V((D,T),BF),V((T,D),F32),V((T,D),BF),V((D,T),BF),V((T,D),BF),V((T,D),BF),V((2*T,D),BF),
           V((CH,T,FC),BF),V((CH,T,FC),BF),V((CH,2,R,128),BF),V((3,R,128),BF),sem((2,CH)),sem((2,)),sem((2,))]+recv
         +[sem((len(plan),n,CH))]*2+[sem((CH,))]*2,
-      compiler_params=pltpu.CompilerParams(vmem_limit_bytes=63*2**20+2**19,collective_id=0,has_side_effects=True),name="feed_forward")(att,wo,x,vin,cot,wu,wd,bu)
-
-def finish_kernel(dp,red,dq_h,dk_h,dv_h,normT_h,wh_h,gwo_h,x_h,gm_h,vin,vec,gbu,gathered,heads_out,vec_out,tok,full,fsem,dq,dk,dv,normT,wh,gwo,x,gm,isem,hp,hg,vbuf,vrecv,own,obuf,orecv,tbuf,trecv,vrow,osem,tsem,*rest):
+      compiler_params=pltpu.CompilerParams(vmem_limit_bytes=63*2**20+2**19,collective_id=0,has_side_effects=True),name="feed_forward")(att,wo,x,vb,vg,vs,vd,cot,wu,wd,bu)
+
+def finish_kernel(dp,red,dq_h,dk_h,dv_h,normT_h,wh_h,gwo_h,x_h,gm_h,gain,vec,gbu,gathered,heads_out,vec_out,tok,full,fsem,dq,dk,dv,normT,wh,gwo,x,gm,isem,hp,hg,vbuf,vrecv,own,obuf,orecv,tbuf,trecv,vrow,osem,tsem,*rest):
     CH=full.shape[0]; R=full.shape[2]; T,D=x.shape; C=dq.shape[1]; Q=T//2
     plan=big_plan(dp,R); n=len(plan[0][0]); K=len(plan)
     HR=hp.shape[2]; hplan=head_plan(dp,HR); HK=len(hplan); HC=hp.shape[0]
@@ -445,7 +466,7 @@
             r=rows_at(quarter*Q+t*128,128)
             e=own[r,:]+orecv[r,:].astype(F32)
             nn,rs=norm_parts(x[r,:].astype(F32))
-            tbuf[r,:]=(gm[r,:]+norm_back(e,nn,rs,vin[4:5,:])).astype(BF)
+            tbuf[r,:]=(gm[r,:]+norm_back(e,nn,rs,gain[...].reshape(1,D))).astype(BF)
             vrow[0:1,:]+=colsum(e*nn); vrow[1:2,:]+=colsum(e)
     def vectors(_):
         tok[p.tw]=tbuf[rows_at(p.tw*Q,Q),:]
@@ -492,7 +513,7 @@
     ocopy().wait_send(); tcopy().wait()
     tok[1-p.tw]=trecv[...]
 
-def finish(dp,red,dq,dk,dv,normT,wh,gwo,x,gm,vin,vec,gbu):
+def finish(dp,red,dq,dk,dv,normT,wh,gwo,x,gm,gain,vec,gbu):
     T,D=x.shape; CH,fin,_=red.shape; R=FC//128*D
     plan=big_plan(dp,R); n=len(plan[0][0])
     HC=D//TT; HR=2*dq.shape[1]//128*TT; hplan=head_plan(dp,HR)
@@ -503,7 +524,7 @@
             if axis=="tw": q=1
             else: rows//=2
             hrecv.append(pltpu.VMEM((HC,q,rows,128),BF))
-    V=(6*D+gbu.shape[1])//128+16; nv=n+1; args=(red,dq,dk,dv,normT,wh,gwo,x,gm,vin,vec,gbu)
+    V=(6*D+gbu.shape[1])//128+16; nv=n+1; args=(red,dq,dk,dv,normT,wh,gwo,x,gm,gain,vec,gbu)
     return pl.pallas_call(functools.partial(finish_kernel,dp),
       in_specs=[pl.BlockSpec(memory_space=pl.ANY if 1<=i<=8 else pltpu.VMEM) for i in range(len(args))],
       out_specs=[pl.BlockSpec(memory_space=pl.ANY)]+[pl.BlockSpec(memory_space=pltpu.VMEM)]*3,
@@ -541,28 +562,33 @@
       compiler_params=pltpu.CompilerParams(vmem_limit_bytes=50*2**20),name="widen")(tw.reshape(1),chunks,heads,mine,got,vec)
     return res[:5],res[5:]
 
-def front_kernel(tok,w,b,vin,seg,x_o,normT_o,q_o,k_o,v_o,wh_o,mq_o,mk_o,x,norm,normT,qkv,wh,wgot,bgot,mq,mk,tsem,bsem,csem,ysem,xsem,osem):
-    p=Peers(); Q,D=tok.shape[1:]; T=2*Q; L=2*T; E=w.shape[1]; HALF=E//2
-    barrier(p,["th","tw",0])
+def front_kernel(tok,w,b,gain,shift,seg,x_o,normT_o,q_o,k_o,v_o,wh_o,mq_o,mk_o,x,norm,normT,qkv,wh,wgot,bgot,bias,mq,mk,tsem,bsem,csem,ysem,xsem,zsem,osem):
+    p=Peers(); Q,D=tok.shape[1:]; T=2*Q; L=2*T; E=w.shape[1]; PART=E//4
+    b0,b1=p.bit(0),p.bit(1)
+    barrier(p,["th","tw",0,1])
     def tcopy(): return send(tok.at[1-p.tw],x.at[rows_at(p.tw*Q,Q),:],tsem.at[0],tsem.at[1],p.peer("tw"))
     def bcopy(): return send(b,bgot,bsem.at[0],bsem.at[1],p.peer("tw"))
     def ycopy(c):
-        r=rows_at(p.bit(0)*HALF,HALF)
+        r=rows_at((2*b1+b0)*PART,PART)
         return send(w.at[c,r,:],wgot.at[c,r,:],ysem.at[0,c],ysem.at[1,c],p.peer("tw"))
     def xcopy(c,landed):
-        ref=wgot.at[c,rows_at((1-p.bit(0) if landed else p.bit(0))*HALF,HALF),:]
+        ref=wgot.at[c,rows_at((2*b1+(1-b0 if landed else b0))*PART,PART),:]
         return send(ref,ref,xsem.at[0,c],xsem.at[1,c],p.peer(0))
+    def zcopy(c,landed):
+        ref=wgot.at[c,rows_at((1-b1 if landed else b1)*2*PART,2*PART),:]
+        return send(ref,ref,zsem.at[0,c],zsem.at[1,c],p.peer(1))
     def ccopy(i,landed):
         core=1-p.th if landed else p.th
         quarter=p.tw if i==0 else 1-p.tw
         ref=norm.at[rows_at(core*T+quarter*Q,Q),:]
         return send(ref,ref,csem.at[0,i],csem.at[1,i],p.peer("th"))
-    tcopy().start(); bcopy().start()
     for c in range(3): ycopy(c).start()
+    bcopy().start()
+    tcopy().start()
+    g_row=gain[...].reshape(1,D); s_row=shift[...].reshape(1,D)
     def normalize(src,row):
         for t in range(Q//128):
-            v=src(t)
-            y=(norm_parts(v.astype(F32))[0]*vin[4:5,:]+vin[5:6,:]).astype(BF)
+            y=(norm_parts(src(t).astype(F32))[0]*g_row+s_row).astype(BF)
             norm[rows_at(row+t*128,128),:]=y
     def put(src,dst,i): return pltpu.make_async_copy(src,dst,osem.at[i])
     x[rows_at(p.tw*Q,Q),:]=tok[p.tw]
@@ -571,52 +597,66 @@
     same=onehot==seg[...]
     mk[...]=jnp.where(same,1.0,0.0).T.astype(BF)
     ccopy(0,False).start()
-    mq[...]=jnp.where(same|(onehot>=8),0.0,-float(2**40)).T.astype(BF)
+    for c in range(3):
+        ycopy(c).wait_recv()
+        xcopy(c,False).start()
+    mq[...]=jnp.where(same|(onehot>=9),0.0,-float(2**40)).T.astype(BF)
     put(mk,mk_o,0).start(); put(mq,mq_o,1).start()
+    bcopy().wait_recv()
+    bias[...]=jnp.zeros_like(bias)
+    for m,src in enumerate((b,bgot)):
+        for i,c in enumerate((0,2)): bias[m,c:c+1,:]=src[i:i+1,:]
+    for c in range(3):
+        xcopy(c,True).wait_recv()
+        zcopy(c,False).start()
+    def project(row,weights,m):
+        r=rows_at(row,Q)
+        def one(c,_):
+            y=(dot(norm[r,:],weights[c],NT)+bias[m,pl.ds(c,1),:]).astype(BF)
+            y=y*jnp.where(c==0,0.125,1.0).astype(BF)
+            qkv[c,r,m*E:(m+1)*E]=y
+            return 0
+        lax.fori_loop(0,3,one,0)
+    def transpose(quarter):
+        for core in range(2):
+            for t in range(Q//128):
+                at=core*T+quarter*Q+t*128
+                normT[:,pl.ds(pl.multiple_of(at,128),128)]=norm[rows_at(at,128),:].T
+    ccopy(0,True).wait_recv()
+    for core in range(2): project(core*T+p.tw*Q,w,0)
+    transpose(p.tw)
+    for c in range(3): zcopy(c,True).wait_recv()
+    for core in range(2): project(core*T+p.tw*Q,wgot,1)
+    for c in range(3): wh[c,0:E,:]=w[c]; wh[c,E:2*E,:]=wgot[c]
+    put(wh,wh_o,7).start()
     tcopy().wait_recv()
     normalize(lambda t: x[rows_at((1-p.tw)*Q+t*128,128),:],p.th*T+(1-p.tw)*Q)
     put(x,x_o,2).start()
-    bcopy().wait_recv()
-    tiles=[slice(t*TT,(t+1)*TT) for t in range(L//TT)]
-    def bias(c,ref): return ref[c//2:c//2+1,:] if c!=1 else None
-    def project(c,wt,bs,r):
-        y=dot(norm[r,:],wt,NT)
-        if bs is not None: y=y+bs
-        y=y.astype(BF)
-        return y*BF(0.125) if c==0 else y
-    ccopy(1,False).start()
-    ccopy(0,True).wait_recv()
+    for m,weights in enumerate((w,wgot)):
+        project(p.th*T+(1-p.tw)*Q,weights,m)
+        if m==0: ccopy(1,False).start()
     ccopy(1,True).wait_recv()
-    for c in range(3):
-        for r in tiles: qkv[c,r,0:E]=project(c,w[c],bias(c,b),r)
-    for r in tiles: normT[:,r]=norm[r,:].T
+    for m,weights in enumerate((w,wgot)): project((1-p.th)*T+(1-p.tw)*Q,weights,m)
+    for c in range(3): put(qkv.at[c],(q_o,k_o,v_o)[c],4+c).start()
+    transpose(1-p.tw)
     put(normT,normT_o,3).start()
-    for c in range(3):
-        ycopy(c).wait_recv()
-        xcopy(c,False).start()
-    for c in range(3):
-        xcopy(c,True).wait_recv()
-        for r in tiles: qkv[c,r,E:2*E]=project(c,wgot[c],bias(c,bgot),r)
-        put(qkv.at[c],(q_o,k_o,v_o)[c],4+c).start()
-        wh[c,0:E,:]=w[c]; wh[c,E:2*E,:]=wgot[c]
-    put(wh,wh_o,7).start()
     for src,dst,i in ((mk,mk_o,0),(mq,mq_o,1),(x,x_o,2),(normT,normT_o,3),(wh,wh_o,7)): put(src,dst,i).wait()
     for c in range(3):
         put(qkv.at[c],(q_o,k_o,v_o)[c],4+c).wait()
-        ycopy(c).wait_send(); xcopy(c,False).wait_send()
+        ycopy(c).wait_send(); xcopy(c,False).wait_send(); zcopy(c,False).wait_send()
     tcopy().wait_send(); bcopy().wait_send()
     for i in range(2): ccopy(i,False).wait_send()
 
-def front(tok,w,b,vin,seg):
+def front(tok,w,b,gain,shift,seg):
     _,Q,D=tok.shape; T=2*Q; L=2*T; E=w.shape[1]
     outs=[((T,D),BF),((D,L),BF)]+[((L,2*E),BF)]*3+[((3,2*E,D),BF)]+[((L,128),BF)]*2
     sem=pltpu.SemaphoreType.DMA
     return pl.pallas_call(front_kernel,
-      in_specs=[pl.BlockSpec(memory_space=pltpu.VMEM)]*5,out_specs=[pl.BlockSpec(memory_space=pl.ANY)]*len(outs),
+      in_specs=[pl.BlockSpec(memory_space=pltpu.VMEM)]*6,out_specs=[pl.BlockSpec(memory_space=pl.ANY)]*len(outs),
       out_shape=[jax.ShapeDtypeStruct(*o) for o in outs],
       scratch_shapes=[pltpu.VMEM((T,D),BF),pltpu.VMEM((L,D),BF),pltpu.VMEM((D,L),BF),pltpu.VMEM((3,L,2*E),BF),pltpu.VMEM((3,2*E,D),BF),pltpu.VMEM((3,E,D),BF),
-        pltpu.VMEM(b.shape,F32),pltpu.VMEM((L,128),BF),pltpu.VMEM((L,128),BF),sem((2,)),sem((2,)),sem((2,2)),sem((2,3)),sem((2,3)),sem((8,))],
-      compiler_params=pltpu.CompilerParams(vmem_limit_bytes=60*2**20,collective_id=2,has_side_effects=True),name="front")(tok,w,b,vin,seg)
+        pltpu.VMEM(b.shape,F32),pltpu.VMEM((2,8,E),F32),pltpu.VMEM((L,128),BF),pltpu.VMEM((L,128),BF),sem((2,)),sem((2,)),sem((2,2)),sem((2,3)),sem((2,3)),sem((2,3)),sem((8,))],
+      compiler_params=pltpu.CompilerParams(vmem_limit_bytes=60*2**20,collective_id=2,has_side_effects=True),name="front")(tok,w,b,gain,shift,seg)
 
 
 SWAP = [(0, 1), (1, 0)]
@@ -659,10 +699,9 @@
     th, tw = lax.axis_index("th"), lax.axis_index("tw")
     d = tokens.shape[-1]
     mine = w_qkv.shape[2]
-    vectors = jnp.stack([b_out, norm2_gain, norm2_shift, b_down, norm1_gain, norm1_shift, b_down, b_down])
     seg = lax.dynamic_index_in_dim(segment_ids, tw, 0)
     x, normed_t, query, key, value, w_heads, mq, mk = front(
-        tokens, w_qkv.transpose(0, 2, 1), b_qv, vectors, seg
+        tokens, w_qkv.transpose(0, 2, 1), b_qv, norm1_gain, norm1_shift, seg
     )
     tables = (mq, mk, *block_ranges(seg[0]))
     later = lax.optimization_barrier((cotangent, w_out, query))
@@ -670,12 +709,12 @@
     w_out_heads = jnp.concatenate([w_out, swap(later[1], "tw")], 0)
     attended, totals = attn_fwd(query, key, value, *tables)
     out_mine, out_other, grad_middle, grad_b_up, sums, red, grad_heads, grad_w_out = ffn(
-        dp_size, attended, w_out_heads, x, vectors, cot, w_up, w_down, b_up[None]
+        dp_size, attended, w_out_heads, x, b_out, norm2_gain, norm2_shift, b_down, cot, w_up, w_down, b_up[None]
     )
     out_got = swap(out_other, "tw")
     dq, dk, dv = attn_bwd(query, key, value, grad_heads, attended, totals, *tables)
     chunks, heads, small, grad_tokens = finish(
-        dp_size, red, dq, dk, dv, normed_t, w_heads, grad_w_out, x, grad_middle, vectors, sums, grad_b_up
+        dp_size, red, dq, dk, dv, normed_t, w_heads, grad_w_out, x, grad_middle, norm1_gain, sums, grad_b_up
     )
     (up, down, w_qkv_grad, w_out_grad, block_out), vecs = widen(tw, chunks, heads, out_mine, out_got, small)
     b_qv_grad = lax.dynamic_slice_in_dim(small[-16:].reshape(4, 2, 256), 2 * th + tw, 1, 0)[0, :, :mine]

time: 272 us -> 249 us (0.915)
  Pallas kernels: 253 us -> 232 us
  local copies, waits for them, and re-layouts: 10.8 us -> 6.21 us
  waiting for transfers between devices: 0.01 us -> 3.16 us
    pallas_call x1, Pallas kernels: 26.8 us -> 16.2 us  [attn_fwd(): pl.pallas_call(fwd_kernel, grid_spec=pltpu.PrefetchScalarGridSpec(num_sca...]
    pallas_call x1, Pallas kernels: 34.8 us -> 25.1 us  [attn_bwd(): pl.pallas_call(bwd_kernel, grid_spec=pltpu.PrefetchScalarGridSpec(num_sca...]
    pallas_call x1, Pallas kernels: 37.7 us -> 32.7 us  [front(): pl.pallas_call(front_kernel, in_specs=[pl.BlockSpec(memory_space=pltpu.VM...]
    another operation x7 -> x0, local copies, waits for them, and re-layouts: 4.87 us -> none  [body(): jnp.stack([b_out, norm2_gain, norm2_shift, b_down, norm1_gain, norm1_shif...]
    pallas_call x1, Pallas kernels: 79.3 us -> 83.7 us  [finish(): pl.pallas_call(functools.partial(finish_kernel, dp), in_specs=[pl.BlockSp...]
    ppermute x3, waiting for transfers between devices: 0.01 us -> 3.16 us  [swap(): return lax.ppermute(value, axis, SWAP)]
  transfers between devices with their start and end apart: 3 -> 3, of which waited for: 0 -> 1; matrix products, arithmetic and copies ran while one was open for 1% -> 1% of each run, Pallas kernels for 52% -> 50%
where the time goes in v2:
time: 249 us
  Pallas kernels  232 us (93%)
  local copies, waits for them, and re-layouts  6.21 us (2%)
  starting transfers between devices  3.31 us (1%)
  waiting for transfers between devices  3.16 us (1%)
  other arithmetic  3.08 us (1%)
    pallas_call x1, Pallas kernels, finish(): pl.pallas_call(functools.partial(finish_kernel, dp), in_specs=[pl.BlockSp...  83.7 us
    pallas_call x1, Pallas kernels, ffn(): pl.pallas_call(functools.partial(ffn_kernel, dp), in_specs=[whole(v.shape...  61.2 us
    pallas_call x1, Pallas kernels, front(): pl.pallas_call(front_kernel, in_specs=[pl.BlockSpec(memory_space=pltpu.VM...  32.7 us
    pallas_call x1, Pallas kernels, attn_bwd(): pl.pallas_call(bwd_kernel, grid_spec=pltpu.PrefetchScalarGridSpec(num_sca...  25.1 us
    pallas_call x1, Pallas kernels, attn_fwd(): pl.pallas_call(fwd_kernel, grid_spec=pltpu.PrefetchScalarGridSpec(num_sca...  16.2 us
    pallas_call x1, Pallas kernels, widen(): pl.pallas_call(widen_kernel, grid=(CH,), in_specs=[pl.BlockSpec(memory_sp...  13.2 us
  transfers between devices with their start and end apart: 3, of which 1 were waited for; matrix products, arithmetic and copies ran while one was open for 1% of the time, Pallas kernels for 50%

profile of v2, /device:TPU:0, one launch (start us, length us, event | category | flops | bytes accessed | tf_op | source)
XLA Modules:
  0.0 248.7 jit_solution(17959121231719347021)
XLA Ops:
  0.7 1.4 fusion.2
  2.1 32.7 %front.1 = (bf16[768,768]{1,0:T(8,128)(2,1)}, bf16[768,1536]{1,0:T(8,128)(2,1)}, bf16[1536,384]{1,0:T(8,128)(2,1)}, bf16[1536,384]{1,0:T(8,128)(2,1)}, bf16[1536...) custom-call(bf16[2,384,768]{2,1,0:T(8,128)(2,1)} %tok.1, ...), custom_call_target="tpu_custom_call" | custom-call | tf_op jit(solution)/shard_map/front/pallas_call | solution.py:654
  34.8 0.1 dynamic-slice_bitcast_fusion.1
  34.9 0.7 collective-permute-start.1
  35.6 0.1 copy-done.5
  35.8 1.2 collective-permute-start
  37.0 0.1 slice.12
  37.1 0.1 slice.13
  37.2 0.2 convert_reduce_fusion
  37.4 0.5 and_select_fusion
  38.0 16.2 %attention_forward.1 = (bf16[1536,384]{1,0:T(8,128)(2,1)}, f32[8,1536]{1,0:T(8,128)}) custom-call(s32[6]{0:T(128)} %get-tuple-element.95.lo_ref, s32[6]{0:T(128)} %get-tuple-element.94.n_ref, bf16[1536,384]{1,0:T(8,128)(2,1)} %get-tuple-element.53.q_ref, bf16[1536,384]{1,0:T(8,128)(2,1)} %get-tuple-element.54.k_ref, ...), custom_call_target="tpu_custom_call" | custom-call | tf_op jit(solution)/shard_map/attention_forward/pallas_call | solution.py:76
  54.2 3.2 %collective-permute-done = bf16[192,768]{1,0:T(8,128)(2,1)S(1)} collective-permute-done((bf16[192,768]{1,0:T(8,128)(2,1)S(1)}, bf16[192,768]{1,0:T(8,128)(2,1)S(1)}, u32[]{:S(2)}, u32[]{:S(2)}) %collective-permute-start) | collective-permute-done | bytes 294944 | tf_op jit(solution)/shard_map/ppermute | solution.py:666
  57.3 0.9 pad_maximum_fusion.wo
  58.2 1.5 maximum_select_fusion.cot
  59.7 61.2 %feed_forward.1 = (bf16[384,768]{1,0:T(8,128)(2,1)}, bf16[384,768]{1,0:T(8,128)(2,1)}, f32[768,768]{1,0:T(8,128)}, f32[1,3072]{1,0:T(1,128)}, f32[8,768]{1,0:T(8...) custom-call(bf16[1536,384]{1,0:T(8,128)(2,1)} %get-tuple-element.58.att.o_ref, ...), custom_call_target="tpu_custom_call" | custom-call | tf_op jit(solution)/shard_map/feed_forward/pallas_call | solution.py:372
  120.9 1.4 collective-permute-start.2
  122.3 25.1 %attention_backward.1 = (bf16[1536,384]{1,0:T(8,128)(2,1)}, bf16[1536,384]{1,0:T(8,128)(2,1)}, bf16[1536,384]{1,0:T(8,128)(2,1)}) custom-call(s32[6]{0:T(128)} %get-tuple-element.95.lo_ref, s32[6]{0:T(128)} %get-tuple-element.94.n_ref, bf16[1536,384]{1,0:T(8,128)(2,1)} %get-tuple-element.53.q_ref, bf16[1536,384]{1,0:T(8,128)(2,1)} %get-tuple-element.54.k_ref, ...), custom_call_target="tpu_custom_call" | custom-call | tf_op jit(solution)/shard_map/attention_backward/pallas_call | solution.py:134
  147.3 83.7 %finish_gradients.1 = (bf16[6,2,3072,128]{3,2,1,0:T(8,128)(2,1)}, bf16[3,1536,128]{2,1,0:T(8,128)(2,1)}, f32[76,128]{1,0:T(8,128)}, bf16[2,384,768]{2,1,0:T(8,128)(2,1)}) custom-call(bf16[6,192,128]{2,1,0:T(8,128)(2,1)} %get-tuple-element.62.red, bf16[1536,384]{1,0:T(8,128)(2,1)} %get-tuple-element.65.dq_h, bf16[1536,384]{1,0:T(8,128)(2,1)} %get-tuple-element.66.dk_h, ...), custom_call_target="tpu_custom_call" | custom-call | tf_op jit(solution)/shard_map/finish_gradients/pallas_call | solution.py:528
  231.1 0.7 slice.14
  231.8 0.6 dynamic-slice_bitcast_fusion.2
  232.4 1.3 copy-done
  233.7 0.8 copy-done.2
  234.4 13.2 %widen.1 = (f32[768,3072]{1,0:T(8,128)}, f32[3072,768]{1,0:T(8,128)}, f32[3,192,768]{2,1,0:T(8,128)}, f32[192,768]{1,0:T(8,128)}, bf16[2,384,768]{2,1,0:T(8,128)...) custom-call(s32[1]{0:T(128)} %bitcast.where, ...), custom_call_target="tpu_custom_call" | custom-call | tf_op jit(solution)/shard_map/widen/pallas_call | solution.py:558
  247.6 1.0 copy.30
  (12 shorter events, 0.0 us)
Async XLA Ops:
  0.6 34.2 %copy-start.3 = (bf16[2,384,768]{2,1,0:T(8,128)(2,1)S(1)}, bf16[2,384,768]{2,1,0:T(8,128)(2,1)}, u32[]{:S(2)}) copy-start(bf16[2,384,768]{2,1,0:T(8,128)(2,1)} %param.29) | copy-start | bytes 3538948
  34.8 1.0 copy-start.5
  34.9 23.3 %collective-permute-start.1 = (bf16[384,768]{1,0:T(8,128)(2,1)S(1)}, bf16[384,768]{1,0:T(8,128)(2,1)S(1)}, u32[]{:S(2)}, u32[]{:S(2)}) collective-permute-start(bf16[384,768]{1,0:T(8,128)(2,1)S(1)} %get-tuple-element.99), channel_id=1, source_target_pairs={{0,1},{1,0},{2,3},{3,2},{4,5},{5,4},{6,7},{7,6},{8,9},{9,8},{10,11... | collective-permute-start | bytes 1769480 | tf_op jit(solution)/shard_map/ppermute | solution.py:666
  35.8 21.5 %collective-permute-start = (bf16[192,768]{1,0:T(8,128)(2,1)S(1)}, bf16[192,768]{1,0:T(8,128)(2,1)S(1)}, u32[]{:S(2)}, u32[]{:S(2)}) collective-permute-start(bf16[192,768]{1,0:T(8,128)(2,1)S(1)} %copy-done.5), channel_id=1, source_target_pairs={{0,1},{1,0},{2,3},{3,2},{4,5},{5,4},{6,7},{7,6},{8,9},{9,8},{10,11... | collective-permute-start | bytes 884744 | tf_op jit(solution)/shard_map/ppermute | solution.py:666
  120.9 111.5 %collective-permute-start.2 = (bf16[384,768]{1,0:T(8,128)(2,1)}, bf16[384,768]{1,0:T(8,128)(2,1)S(1)}, u32[]{:S(2)}, u32[]{:S(2)}) collective-permute-start(bf16[384,768]{1,0:T(8,128)(2,1)} %get-tuple-element.77), channel_id=1, source_target_pairs={{0,1},{1,0},{2,3},{3,2},{4,5},{5,4},{6,7},{7,6},{8,9},{9,8},{10,11... | collective-permute-start | bytes 1769480 | tf_op jit(solution)/shard_map/ppermute | solution.py:666
  147.3 85.1 %copy-start.1 = (bf16[384,768]{1,0:T(8,128)(2,1)S(1)}, bf16[384,768]{1,0:T(8,128)(2,1)}, u32[]{:S(2)}) copy-start(bf16[384,768]{1,0:T(8,128)(2,1)} %get-tuple-element.76.mine) | copy-start | bytes 1769476
  232.4 1.3 copy-start
  233.7 0.8 copy-start.2
  234.4 13.2 %copy-start.4 = (bf16[2,384,768]{2,1,0:T(8,128)(2,1)S(1)}, bf16[2,384,768]{2,1,0:T(8,128)(2,1)}, u32[]{:S(2)}) copy-start(bf16[2,384,768]{2,1,0:T(8,128)(2,1)} %get-tuple-element.115) | copy-start | bytes 3538948

commit v3 on v2

--- a/solution.py
+++ b/solution.py
@@ -12,16 +12,16 @@
 BQ=256; BK=256; HD=64
 def dot(a,b,d): return lax.dot_general(a,b,d,preferred_element_type=F32)
 
-AL=128; VR=80
+AL=128; VR=80; GRP=3
 def key_rows(lo_ref,mk_ref,i,j):
     L=mk_ref.shape[0]
     want=lo_ref[i]+j*BK
     start=pl.multiple_of(jnp.minimum(want,L-BK),AL)
     row=lax.broadcasted_iota(jnp.int32,(BK,128),0); lane=lax.broadcasted_iota(jnp.int32,(BK,128),1)
     ks=pl.ds(start,BK)
-    return ks,jnp.where((lane==8)&(row<want-start),jnp.ones((BK,128),BF),mk_ref[ks,:])
-
-def fwd_kernel(lo_ref, n_ref, q_ref, k_ref, v_ref, mq_ref, mk_ref, o_ref, lse_ref, m_ref, acc_ref, vT_ref, *score_refs):
+    return ks,jnp.where(((lane==8)|(lane==HD+8))&(row<want-start),jnp.ones((BK,128),BF),mk_ref[ks,:])
+
+def fwd_kernel(lo_ref, n_ref, q_ref, k_ref, v_ref, mq_ref, mk_ref, o_ref, lse_ref, m_ref, acc_ref, vT_ref, qm_ref, *score_refs):
     i=pl.program_id(0); H=q_ref.shape[1]//HD
     lane=lax.broadcasted_iota(jnp.int32,(1,128),1)
     halves=(lane<HD, lane>=HD)
@@ -35,10 +35,10 @@
                 vT_ref[2*p+e,HD:VR,:]=jnp.where(row==0,1.0,0.0).astype(BF)
     m_ref[...]=jnp.full(m_ref.shape,-1e30,F32)
     acc_ref[...]=jnp.zeros_like(acc_ref)
+    for h in range(H): qm_ref[h]=jnp.where(halves[h%2],q_ref[:,h//2*128:h//2*128+128],mq_ref[...])
     def score(h,ks,mk):
         cols=slice(h//2*128,h//2*128+128)
-        k2=k_ref[ks,cols]
-        return dot(jnp.concatenate([jnp.where(halves[h%2],k2,jnp.zeros_like(k2)),mk],1),jnp.concatenate([q_ref[:,cols],mq_ref[...]],1),NT)
+        return dot(jnp.where(halves[h%2],k_ref[ks,cols],mk),qm_ref[h],NT)
     def soft(h,s):
         m_old=m_ref[h:h+1,:]
         m_new=jnp.maximum(m_old,jnp.max(s,axis=0,keepdims=True))
@@ -78,12 +78,12 @@
           in_specs=[pl.BlockSpec((BQ,C),lambda i,*_:(i,0)),pl.BlockSpec((L,C),lambda i,*_:(0,0)),pl.BlockSpec((L,C),lambda i,*_:(0,0)),
                     pl.BlockSpec((BQ,128),lambda i,*_:(i,0)),pl.BlockSpec((L,128),lambda i,*_:(0,0))],
           out_specs=[pl.BlockSpec((BQ,C),lambda i,*_:(i,0)),pl.BlockSpec((8,BQ),lambda i,*_:(0,i))],
-          scratch_shapes=[pltpu.VMEM((8,BQ),F32),pltpu.VMEM((C//HD,VR,BQ),F32),pltpu.VMEM((C//HD,VR,L),BF),pltpu.VMEM((C//HD,BK,BQ),F32),pltpu.VMEM((C//HD,BK,BQ),F32)]),
+          scratch_shapes=[pltpu.VMEM((8,BQ),F32),pltpu.VMEM((C//HD,VR,BQ),F32),pltpu.VMEM((C//HD,VR,L),BF),pltpu.VMEM((C//HD,BQ,128),BF),pltpu.VMEM((C//HD,BK,BQ),F32),pltpu.VMEM((C//HD,BK,BQ),F32)]),
         out_shape=[jax.ShapeDtypeStruct((L,C),BF),jax.ShapeDtypeStruct((8,L),F32)],
         name="attention_forward",
     )(lo,n,q,k,v,mq,mk)
 
-def bwd_kernel(lo_ref, n_ref, q_ref, k_ref, v_ref, do_ref, o_ref, lse_ref, mq_ref, mk_ref, dq_ref, dk_ref, dv_ref, dk_acc, dv_acc, dq_acc, qcat, docat):
+def bwd_kernel(lo_ref, n_ref, q_ref, k_ref, v_ref, do_ref, o_ref, lse_ref, mq_ref, mk_ref, dq_ref, dk_ref, dv_ref, dk_acc, dv_acc, dq_acc, qcat, docat, qm, kT):
     i=pl.program_id(0); n=pl.num_programs(0)
     C=q_ref.shape[1]; pairs=C//128
     lane=lax.broadcasted_iota(jnp.int32,(1,128),1)
@@ -91,6 +91,7 @@
     @pl.when(i==0)
     def _():
         dk_acc[...]=jnp.zeros_like(dk_acc); dv_acc[...]=jnp.zeros_like(dv_acc)
+        kT[...]=k_ref[...].T
     dq_acc[...]=jnp.zeros_like(dq_acc)
     sel=(lax.broadcasted_iota(jnp.int32,(8,C),1)//HD==lax.broadcasted_iota(jnp.int32,(8,C),0)).astype(BF)
     prod=do_ref[...].astype(F32)*o_ref[...].astype(F32)
@@ -101,26 +102,32 @@
         for e in range(2):
             q2=q_ref[:,cols]; d2=do_ref[:,cols]
             qcat[p,e*BQ:(e+1)*BQ,:]=jnp.where(halves[e],q2,jnp.zeros_like(q2))
+            qm[p,e*BQ:(e+1)*BQ,:]=jnp.where(halves[e],q2,mq_ref[...])
             docat[p,e*BQ:(e+1)*BQ,:]=jnp.where(halves[e],d2,jnp.zeros_like(d2))
     lse=lse_ref[...]
     def body(j,_):
         ks,mk=key_rows(lo_ref,mk_ref,i,j)
-        for p in range(pairs):
-            cols=slice(p*128,(p+1)*128)
-            qx=jnp.concatenate([q_ref[:,cols],mq_ref[...]],1)
-            k2=k_ref[ks,cols]; v2=v_ref[ks,cols]; d2=do_ref[:,cols]
-            ps=[]; dss=[]; kms=[]
-            for e in range(2):
-                h=2*p+e
-                km=jnp.where(halves[e],k2,jnp.zeros_like(k2)); vm=jnp.where(halves[e],v2,jnp.zeros_like(v2))
-                s=dot(jnp.concatenate([km,mk],1),qx,NT)
+        for g in range(0,pairs,GRP):
+            work=[]
+            for p in range(g,g+GRP):
+                cols=slice(p*128,(p+1)*128)
+                k2=k_ref[ks,cols]; v2=v_ref[ks,cols]; d2=do_ref[:,cols]
+                for e in range(2):
+                    s=dot(jnp.where(halves[e],k2,mk),qm[p,e*BQ:(e+1)*BQ,:],NT)
+                    work.append((s,dot(jnp.where(halves[e],v2,jnp.zeros_like(v2)),d2,NT)))
+            out=[]
+            for t,(s,dp) in enumerate(work):
+                h=2*g+t
                 pr=jnp.exp(s-lse[h:h+1,:])
-                dp=dot(vm,d2,NT)
-                ds=pr*(dp-delta[h:h+1,:])
-                ps.append(pr.astype(BF)); dss.append(ds.astype(BF)); kms.append(km)
-            dv_acc[ks,cols]+=dot(jnp.concatenate(ps,1),docat[p],NN)
-            dk_acc[ks,cols]+=dot(jnp.concatenate(dss,1),qcat[p],NN)
-            dq_acc[cols,:]+=dot(jnp.concatenate(kms,0),jnp.concatenate(dss,0),TN)
+                out.append((pr.astype(BF),(pr*(dp-delta[h:h+1,:])).astype(BF)))
+            for p in range(g,g+GRP):
+                cols=slice(p*128,(p+1)*128); k2=k_ref[ks,cols]
+                (p0,d0),(p1,d1)=out[2*(p-g):2*(p-g)+2]
+                dv_acc[ks,cols]+=dot(jnp.concatenate([p0,p1],1),docat[p],NN)
+                dk_acc[ks,cols]+=dot(jnp.concatenate([d0,d1],1),qcat[p],NN)
+                for e,d in enumerate((d0,d1)):
+                    r=slice((2*p+e)*HD,(2*p+e+1)*HD)
+                    dq_acc[r,:]+=dot(kT[r,ks],d,NN)
         return 0
     lax.fori_loop(0,n_ref[i],body,0)
     dq_ref[...]=(dq_acc[...]*0.125).T.astype(BF)
@@ -135,7 +142,7 @@
         grid_spec=pltpu.PrefetchScalarGridSpec(num_scalar_prefetch=2,grid=(L//BQ,),
           in_specs=[blk,full,full,blk,blk,pl.BlockSpec((8,BQ),lambda i,*_:(0,i)),pl.BlockSpec((BQ,128),lambda i,*_:(i,0)),pl.BlockSpec((L,128),lambda i,*_:(0,0))],
           out_specs=[blk,full,full],
-          scratch_shapes=[pltpu.VMEM((L,C),F32),pltpu.VMEM((L,C),F32),pltpu.VMEM((C,BQ),F32),pltpu.VMEM((C//128,2*BQ,128),BF),pltpu.VMEM((C//128,2*BQ,128),BF)]),
+          scratch_shapes=[pltpu.VMEM((L,C),F32),pltpu.VMEM((L,C),F32),pltpu.VMEM((C,BQ),F32),pltpu.VMEM((C//128,2*BQ,128),BF),pltpu.VMEM((C//128,2*BQ,128),BF),pltpu.VMEM((C//128,2*BQ,128),BF),pltpu.VMEM((C,L),BF)]),
         out_shape=[jax.ShapeDtypeStruct((L,C),BF)]*3,
         name="attention_backward",
     )(lo,n,q,k,v,do,o,lse,mq,mk)
@@ -231,8 +238,8 @@
     return r*(t-jnp.mean(t,axis=-1,keepdims=True)-n*jnp.mean(t*n,axis=-1,keepdims=True))
 def colsum(x): return jnp.sum(x,axis=0,keepdims=True)
 
-def ffn_kernel(dp,att,wo,x,vb,vg,vs,vd,cot,wu_h,wd_h,bu,mine,other,gm,gb,vec,red,gheads,gwo,
-               wu,wd,cotT,mid,n2,n2T,obuf,orecv,grow,act,gh,dw,chip_recv,wsem,osem,gsem,*rest):
+def ffn_kernel(dp,att,x,vb,vg,vs,vd,wo_h,wo_got,cot_h,cot_got,wu_h,wd_h,bu,mine,other,gm,gb,vec,red,gheads,gwo,
+               wo,cot,lsem,wu,wd,cotT,mid,n2,n2T,obuf,orecv,grow,act,gh,dw,chip_recv,wsem,osem,gsem,*rest):
     CH=dw.shape[0]; T,D=x.shape; SLOTS=chip_recv.shape[0]
     plan=big_plan(dp,dw.shape[2]); n=len(plan[0][0]); K=len(plan)
     recv=[rest[k*n:(k+1)*n] for k in range(K)]
@@ -253,13 +260,19 @@
     def wload(c):
         return (pltpu.make_async_copy(wu_h.at[:,pl.ds(pl.multiple_of(c*FC,FC),FC)],wu.at[c],wsem.at[0,c]),
                 pltpu.make_async_copy(wd_h.at[pl.ds(pl.multiple_of(c*FC,FC),FC),:],wd.at[c],wsem.at[1,c]))
+    E=wo_h.shape[0]; Q=T//2
+    loads=[pltpu.make_async_copy(a,b,lsem.at[i]) for i,(a,b) in enumerate(((wo_h,wo.at[0:E,:]),(wo_got,wo.at[E:2*E,:]),
+        (cot_h.at[p.tw],cot.at[rows_at(p.tw*Q,Q),:]),(cot_got,cot.at[rows_at((1-p.tw)*Q,Q),:])))]
+    for l in loads: l.start()
     def load(c,_):
         for w in wload(c): w.start()
         return 0
     lax.fori_loop(0,CH,load,0)
     barrier(p,["th"]+plan[0][0])
+    for l in loads[:2]: l.wait()
     for r in tiles:
         obuf[r,:]=dot(att[rows_at((1-p.th)*T+r.start,TT),:],wo[...],NN).astype(BF)
+    for l in loads[2:]: l.wait()
     for t,r in enumerate(tiles):
         mid[r,:]=x[r,:].astype(F32)+dot(att[rows_at(p.th*T+r.start,TT),:],wo[...],NN)+b_row
         if t==0: ocopy().start()
@@ -360,7 +373,7 @@
 def whole(shape):
     return pl.BlockSpec(memory_space=pltpu.VMEM)
 
-def ffn(dp,att,wo,x,vb,vg,vs,vd,cot,wu,wd,bu):
+def ffn(dp,att,x,vb,vg,vs,vd,wo,wo_got,cot,cot_got,wu,wd,bu):
     T,D=x.shape; FF=wu.shape[1]; CH=FF//FC; R=FC//128*D; C=att.shape[1]
     plan=big_plan(dp,R); n=len(plan[0][0])
     fin=R>>n
@@ -370,12 +383,12 @@
     hbm=pl.BlockSpec(memory_space=pl.ANY)
     V=pltpu.VMEM; sem=pltpu.SemaphoreType.DMA
     return pl.pallas_call(functools.partial(ffn_kernel,dp),
-      in_specs=[whole(v.shape) for v in (att,wo,x,vb,vg,vs,vd,cot)]+[hbm,hbm,whole(bu.shape)],
+      in_specs=[whole(v.shape) for v in (att,x,vb,vg,vs,vd)]+[hbm]*6+[whole(bu.shape)],
       out_specs=specs,out_shape=[jax.ShapeDtypeStruct(*o) for o in outs],
-      scratch_shapes=[V((CH,D,FC),BF),V((CH,FC,D),BF),V((D,T),BF),V((T,D),F32),V((T,D),BF),V((D,T),BF),V((T,D),BF),V((T,D),BF),V((2*T,D),BF),
+      scratch_shapes=[V((C,D),BF),V((T,D),BF),sem((4,)),V((CH,D,FC),BF),V((CH,FC,D),BF),V((D,T),BF),V((T,D),F32),V((T,D),BF),V((D,T),BF),V((T,D),BF),V((T,D),BF),V((2*T,D),BF),
           V((CH,T,FC),BF),V((CH,T,FC),BF),V((CH,2,R,128),BF),V((3,R,128),BF),sem((2,CH)),sem((2,)),sem((2,))]+recv
         +[sem((len(plan),n,CH))]*2+[sem((CH,))]*2,
-      compiler_params=pltpu.CompilerParams(vmem_limit_bytes=63*2**20+2**19,collective_id=0,has_side_effects=True),name="feed_forward")(att,wo,x,vb,vg,vs,vd,cot,wu,wd,bu)
+      compiler_params=pltpu.CompilerParams(vmem_limit_bytes=63*2**20+2**19,collective_id=0,has_side_effects=True),name="feed_forward")(att,x,vb,vg,vs,vd,wo,wo_got,cot,cot_got,wu,wd,bu)
 
 def finish_kernel(dp,red,dq_h,dk_h,dv_h,normT_h,wh_h,gwo_h,x_h,gm_h,gain,vec,gbu,gathered,heads_out,vec_out,tok,full,fsem,dq,dk,dv,normT,wh,gwo,x,gm,isem,hp,hg,vbuf,vrecv,own,obuf,orecv,tbuf,trecv,vrow,osem,tsem,*rest):
     CH=full.shape[0]; R=full.shape[2]; T,D=x.shape; C=dq.shape[1]; Q=T//2
@@ -533,7 +546,7 @@
         +[pltpu.SemaphoreType.DMA((len(plan),n,CH))]*2+[pltpu.SemaphoreType.DMA((CH,))]*2+[pltpu.SemaphoreType.DMA((len(hplan),n,HC))]*4+[pltpu.SemaphoreType.DMA((nv,))]*2,
       compiler_params=pltpu.CompilerParams(vmem_limit_bytes=60*2**20,collective_id=1,has_side_effects=True),name="finish_gradients")(*args)
 
-def widen_kernel(where,chunk,heads,mine,got,vec,wup,wdown,wqkv,wout,blk,*vectors):
+def widen_kernel(where,chunk,heads,mine,got,vec,tok,wup,wdown,wqkv,wout,blk,tok_o,bqv,*vectors):
     D=wup.shape[0]; q=wout.shape[0]; g=pl.program_id(0); HT=D//heads.shape[0]
     for i in range(FC//128):
         cols=slice(i*128,(i+1)*128)
@@ -547,20 +560,24 @@
             for c in range(3): wqkv[c,:,rr]=y[c*q:(c+1)*q,:]
             wout[:,rr]=y[3*q:,:]
         blk[where[0]]=mine[...]; blk[1-where[0]]=got[...]
+        tok_o[...]=tok[...]
+        at=sum(v.shape[0] for v in vectors)//128
+        for i in range(2):
+            for z,w in ((0,128),(1,q-128)): bqv[i:i+1,z*128:z*128+w]=vec[pl.ds(at+4*where[1]+2*i+z,1),0:w]
         at=0
         for v in vectors:
             for i in range(v.shape[0]//128):
                 v[i*128:(i+1)*128]=vec[at,:]; at+=1
 
-def widen(tw,chunks,heads,mine,got,vec):
+def widen(where,chunks,heads,mine,got,vec,tok):
     CH,_,R,_=chunks.shape; D=R*128//FC; FF=CH*FC; q=heads.shape[0]*heads.shape[1]*128//(4*D); T2=mine.shape[0]
     outs=[(D,FF),(FF,D),(3,q,D),(q,D)]; sizes=[D]*6+[FF]
     res=pl.pallas_call(widen_kernel,grid=(CH,),
-      in_specs=[pl.BlockSpec(memory_space=pltpu.SMEM),pl.BlockSpec((None,2,R,128),lambda g:(g,0,0,0))]+[pl.BlockSpec(memory_space=pltpu.VMEM)]*4,
-      out_specs=[pl.BlockSpec((D,FC),lambda g:(0,g)),pl.BlockSpec((FC,D),lambda g:(g,0))]+[pl.BlockSpec(memory_space=pltpu.VMEM)]*(3+len(sizes)),
-      out_shape=[jax.ShapeDtypeStruct(o,F32) for o in outs]+[jax.ShapeDtypeStruct((2,T2,D),BF)]+[jax.ShapeDtypeStruct((z,),F32) for z in sizes],
-      compiler_params=pltpu.CompilerParams(vmem_limit_bytes=50*2**20),name="widen")(tw.reshape(1),chunks,heads,mine,got,vec)
-    return res[:5],res[5:]
+      in_specs=[pl.BlockSpec(memory_space=pltpu.SMEM),pl.BlockSpec((None,2,R,128),lambda g:(g,0,0,0))]+[pl.BlockSpec(memory_space=pltpu.VMEM)]*5,
+      out_specs=[pl.BlockSpec((D,FC),lambda g:(0,g)),pl.BlockSpec((FC,D),lambda g:(g,0))]+[pl.BlockSpec(memory_space=pltpu.VMEM)]*(5+len(sizes)),
+      out_shape=[jax.ShapeDtypeStruct(o,F32) for o in outs]+[jax.ShapeDtypeStruct((2,T2,D),BF)]*2+[jax.ShapeDtypeStruct((2,q),F32)]+[jax.ShapeDtypeStruct((z,),F32) for z in sizes],
+      compiler_params=pltpu.CompilerParams(vmem_limit_bytes=50*2**20),name="widen")(where,chunks,heads,mine,got,vec,tok)
+    return res[:7],res[7:]
 
 def front_kernel(tok,w,b,gain,shift,seg,x_o,normT_o,q_o,k_o,v_o,wh_o,mq_o,mk_o,x,norm,normT,qkv,wh,wgot,bgot,bias,mq,mk,tsem,bsem,csem,ysem,xsem,zsem,osem):
     p=Peers(); Q,D=tok.shape[1:]; T=2*Q; L=2*T; E=w.shape[1]; PART=E//4
@@ -594,7 +611,8 @@
     x[rows_at(p.tw*Q,Q),:]=tok[p.tw]
     normalize(lambda t: tok[p.tw,t*128:(t+1)*128,:],p.th*T+p.tw*Q)
     onehot=lax.broadcasted_iota(jnp.int32,(128,L),0)
-    same=onehot==seg[...]
+    onehot=jnp.where(onehot<HD,onehot,onehot-HD)
+    same=onehot==seg[pl.ds(p.tw,1),:]
     mk[...]=jnp.where(same,1.0,0.0).T.astype(BF)
     ccopy(0,False).start()
     for c in range(3):
@@ -666,18 +684,6 @@
     return lax.ppermute(value, axis, SWAP)
 
 
-def in_order(mine, other, index, axis):
-    return jnp.where(
-        index == 0, jnp.concatenate([mine, other], axis), jnp.concatenate([other, mine], axis)
-    )
-
-
-def own_row(rows, tw):
-    mine = lax.dynamic_index_in_dim(rows, tw, 0, keepdims=False)
-    other = lax.dynamic_index_in_dim(rows, 1 - tw, 0, keepdims=False)
-    return in_order(mine, swap(other, "tw"), tw, 0)
-
-
 def body(
     dp_size,
     tokens,
@@ -697,27 +703,26 @@
     cotangent,
 ):
     th, tw = lax.axis_index("th"), lax.axis_index("tw")
-    d = tokens.shape[-1]
-    mine = w_qkv.shape[2]
-    seg = lax.dynamic_index_in_dim(segment_ids, tw, 0)
     x, normed_t, query, key, value, w_heads, mq, mk = front(
-        tokens, w_qkv.transpose(0, 2, 1), b_qv, norm1_gain, norm1_shift, seg
+        tokens, w_qkv.transpose(0, 2, 1), b_qv, norm1_gain, norm1_shift, segment_ids
     )
-    tables = (mq, mk, *block_ranges(seg[0]))
+    tables = (mq, mk, *block_ranges(lax.dynamic_index_in_dim(segment_ids, tw, 0, False)))
     later = lax.optimization_barrier((cotangent, w_out, query))
-    cot = own_row(later[0], tw)
-    w_out_heads = jnp.concatenate([w_out, swap(later[1], "tw")], 0)
+    cot_got = swap(lax.dynamic_index_in_dim(later[0], 1 - tw, 0, False), "tw")
+    w_out_got = swap(later[1], "tw")
     attended, totals = attn_fwd(query, key, value, *tables)
     out_mine, out_other, grad_middle, grad_b_up, sums, red, grad_heads, grad_w_out = ffn(
-        dp_size, attended, w_out_heads, x, b_out, norm2_gain, norm2_shift, b_down, cot, w_up, w_down, b_up[None]
+        dp_size, attended, x, b_out, norm2_gain, norm2_shift, b_down, w_out, w_out_got, cotangent, cot_got, w_up, w_down, b_up[None]
     )
     out_got = swap(out_other, "tw")
     dq, dk, dv = attn_bwd(query, key, value, grad_heads, attended, totals, *tables)
     chunks, heads, small, grad_tokens = finish(
         dp_size, red, dq, dk, dv, normed_t, w_heads, grad_w_out, x, grad_middle, norm1_gain, sums, grad_b_up
     )
-    (up, down, w_qkv_grad, w_out_grad, block_out), vecs = widen(tw, chunks, heads, out_mine, out_got, small)
-    b_qv_grad = lax.dynamic_slice_in_dim(small[-16:].reshape(4, 2, 256), 2 * th + tw, 1, 0)[0, :, :mine]
+    where = jnp.stack([tw, 2 * th + tw]).astype(jnp.int32)
+    (up, down, w_qkv_grad, w_out_grad, block_out, grad_tokens, b_qv_grad), vecs = widen(
+        where, chunks, heads, out_mine, out_got, small, grad_tokens
+    )
     return (
         block_out,
         grad_tokens,

time: 249 us -> 245 us (0.984)
  waiting for transfers between devices: 3.16 us -> 0.01 us
    pallas_call x1, Pallas kernels: 83.7 us -> 76.3 us  [finish(): pl.pallas_call(functools.partial(finish_kernel, dp), in_specs=[pl.BlockSp...]
    pallas_call x1, Pallas kernels: 25.1 us -> 31.1 us  [attn_bwd(): pl.pallas_call(bwd_kernel, grid_spec=pltpu.PrefetchScalarGridSpec(num_sca...]
    pallas_call x1, Pallas kernels: 16.2 us -> 20.6 us  [attn_fwd(): pl.pallas_call(fwd_kernel, grid_spec=pltpu.PrefetchScalarGridSpec(num_sca...]
    ppermute x3, waiting for transfers between devices: 3.16 us -> 0.01 us  [swap(): return lax.ppermute(value, axis, SWAP)]
  transfers between devices with their start and end apart: 3 -> 3, of which waited for: 1 -> 0; matrix products, arithmetic and copies ran while one was open for 1% -> 0% of each run, Pallas kernels for 50% -> 53%
where the time goes in v3:
time: 245 us; the launch traced here: 243 us
  Pallas kernels  234 us (96%)
  local copies, waits for them, and re-layouts  4.28 us (2%)
  starting transfers between devices  3.27 us (1%)
    pallas_call x1, Pallas kernels, finish(): pl.pallas_call(functools.partial(finish_kernel, dp), in_specs=[pl.BlockSp...  76.3 us
    pallas_call x1, Pallas kernels, ffn(): pl.pallas_call(functools.partial(ffn_kernel, dp), in_specs=[whole(v.shape...  59.4 us
    pallas_call x1, Pallas kernels, front(): pl.pallas_call(front_kernel, in_specs=[pl.BlockSpec(memory_space=pltpu.VM...  33.1 us
    pallas_call x1, Pallas kernels, attn_bwd(): pl.pallas_call(bwd_kernel, grid_spec=pltpu.PrefetchScalarGridSpec(num_sca...  31.1 us
    pallas_call x1, Pallas kernels, attn_fwd(): pl.pallas_call(fwd_kernel, grid_spec=pltpu.PrefetchScalarGridSpec(num_sca...  20.6 us
    pallas_call x1, Pallas kernels, widen(): pl.pallas_call(widen_kernel, grid=(CH,), in_specs=[pl.BlockSpec(memory_sp...  13.5 us
  transfers between devices with their start and end apart: 3, of which 0 were waited for; matrix products, arithmetic and copies ran while one was open for 0% of the time, Pallas kernels for 53%

profile of v3, /device:TPU:0, one launch (start us, length us, event | category | flops | bytes accessed | tf_op | source)
XLA Modules:
  0.0 243.3 jit_solution(12484548184485754654)
XLA Ops:
  0.6 0.0 copy-start.4
  0.7 0.0 copy-start.5
  0.7 33.1 %front.1 = (bf16[768,768]{1,0:T(8,128)(2,1)}, bf16[768,1536]{1,0:T(8,128)(2,1)}, bf16[1536,384]{1,0:T(8,128)(2,1)}, bf16[1536,384]{1,0:T(8,128)(2,1)}, bf16[1536...) custom-call(bf16[2,384,768]{2,1,0:T(8,128)(2,1)} %tok.1, ...), custom_call_target="tpu_custom_call" | custom-call | tf_op jit(solution)/shard_map/front/pallas_call | solution.py:672
  33.8 0.7 collective-permute-start.1
  34.5 1.4 collective-permute-start
  35.9 0.1 slice.7
  36.0 0.1 slice.6
  36.1 0.2 convert_reduce_fusion
  36.4 0.5 and_select_fusion
  36.9 20.6 %attention_forward.1 = (bf16[1536,384]{1,0:T(8,128)(2,1)}, f32[8,1536]{1,0:T(8,128)}) custom-call(s32[6]{0:T(128)} %get-tuple-element.99.lo_ref, s32[6]{0:T(128)} %get-tuple-element.98.n_ref, bf16[1536,384]{1,0:T(8,128)(2,1)} %get-tuple-element.55.q_ref, bf16[1536,384]{1,0:T(8,128)(2,1)} %get-tuple-element.56.k_ref, ...), custom_call_target="tpu_custom_call" | custom-call | tf_op jit(solution)/shard_map/attention_forward/pallas_call | solution.py:76
  57.5 0.0 collective-permute-done.wo_got
  57.5 0.0 copy-start.6
  57.5 0.0 collective-permute-done.1.cot_got
  57.5 0.7 copy-done.6
  58.2 59.4 %feed_forward.1 = (bf16[384,768]{1,0:T(8,128)(2,1)}, bf16[384,768]{1,0:T(8,128)(2,1)}, f32[768,768]{1,0:T(8,128)}, f32[1,3072]{1,0:T(1,128)}, f32[8,768]{1,0:T(8...) custom-call(bf16[1536,384]{1,0:T(8,128)(2,1)} %get-tuple-element.60.att.o_ref, ...), custom_call_target="tpu_custom_call" | custom-call | tf_op jit(solution)/shard_map/feed_forward/pallas_call | solution.py:385
  117.7 1.2 collective-permute-start.2
  118.8 0.1 pad_add_fusion.where
  118.9 31.1 %attention_backward.1 = (bf16[1536,384]{1,0:T(8,128)(2,1)}, bf16[1536,384]{1,0:T(8,128)(2,1)}, bf16[1536,384]{1,0:T(8,128)(2,1)}) custom-call(s32[6]{0:T(128)} %get-tuple-element.99.lo_ref, s32[6]{0:T(128)} %get-tuple-element.98.n_ref, bf16[1536,384]{1,0:T(8,128)(2,1)} %get-tuple-element.55.q_ref, bf16[1536,384]{1,0:T(8,128)(2,1)} %get-tuple-element.56.k_ref, ...), custom_call_target="tpu_custom_call" | custom-call | tf_op jit(solution)/shard_map/attention_backward/pallas_call | solution.py:141
  150.0 76.3 %finish_gradients.1 = (bf16[6,2,3072,128]{3,2,1,0:T(8,128)(2,1)}, bf16[3,1536,128]{2,1,0:T(8,128)(2,1)}, f32[76,128]{1,0:T(8,128)}, bf16[2,384,768]{2,1,0:T(8,128)(2,1)}) custom-call(bf16[6,192,128]{2,1,0:T(8,128)(2,1)} %get-tuple-element.64.red, bf16[1536,384]{1,0:T(8,128)(2,1)} %get-tuple-element.67.dq_h, bf16[1536,384]{1,0:T(8,128)(2,1)} %get-tuple-element.68.dk_h, ...), custom_call_target="tpu_custom_call" | custom-call | tf_op jit(solution)/shard_map/finish_gradients/pallas_call | solution.py:541
  226.3 0.0 collective-permute-done.2.got
  226.3 1.3 copy-done
  227.6 1.3 copy-done.1
  228.8 0.8 copy-done.3
  229.6 13.5 %widen.1 = (f32[768,3072]{1,0:T(8,128)}, f32[3072,768]{1,0:T(8,128)}, f32[3,192,768]{2,1,0:T(8,128)}, f32[192,768]{1,0:T(8,128)}, bf16[2,384,768]{2,1,0:T(8,128)...) custom-call(s32[2]{0:T(128)S(1)} %pad_add_fusion.where, ...), custom_call_target="tpu_custom_call" | custom-call | tf_op jit(solution)/shard_map/widen/pallas_call | solution.py:575
  (11 shorter events, 0.1 us)
Async XLA Ops:
  0.6 33.1 %copy-start.4 = (bf16[2,384,768]{2,1,0:T(8,128)(2,1)S(1)}, bf16[2,384,768]{2,1,0:T(8,128)(2,1)}, u32[]{:S(2)}) copy-start(bf16[2,384,768]{2,1,0:T(8,128)(2,1)} %cot_h.1) | copy-start | bytes 3538948
  0.7 33.9 %copy-start.5 = (bf16[192,768]{1,0:T(8,128)(2,1)S(1)}, bf16[192,768]{1,0:T(8,128)(2,1)}, u32[]{:S(2)}) copy-start(bf16[192,768]{1,0:T(8,128)(2,1)} %wo_h.1) | copy-start | bytes 884740
  0.7 35.2 %copy-start.7 = (s32[2,1536]{1,0:T(2,128)S(1)}, s32[2,1536]{1,0:T(2,128)}, u32[]{:S(2)}) copy-start(s32[2,1536]{1,0:T(2,128)} %seg.1) | copy-start | bytes 36868
  33.8 23.7 %collective-permute-start.1 = (bf16[384,768]{1,0:T(8,128)(2,1)S(1)}, bf16[384,768]{1,0:T(8,128)(2,1)}, u32[]{:S(2)}, u32[]{:S(2)}) collective-permute-start(bf16[384,768]{1,0:T(8,128)(2,1)S(1)} %dynamic-slice_bitcast_fusion), channel_id=1, source_target_pairs={{0,1},{1,0},{2,3},{3,2},{4,5},{5,4},{6,7},{7,6},{8,9},{9,8},{10,11... | collective-permute-start | bytes 1769480 | tf_op jit(solution)/shard_map/ppermute | solution.py:684
  34.5 23.0 %collective-permute-start = (bf16[192,768]{1,0:T(8,128)(2,1)S(1)}, bf16[192,768]{1,0:T(8,128)(2,1)S(1)}, u32[]{:S(2)}, u32[]{:S(2)}) collective-permute-start(bf16[192,768]{1,0:T(8,128)(2,1)S(1)} %copy-done.5), channel_id=1, source_target_pairs={{0,1},{1,0},{2,3},{3,2},{4,5},{5,4},{6,7},{7,6},{8,9},{9,8},{10,11... | collective-permute-start | bytes 884744 | tf_op jit(solution)/shard_map/ppermute | solution.py:684
  57.5 0.7 copy-start.6
  117.7 108.6 %collective-permute-start.2 = (bf16[384,768]{1,0:T(8,128)(2,1)}, bf16[384,768]{1,0:T(8,128)(2,1)S(1)}, u32[]{:S(2)}, u32[]{:S(2)}) collective-permute-start(bf16[384,768]{1,0:T(8,128)(2,1)} %get-tuple-element.79), channel_id=1, source_target_pairs={{0,1},{1,0},{2,3},{3,2},{4,5},{5,4},{6,7},{7,6},{8,9},{9,8},{10,11... | collective-permute-start | bytes 1769480 | tf_op jit(solution)/shard_map/ppermute | solution.py:684
  150.0 76.3 %copy-start.2 = (bf16[384,768]{1,0:T(8,128)(2,1)S(1)}, bf16[384,768]{1,0:T(8,128)(2,1)}, u32[]{:S(2)}) copy-start(bf16[384,768]{1,0:T(8,128)(2,1)} %get-tuple-element.78.mine) | copy-start | bytes 1769476
  226.3 1.3 copy-start
  227.6 1.3 copy-start.1
  228.8 0.8 copy-start.3

commit v4 on v3

--- a/solution.py
+++ b/solution.py
@@ -13,15 +13,16 @@
 def dot(a,b,d): return lax.dot_general(a,b,d,preferred_element_type=F32)
 
 AL=128; VR=80; GRP=3
-def key_rows(lo_ref,mk_ref,i,j):
-    L=mk_ref.shape[0]
-    want=lo_ref[i]+j*BK
-    start=pl.multiple_of(jnp.minimum(want,L-BK),AL)
-    row=lax.broadcasted_iota(jnp.int32,(BK,128),0); lane=lax.broadcasted_iota(jnp.int32,(BK,128),1)
-    ks=pl.ds(start,BK)
-    return ks,jnp.where(((lane==8)|(lane==HD+8))&(row<want-start),jnp.ones((BK,128),BF),mk_ref[ks,:])
-
-def fwd_kernel(lo_ref, n_ref, q_ref, k_ref, v_ref, mq_ref, mk_ref, o_ref, lse_ref, m_ref, acc_ref, vT_ref, qm_ref, *score_refs):
+def each_chunk(lo_ref,n_ref,i,body):
+    lo=lo_ref[i]; n=n_ref[i]
+    def full(j,_):
+        body(pl.ds(pl.multiple_of(lo+j*BK,AL),BK))
+        return 0
+    lax.fori_loop(0,n//2,full,0)
+    @pl.when(n%2==1)
+    def _(): body(pl.ds(pl.multiple_of(lo+n//2*BK,AL),AL))
+
+def fwd_kernel(lo_ref, n_ref, q_ref, k_ref, v_ref, mq_ref, mk_ref, o_ref, lse_ref, m_ref, acc_ref, vT_ref, qm_ref):
     i=pl.program_id(0); H=q_ref.shape[1]//HD
     lane=lax.broadcasted_iota(jnp.int32,(1,128),1)
     halves=(lane<HD, lane>=HD)
@@ -46,25 +47,12 @@
         return jnp.exp(s-m_new).astype(BF),jnp.exp(m_old-m_new)
     def weigh(h,ks,pe,alpha):
         acc_ref[h]=acc_ref[h]*alpha+dot(vT_ref[h,:,ks],pe,NN)
-    n=n_ref[i]
-    def half(j,now,then):
-        ks,_=key_rows(lo_ref,mk_ref,i,j)
-        kn,mk=key_rows(lo_ref,mk_ref,i,j+1)
-        last=None
-        for h in range(H):
-            then[h]=score(h,kn,mk)
-            probs=soft(h,now[h])
-            if last is not None: weigh(h-1,ks,*last)
-            last=probs
-        weigh(H-1,ks,*last)
-    ks,mk=key_rows(lo_ref,mk_ref,i,0)
-    for h in range(H): score_refs[0][h]=score(h,ks,mk)
-    def body(t,_):
-        half(2*t,*score_refs)
-        @pl.when(2*t+1<n)
-        def _(): half(2*t+1,*score_refs[::-1])
-        return 0
-    lax.fori_loop(0,(n+1)//2,body,0)
+    def body(ks):
+        mk=mk_ref[ks,:]
+        scores=[score(h,ks,mk) for h in range(H)]
+        probs=[soft(h,scores[h]) for h in range(H)]
+        for h in range(H): weigh(h,ks,*probs[h])
+    each_chunk(lo_ref,n_ref,i,body)
     for p in range(H//2):
         parts=[acc_ref[h,0:HD,:]*(1.0/acc_ref[h,HD:HD+1,:]) for h in (2*p,2*p+1)]
         o_ref[:,p*128:(p+1)*128]=jnp.concatenate(parts,0).T.astype(BF)
@@ -78,7 +66,7 @@
           in_specs=[pl.BlockSpec((BQ,C),lambda i,*_:(i,0)),pl.BlockSpec((L,C),lambda i,*_:(0,0)),pl.BlockSpec((L,C),lambda i,*_:(0,0)),
                     pl.BlockSpec((BQ,128),lambda i,*_:(i,0)),pl.BlockSpec((L,128),lambda i,*_:(0,0))],
           out_specs=[pl.BlockSpec((BQ,C),lambda i,*_:(i,0)),pl.BlockSpec((8,BQ),lambda i,*_:(0,i))],
-          scratch_shapes=[pltpu.VMEM((8,BQ),F32),pltpu.VMEM((C//HD,VR,BQ),F32),pltpu.VMEM((C//HD,VR,L),BF),pltpu.VMEM((C//HD,BQ,128),BF),pltpu.VMEM((C//HD,BK,BQ),F32),pltpu.VMEM((C//HD,BK,BQ),F32)]),
+          scratch_shapes=[pltpu.VMEM((8,BQ),F32),pltpu.VMEM((C//HD,VR,BQ),F32),pltpu.VMEM((C//HD,VR,L),BF),pltpu.VMEM((C//HD,BQ,128),BF)]),
         out_shape=[jax.ShapeDtypeStruct((L,C),BF),jax.ShapeDtypeStruct((8,L),F32)],
         name="attention_forward",
     )(lo,n,q,k,v,mq,mk)
@@ -105,8 +93,8 @@
             qm[p,e*BQ:(e+1)*BQ,:]=jnp.where(halves[e],q2,mq_ref[...])
             docat[p,e*BQ:(e+1)*BQ,:]=jnp.where(halves[e],d2,jnp.zeros_like(d2))
     lse=lse_ref[...]
-    def body(j,_):
-        ks,mk=key_rows(lo_ref,mk_ref,i,j)
+    def body(ks):
+        mk=mk_ref[ks,:]
         for g in range(0,pairs,GRP):
             work=[]
             for p in range(g,g+GRP):
@@ -128,8 +116,7 @@
                 for e,d in enumerate((d0,d1)):
                     r=slice((2*p+e)*HD,(2*p+e+1)*HD)
                     dq_acc[r,:]+=dot(kT[r,ks],d,NN)
-        return 0
-    lax.fori_loop(0,n_ref[i],body,0)
+    each_chunk(lo_ref,n_ref,i,body)
     dq_ref[...]=(dq_acc[...]*0.125).T.astype(BF)
     @pl.when(i==n-1)
     def _():
@@ -151,7 +138,7 @@
     first=seg[::BQ]; last=seg[BQ-1::BQ]
     lo=jnp.sum(seg[None,:]<first[:,None],axis=1,dtype=jnp.int32)//AL*AL
     hi=jnp.sum(seg[None,:]<=last[:,None],axis=1,dtype=jnp.int32)
-    return lo,(hi-lo+BK-1)//BK
+    return lo,(hi-lo+AL-1)//AL
 
 
 TT=256; FC=512
@@ -573,10 +560,10 @@
     CH,_,R,_=chunks.shape; D=R*128//FC; FF=CH*FC; q=heads.shape[0]*heads.shape[1]*128//(4*D); T2=mine.shape[0]
     outs=[(D,FF),(FF,D),(3,q,D),(q,D)]; sizes=[D]*6+[FF]
     res=pl.pallas_call(widen_kernel,grid=(CH,),
-      in_specs=[pl.BlockSpec(memory_space=pltpu.SMEM),pl.BlockSpec((None,2,R,128),lambda g:(g,0,0,0))]+[pl.BlockSpec(memory_space=pltpu.VMEM)]*5,
+      in_specs=[pl.BlockSpec(memory_space=pltpu.SMEM),pl.BlockSpec((None,2,R,128),lambda g:(g,0,0,0))]+[pl.BlockSpec(a.shape,lambda g,n=a.ndim:(0,)*n) for a in (heads,mine,got,vec,tok)],
       out_specs=[pl.BlockSpec((D,FC),lambda g:(0,g)),pl.BlockSpec((FC,D),lambda g:(g,0))]+[pl.BlockSpec(memory_space=pltpu.VMEM)]*(5+len(sizes)),
       out_shape=[jax.ShapeDtypeStruct(o,F32) for o in outs]+[jax.ShapeDtypeStruct((2,T2,D),BF)]*2+[jax.ShapeDtypeStruct((2,q),F32)]+[jax.ShapeDtypeStruct((z,),F32) for z in sizes],
-      compiler_params=pltpu.CompilerParams(vmem_limit_bytes=50*2**20),name="widen")(where,chunks,heads,mine,got,vec,tok)
+      compiler_params=pltpu.CompilerParams(vmem_limit_bytes=63*2**20),name="widen")(where,chunks,heads,mine,got,vec,tok)
     return res[:7],res[7:]
 
 def front_kernel(tok,w,b,gain,shift,seg,x_o,normT_o,q_o,k_o,v_o,wh_o,mq_o,mk_o,x,norm,normT,qkv,wh,wgot,bgot,bias,mq,mk,tsem,bsem,csem,ysem,xsem,zsem,osem):

time: 245 us -> 240 us (0.980)
  Pallas kernels: 234 us -> 230 us
  waiting for transfers between devices: 0.01 us -> 3.23 us
  local copies, waits for them, and re-layouts: 4.28 us -> 1.8 us
    pallas_call x1, Pallas kernels: 31.1 us -> 23.4 us  [attn_bwd(): pl.pallas_call(bwd_kernel, grid_spec=pltpu.PrefetchScalarGridSpec(num_sca...]
    pallas_call x1, Pallas kernels: 76.3 us -> 81.8 us  [finish(): pl.pallas_call(functools.partial(finish_kernel, dp), in_specs=[pl.BlockSp...]
    pallas_call x1, Pallas kernels: 20.6 us -> 16.1 us  [attn_fwd(): pl.pallas_call(fwd_kernel, grid_spec=pltpu.PrefetchScalarGridSpec(num_sca...]
    ppermute x3, waiting for transfers between devices: 0.01 us -> 3.23 us  [swap(): return lax.ppermute(value, axis, SWAP)]
    unnamed x16 -> x10, local copies, waits for them, and re-layouts: 4.03 us -> 1.55 us
  transfers between devices with their start and end apart: 3 -> 3, of which waited for: 0 -> 1; matrix products, arithmetic and copies ran while one was open for 0% -> 1% of each run, Pallas kernels for 53% -> 50%
where the time goes in v4:
time: 240 us
  Pallas kernels  230 us (96%)
  starting transfers between devices  3.35 us (1%)
  waiting for transfers between devices  3.23 us (1%)
    pallas_call x1, Pallas kernels, finish(): pl.pallas_call(functools.partial(finish_kernel, dp), in_specs=[pl.BlockSp...  81.8 us
    pallas_call x1, Pallas kernels, ffn(): pl.pallas_call(functools.partial(ffn_kernel, dp), in_specs=[whole(v.shape...  60.9 us
    pallas_call x1, Pallas kernels, front(): pl.pallas_call(front_kernel, in_specs=[pl.BlockSpec(memory_space=pltpu.VM...  32.9 us
    pallas_call x1, Pallas kernels, attn_bwd(): pl.pallas_call(bwd_kernel, grid_spec=pltpu.PrefetchScalarGridSpec(num_sca...  23.4 us
    pallas_call x1, Pallas kernels, attn_fwd(): pl.pallas_call(fwd_kernel, grid_spec=pltpu.PrefetchScalarGridSpec(num_sca...  16.1 us
    pallas_call x1, Pallas kernels, widen(): pl.pallas_call(widen_kernel, grid=(CH,), in_specs=[pl.BlockSpec(memory_sp...  14.6 us
  transfers between devices with their start and end apart: 3, of which 1 were waited for; matrix products, arithmetic and copies ran while one was open for 1% of the time, Pallas kernels for 50%

profile of v4, /device:TPU:0, one launch (start us, length us, event | category | flops | bytes accessed | tf_op | source)
XLA Modules:
  0.0 240.4 jit_solution(5936669540112666050)
XLA Ops:
  0.6 0.0 copy-start
  0.7 0.0 copy-start.2
  0.7 0.0 copy-start.4
  0.7 32.9 %front.1 = (bf16[768,768]{1,0:T(8,128)(2,1)}, bf16[768,1536]{1,0:T(8,128)(2,1)}, bf16[1536,384]{1,0:T(8,128)(2,1)}, bf16[1536,384]{1,0:T(8,128)(2,1)}, bf16[1536...) custom-call(bf16[2,384,768]{2,1,0:T(8,128)(2,1)} %tok.1, ...), custom_call_target="tpu_custom_call" | custom-call | tf_op jit(solution)/shard_map/front/pallas_call | solution.py:659
  33.6 0.7 collective-permute-start.1
  34.3 1.4 collective-permute-start
  35.7 0.0 copy-done.4
  35.8 0.1 slice.7
  35.9 0.1 slice.6
  35.9 0.2 convert_reduce_fusion
  36.2 0.5 and_select_fusion
  36.7 16.1 %attention_forward.1 = (bf16[1536,384]{1,0:T(8,128)(2,1)}, f32[8,1536]{1,0:T(8,128)}) custom-call(s32[6]{0:T(128)} %get-tuple-element.99.lo_ref, s32[6]{0:T(128)} %get-tuple-element.98.n_ref, bf16[1536,384]{1,0:T(8,128)(2,1)} %get-tuple-element.55.q_ref, bf16[1536,384]{1,0:T(8,128)(2,1)} %get-tuple-element.56.k_ref, ...), custom_call_target="tpu_custom_call" | custom-call | tf_op jit(solution)/shard_map/attention_forward/pallas_call | solution.py:64
  52.8 3.2 %collective-permute-done.wo_got = bf16[192,768]{1,0:T(8,128)(2,1)S(1)} collective-permute-done((bf16[192,768]{1,0:T(8,128)(2,1)S(1)}, bf16[192,768]{1,0:T(8,128)(2,1)S(1)}, u32[]{:S(2)}, u32[]{:S(2)}) %collective-permute-start) | collective-permute-done | bytes 294944 | tf_op jit(solution)/shard_map/ppermute | solution.py:671
  56.0 0.0 collective-permute-done.1.cot_got
  56.0 0.7 copy-done.3
  56.8 60.9 %feed_forward.1 = (bf16[384,768]{1,0:T(8,128)(2,1)}, bf16[384,768]{1,0:T(8,128)(2,1)}, f32[768,768]{1,0:T(8,128)}, f32[1,3072]{1,0:T(1,128)}, f32[8,768]{1,0:T(8...) custom-call(bf16[1536,384]{1,0:T(8,128)(2,1)} %get-tuple-element.60.att.o_ref, ...), custom_call_target="tpu_custom_call" | custom-call | tf_op jit(solution)/shard_map/feed_forward/pallas_call | solution.py:372
  117.7 1.3 collective-permute-start.2
  119.0 0.6 pad_add_fusion.where
  119.6 23.4 %attention_backward.1 = (bf16[1536,384]{1,0:T(8,128)(2,1)}, bf16[1536,384]{1,0:T(8,128)(2,1)}, bf16[1536,384]{1,0:T(8,128)(2,1)}) custom-call(s32[6]{0:T(128)} %get-tuple-element.99.lo_ref, s32[6]{0:T(128)} %get-tuple-element.98.n_ref, bf16[1536,384]{1,0:T(8,128)(2,1)} %get-tuple-element.55.q_ref, bf16[1536,384]{1,0:T(8,128)(2,1)} %get-tuple-element.56.k_ref, ...), custom_call_target="tpu_custom_call" | custom-call | tf_op jit(solution)/shard_map/attention_backward/pallas_call | solution.py:128
  143.0 81.8 %finish_gradients.1 = (bf16[6,2,3072,128]{3,2,1,0:T(8,128)(2,1)}, bf16[3,1536,128]{2,1,0:T(8,128)(2,1)}, f32[76,128]{1,0:T(8,128)}, bf16[2,384,768]{2,1,0:T(8,128)(2,1)}) custom-call(bf16[6,192,128]{2,1,0:T(8,128)(2,1)} %get-tuple-element.64.red, bf16[1536,384]{1,0:T(8,128)(2,1)} %get-tuple-element.67.dq_h, bf16[1536,384]{1,0:T(8,128)(2,1)} %get-tuple-element.68.dk_h, ...), custom_call_target="tpu_custom_call" | custom-call | tf_op jit(solution)/shard_map/finish_gradients/pallas_call | solution.py:528
  224.8 0.0 collective-permute-done.2.got
  224.8 0.0 copy-start.1
  224.8 0.8 copy-done.1
  225.7 14.6 %widen.1 = (f32[768,3072]{1,0:T(8,128)}, f32[3072,768]{1,0:T(8,128)}, f32[3,192,768]{2,1,0:T(8,128)}, f32[192,768]{1,0:T(8,128)}, bf16[2,384,768]{2,1,0:T(8,128)...) custom-call(s32[2]{0:T(128)} %pad_add_fusion.where, ...), custom_call_target="tpu_custom_call" | custom-call | tf_op jit(solution)/shard_map/widen/pallas_call | solution.py:562
  (5 shorter events, 0.1 us)
Async XLA Ops:
  0.6 32.9 %copy-start = (bf16[2,384,768]{2,1,0:T(8,128)(2,1)S(1)}, bf16[2,384,768]{2,1,0:T(8,128)(2,1)}, u32[]{:S(2)}) copy-start(bf16[2,384,768]{2,1,0:T(8,128)(2,1)} %cot_h.1) | copy-start | bytes 3538948
  0.7 33.7 %copy-start.2 = (bf16[192,768]{1,0:T(8,128)(2,1)S(1)}, bf16[192,768]{1,0:T(8,128)(2,1)}, u32[]{:S(2)}) copy-start(bf16[192,768]{1,0:T(8,128)(2,1)} %wo_h.1) | copy-start | bytes 884740
  0.7 35.1 %copy-start.4 = (s32[2,1536]{1,0:T(2,128)S(1)}, s32[2,1536]{1,0:T(2,128)}, u32[]{:S(2)}) copy-start(s32[2,1536]{1,0:T(2,128)} %seg.1) | copy-start | bytes 36868
  33.6 22.4 %collective-permute-start.1 = (bf16[384,768]{1,0:T(8,128)(2,1)S(1)}, bf16[384,768]{1,0:T(8,128)(2,1)}, u32[]{:S(2)}, u32[]{:S(2)}) collective-permute-start(bf16[384,768]{1,0:T(8,128)(2,1)S(1)} %dynamic-slice_bitcast_fusion), channel_id=1, source_target_pairs={{0,1},{1,0},{2,3},{3,2},{4,5},{5,4},{6,7},{7,6},{8,9},{9,8},{10,11... | collective-permute-start | bytes 1769480 | tf_op jit(solution)/shard_map/ppermute | solution.py:671
  34.3 21.7 %collective-permute-start = (bf16[192,768]{1,0:T(8,128)(2,1)S(1)}, bf16[192,768]{1,0:T(8,128)(2,1)S(1)}, u32[]{:S(2)}, u32[]{:S(2)}) collective-permute-start(bf16[192,768]{1,0:T(8,128)(2,1)S(1)} %copy-done.2), channel_id=1, source_target_pairs={{0,1},{1,0},{2,3},{3,2},{4,5},{5,4},{6,7},{7,6},{8,9},{9,8},{10,11... | collective-permute-start | bytes 884744 | tf_op jit(solution)/shard_map/ppermute | solution.py:671
  56.0 0.7 copy-start.3
  117.7 107.1 %collective-permute-start.2 = (bf16[384,768]{1,0:T(8,128)(2,1)}, bf16[384,768]{1,0:T(8,128)(2,1)S(1)}, u32[]{:S(2)}, u32[]{:S(2)}) collective-permute-start(bf16[384,768]{1,0:T(8,128)(2,1)} %get-tuple-element.79), channel_id=1, source_target_pairs={{0,1},{1,0},{2,3},{3,2},{4,5},{5,4},{6,7},{7,6},{8,9},{9,8},{10,11... | collective-permute-start | bytes 1769480 | tf_op jit(solution)/shard_map/ppermute | solution.py:671
  224.8 0.8 copy-start.1

commit v5 on v4

--- a/solution.py
+++ b/solution.py
@@ -160,7 +160,7 @@
     orders=(["tw"]+list(range(n)),[0,"tw"]+list(range(1,n)),[1,2,0,"tw"]+list(range(3,n)))
     unit=16<<n
     units=rows//unit
-    low=max(1,units//6)
+    low=max(1,units//4)
     mid=max(1,units//3)
     return streams(orders,[units-mid-low,mid,low],unit)
 
@@ -567,10 +567,10 @@
     return res[:7],res[7:]
 
 def front_kernel(tok,w,b,gain,shift,seg,x_o,normT_o,q_o,k_o,v_o,wh_o,mq_o,mk_o,x,norm,normT,qkv,wh,wgot,bgot,bias,mq,mk,tsem,bsem,csem,ysem,xsem,zsem,osem):
-    p=Peers(); Q,D=tok.shape[1:]; T=2*Q; L=2*T; E=w.shape[1]; PART=E//4
+    p=Peers(); Q,D=tok.shape[1:]; T=2*Q; L=2*T; E=w.shape[1]; PART=E//4; HQ=Q//2
     b0,b1=p.bit(0),p.bit(1)
     barrier(p,["th","tw",0,1])
-    def tcopy(): return send(tok.at[1-p.tw],x.at[rows_at(p.tw*Q,Q),:],tsem.at[0],tsem.at[1],p.peer("tw"))
+    def tcopy(i): return send(tok.at[1-p.tw,i*HQ:(i+1)*HQ,:],x.at[rows_at(p.tw*Q+i*HQ,HQ),:],tsem.at[0,i],tsem.at[1,i],p.peer("tw"))
     def bcopy(): return send(b,bgot,bsem.at[0],bsem.at[1],p.peer("tw"))
     def ycopy(c):
         r=rows_at((2*b1+b0)*PART,PART)
@@ -583,20 +583,20 @@
         return send(ref,ref,zsem.at[0,c],zsem.at[1,c],p.peer(1))
     def ccopy(i,landed):
         core=1-p.th if landed else p.th
-        quarter=p.tw if i==0 else 1-p.tw
-        ref=norm.at[rows_at(core*T+quarter*Q,Q),:]
+        row=core*T+(p.tw*Q if i==0 else (1-p.tw)*Q+(i-1)*HQ)
+        ref=norm.at[rows_at(row,Q if i==0 else HQ),:]
         return send(ref,ref,csem.at[0,i],csem.at[1,i],p.peer("th"))
     for c in range(3): ycopy(c).start()
     bcopy().start()
-    tcopy().start()
+    for i in range(2): tcopy(i).start()
     g_row=gain[...].reshape(1,D); s_row=shift[...].reshape(1,D)
-    def normalize(src,row):
-        for t in range(Q//128):
+    def normalize(src,row,rows):
+        for t in range(rows//HQ):
             y=(norm_parts(src(t).astype(F32))[0]*g_row+s_row).astype(BF)
-            norm[rows_at(row+t*128,128),:]=y
+            norm[rows_at(row+t*HQ,HQ),:]=y
     def put(src,dst,i): return pltpu.make_async_copy(src,dst,osem.at[i])
     x[rows_at(p.tw*Q,Q),:]=tok[p.tw]
-    normalize(lambda t: tok[p.tw,t*128:(t+1)*128,:],p.th*T+p.tw*Q)
+    normalize(lambda t: tok[p.tw,t*HQ:(t+1)*HQ,:],p.th*T+p.tw*Q,Q)
     onehot=lax.broadcasted_iota(jnp.int32,(128,L),0)
     onehot=jnp.where(onehot<HD,onehot,onehot-HD)
     same=onehot==seg[pl.ds(p.tw,1),:]
@@ -614,8 +614,8 @@
     for c in range(3):
         xcopy(c,True).wait_recv()
         zcopy(c,False).start()
-    def project(row,weights,m):
-        r=rows_at(row,Q)
+    def project(row,weights,m,rows=Q):
+        r=rows_at(row,rows)
         def one(c,_):
             y=(dot(norm[r,:],weights[c],NT)+bias[m,pl.ds(c,1),:]).astype(BF)
             y=y*jnp.where(c==0,0.125,1.0).astype(BF)
@@ -634,14 +634,16 @@
     for core in range(2): project(core*T+p.tw*Q,wgot,1)
     for c in range(3): wh[c,0:E,:]=w[c]; wh[c,E:2*E,:]=wgot[c]
     put(wh,wh_o,7).start()
-    tcopy().wait_recv()
-    normalize(lambda t: x[rows_at((1-p.tw)*Q+t*128,128),:],p.th*T+(1-p.tw)*Q)
-    put(x,x_o,2).start()
-    for m,weights in enumerate((w,wgot)):
-        project(p.th*T+(1-p.tw)*Q,weights,m)
-        if m==0: ccopy(1,False).start()
-    ccopy(1,True).wait_recv()
-    for m,weights in enumerate((w,wgot)): project((1-p.th)*T+(1-p.tw)*Q,weights,m)
+    for i in range(2):
+        row=(1-p.tw)*Q+i*HQ
+        tcopy(i).wait_recv()
+        normalize(lambda t: x[rows_at(row,HQ),:],p.th*T+row,HQ)
+        if i==1: put(x,x_o,2).start()
+        for m,weights in enumerate((w,wgot)):
+            project(p.th*T+row,weights,m,HQ)
+            if m==0: ccopy(1+i,False).start()
+        ccopy(1+i,True).wait_recv()
+        for m,weights in enumerate((w,wgot)): project((1-p.th)*T+row,weights,m,HQ)
     for c in range(3): put(qkv.at[c],(q_o,k_o,v_o)[c],4+c).start()
     transpose(1-p.tw)
     put(normT,normT_o,3).start()
@@ -649,8 +651,9 @@
     for c in range(3):
         put(qkv.at[c],(q_o,k_o,v_o)[c],4+c).wait()
         ycopy(c).wait_send(); xcopy(c,False).wait_send(); zcopy(c,False).wait_send()
-    tcopy().wait_send(); bcopy().wait_send()
-    for i in range(2): ccopy(i,False).wait_send()
+    bcopy().wait_send()
+    for i in range(2): tcopy(i).wait_send()
+    for i in range(3): ccopy(i,False).wait_send()
 
 def front(tok,w,b,gain,shift,seg):
     _,Q,D=tok.shape; T=2*Q; L=2*T; E=w.shape[1]
@@ -660,7 +663,7 @@
       in_specs=[pl.BlockSpec(memory_space=pltpu.VMEM)]*6,out_specs=[pl.BlockSpec(memory_space=pl.ANY)]*len(outs),
       out_shape=[jax.ShapeDtypeStruct(*o) for o in outs],
       scratch_shapes=[pltpu.VMEM((T,D),BF),pltpu.VMEM((L,D),BF),pltpu.VMEM((D,L),BF),pltpu.VMEM((3,L,2*E),BF),pltpu.VMEM((3,2*E,D),BF),pltpu.VMEM((3,E,D),BF),
-        pltpu.VMEM(b.shape,F32),pltpu.VMEM((2,8,E),F32),pltpu.VMEM((L,128),BF),pltpu.VMEM((L,128),BF),sem((2,)),sem((2,)),sem((2,2)),sem((2,3)),sem((2,3)),sem((2,3)),sem((8,))],
+        pltpu.VMEM(b.shape,F32),pltpu.VMEM((2,8,E),F32),pltpu.VMEM((L,128),BF),pltpu.VMEM((L,128),BF),sem((2,2)),sem((2,)),sem((2,3)),sem((2,3)),sem((2,3)),sem((2,3)),sem((8,))],
       compiler_params=pltpu.CompilerParams(vmem_limit_bytes=60*2**20,collective_id=2,has_side_effects=True),name="front")(tok,w,b,gain,shift,seg)
 
 

time: 240 us -> 243 us (1.012)
  Pallas kernels: 230 us -> 235 us
  waiting for transfers between devices: 3.23 us -> 0.01 us
    pallas_call x1, Pallas kernels: 81.8 us -> 75 us  [finish(): pl.pallas_call(functools.partial(finish_kernel, dp), in_specs=[pl.BlockSp...]
    pallas_call x1, Pallas kernels: 23.4 us -> 29 us  [attn_bwd(): pl.pallas_call(bwd_kernel, grid_spec=pltpu.PrefetchScalarGridSpec(num_sca...]
    pallas_call x1, Pallas kernels: 16.1 us -> 20.4 us  [attn_fwd(): pl.pallas_call(fwd_kernel, grid_spec=pltpu.PrefetchScalarGridSpec(num_sca...]
    pallas_call x1, Pallas kernels: 32.9 us -> 36.4 us  [front(): pl.pallas_call(front_kernel, in_specs=[pl.BlockSpec(memory_space=pltpu.VM...]
    ppermute x3, waiting for transfers between devices: 3.23 us -> 0.01 us  [swap(): return lax.ppermute(value, axis, SWAP)]
  transfers between devices with their start and end apart: 3 -> 3, of which waited for: 1 -> 0; matrix products, arithmetic and copies ran while one was open for 1% -> 1% of each run, Pallas kernels for 50% -> 51%
where the time goes in v5:
time: 243 us
  Pallas kernels  235 us (97%)
  starting transfers between devices  3.99 us (2%)
    pallas_call x1, Pallas kernels, finish(): pl.pallas_call(functools.partial(finish_kernel, dp), in_specs=[pl.BlockSp...  75 us
    pallas_call x1, Pallas kernels, ffn(): pl.pallas_call(functools.partial(ffn_kernel, dp), in_specs=[whole(v.shape...  59.7 us
    pallas_call x1, Pallas kernels, front(): pl.pallas_call(front_kernel, in_specs=[pl.BlockSpec(memory_space=pltpu.VM...  36.4 us
    pallas_call x1, Pallas kernels, attn_bwd(): pl.pallas_call(bwd_kernel, grid_spec=pltpu.PrefetchScalarGridSpec(num_sca...  29 us
    pallas_call x1, Pallas kernels, attn_fwd(): pl.pallas_call(fwd_kernel, grid_spec=pltpu.PrefetchScalarGridSpec(num_sca...  20.4 us
    pallas_call x1, Pallas kernels, widen(): pl.pallas_call(widen_kernel, grid=(CH,), in_specs=[pl.BlockSpec(memory_sp...  14.6 us
  transfers between devices with their start and end apart: 3, of which 0 were waited for; matrix products, arithmetic and copies ran while one was open for 1% of the time, Pallas kernels for 51%

profile of v5, /device:TPU:0, one launch (start us, length us, event | category | flops | bytes accessed | tf_op | source)
XLA Modules:
  0.0 243.2 jit_solution(11529217513418450923)
XLA Ops:
  0.6 0.0 copy-start
  0.7 0.0 copy-start.2
  0.7 0.0 copy-start.4
  0.7 36.4 %front.1 = (bf16[768,768]{1,0:T(8,128)(2,1)}, bf16[768,1536]{1,0:T(8,128)(2,1)}, bf16[1536,384]{1,0:T(8,128)(2,1)}, bf16[1536,384]{1,0:T(8,128)(2,1)}, bf16[1536...) custom-call(bf16[2,384,768]{2,1,0:T(8,128)(2,1)} %tok.1, ...), custom_call_target="tpu_custom_call" | custom-call | tf_op jit(solution)/shard_map/front/pallas_call | solution.py:662
  37.1 0.0 copy-done
  37.2 0.7 collective-permute-start.1
  37.9 1.4 collective-permute-start
  39.3 0.1 slice.7
  39.4 0.1 slice.6
  39.5 0.2 convert_reduce_fusion
  39.7 0.5 and_select_fusion
  40.2 20.4 %attention_forward.1 = (bf16[1536,384]{1,0:T(8,128)(2,1)}, f32[8,1536]{1,0:T(8,128)}) custom-call(s32[6]{0:T(128)} %get-tuple-element.99.lo_ref, s32[6]{0:T(128)} %get-tuple-element.98.n_ref, bf16[1536,384]{1,0:T(8,128)(2,1)} %get-tuple-element.55.q_ref, bf16[1536,384]{1,0:T(8,128)(2,1)} %get-tuple-element.56.k_ref, ...), custom_call_target="tpu_custom_call" | custom-call | tf_op jit(solution)/shard_map/attention_forward/pallas_call | solution.py:64
  60.6 0.0 collective-permute-done.wo_got
  60.6 0.0 copy-start.3
  60.6 0.0 collective-permute-done.1.cot_got
  60.6 0.7 copy-done.3
  61.3 59.7 %feed_forward.1 = (bf16[384,768]{1,0:T(8,128)(2,1)}, bf16[384,768]{1,0:T(8,128)(2,1)}, f32[768,768]{1,0:T(8,128)}, f32[1,3072]{1,0:T(1,128)}, f32[8,768]{1,0:T(8...) custom-call(bf16[1536,384]{1,0:T(8,128)(2,1)} %get-tuple-element.60.att.o_ref, ...), custom_call_target="tpu_custom_call" | custom-call | tf_op jit(solution)/shard_map/feed_forward/pallas_call | solution.py:372
  121.0 1.9 collective-permute-start.2
  122.9 0.6 pad_add_fusion.where
  123.6 29.0 %attention_backward.1 = (bf16[1536,384]{1,0:T(8,128)(2,1)}, bf16[1536,384]{1,0:T(8,128)(2,1)}, bf16[1536,384]{1,0:T(8,128)(2,1)}) custom-call(s32[6]{0:T(128)} %get-tuple-element.99.lo_ref, s32[6]{0:T(128)} %get-tuple-element.98.n_ref, bf16[1536,384]{1,0:T(8,128)(2,1)} %get-tuple-element.55.q_ref, bf16[1536,384]{1,0:T(8,128)(2,1)} %get-tuple-element.56.k_ref, ...), custom_call_target="tpu_custom_call" | custom-call | tf_op jit(solution)/shard_map/attention_backward/pallas_call | solution.py:128
  152.6 75.0 %finish_gradients.1 = (bf16[6,2,3072,128]{3,2,1,0:T(8,128)(2,1)}, bf16[3,1536,128]{2,1,0:T(8,128)(2,1)}, f32[76,128]{1,0:T(8,128)}, bf16[2,384,768]{2,1,0:T(8,128)(2,1)}) custom-call(bf16[6,192,128]{2,1,0:T(8,128)(2,1)} %get-tuple-element.64.red, bf16[1536,384]{1,0:T(8,128)(2,1)} %get-tuple-element.67.dq_h, bf16[1536,384]{1,0:T(8,128)(2,1)} %get-tuple-element.68.dk_h, ...), custom_call_target="tpu_custom_call" | custom-call | tf_op jit(solution)/shard_map/finish_gradients/pallas_call | solution.py:528
  227.6 0.0 collective-permute-done.2.got
  227.7 0.8 copy-done.1
  228.5 14.6 %widen.1 = (f32[768,3072]{1,0:T(8,128)}, f32[3072,768]{1,0:T(8,128)}, f32[3,192,768]{2,1,0:T(8,128)}, f32[192,768]{1,0:T(8,128)}, bf16[2,384,768]{2,1,0:T(8,128)...) custom-call(s32[2]{0:T(128)} %pad_add_fusion.where, ...), custom_call_target="tpu_custom_call" | custom-call | tf_op jit(solution)/shard_map/widen/pallas_call | solution.py:562
  (5 shorter events, 0.1 us)
Async XLA Ops:
  0.6 36.4 %copy-start = (bf16[2,384,768]{2,1,0:T(8,128)(2,1)S(1)}, bf16[2,384,768]{2,1,0:T(8,128)(2,1)}, u32[]{:S(2)}) copy-start(bf16[2,384,768]{2,1,0:T(8,128)(2,1)} %cot_h.1) | copy-start | bytes 3538948
  0.7 37.2 %copy-start.2 = (bf16[192,768]{1,0:T(8,128)(2,1)S(1)}, bf16[192,768]{1,0:T(8,128)(2,1)}, u32[]{:S(2)}) copy-start(bf16[192,768]{1,0:T(8,128)(2,1)} %wo_h.1) | copy-start | bytes 884740
  0.7 38.6 %copy-start.4 = (s32[2,1536]{1,0:T(2,128)S(1)}, s32[2,1536]{1,0:T(2,128)}, u32[]{:S(2)}) copy-start(s32[2,1536]{1,0:T(2,128)} %seg.1) | copy-start | bytes 36868
  37.2 23.5 %collective-permute-start.1 = (bf16[384,768]{1,0:T(8,128)(2,1)S(1)}, bf16[384,768]{1,0:T(8,128)(2,1)}, u32[]{:S(2)}, u32[]{:S(2)}) collective-permute-start(bf16[384,768]{1,0:T(8,128)(2,1)S(1)} %dynamic-slice_bitcast_fusion), channel_id=1, source_target_pairs={{0,1},{1,0},{2,3},{3,2},{4,5},{5,4},{6,7},{7,6},{8,9},{9,8},{10,11... | collective-permute-start | bytes 1769480 | tf_op jit(solution)/shard_map/ppermute | solution.py:674
  37.9 22.7 %collective-permute-start = (bf16[192,768]{1,0:T(8,128)(2,1)S(1)}, bf16[192,768]{1,0:T(8,128)(2,1)S(1)}, u32[]{:S(2)}, u32[]{:S(2)}) collective-permute-start(bf16[192,768]{1,0:T(8,128)(2,1)S(1)} %copy-done.2), channel_id=1, source_target_pairs={{0,1},{1,0},{2,3},{3,2},{4,5},{5,4},{6,7},{7,6},{8,9},{9,8},{10,11... | collective-permute-start | bytes 884744 | tf_op jit(solution)/shard_map/ppermute | solution.py:674
  60.6 0.7 copy-start.3
  121.0 106.6 %collective-permute-start.2 = (bf16[384,768]{1,0:T(8,128)(2,1)}, bf16[384,768]{1,0:T(8,128)(2,1)S(1)}, u32[]{:S(2)}, u32[]{:S(2)}) collective-permute-start(bf16[384,768]{1,0:T(8,128)(2,1)} %get-tuple-element.79), channel_id=1, source_target_pairs={{0,1},{1,0},{2,3},{3,2},{4,5},{5,4},{6,7},{7,6},{8,9},{9,8},{10,11... | collective-permute-start | bytes 1769480 | tf_op jit(solution)/shard_map/ppermute | solution.py:674
  227.6 0.8 copy-start.1

commit v6 on v4

--- a/solution.py
+++ b/solution.py
@@ -160,7 +160,7 @@
     orders=(["tw"]+list(range(n)),[0,"tw"]+list(range(1,n)),[1,2,0,"tw"]+list(range(3,n)))
     unit=16<<n
     units=rows//unit
-    low=max(1,units//6)
+    low=max(1,units//4)
     mid=max(1,units//3)
     return streams(orders,[units-mid-low,mid,low],unit)
 
@@ -533,7 +533,7 @@
         +[pltpu.SemaphoreType.DMA((len(plan),n,CH))]*2+[pltpu.SemaphoreType.DMA((CH,))]*2+[pltpu.SemaphoreType.DMA((len(hplan),n,HC))]*4+[pltpu.SemaphoreType.DMA((nv,))]*2,
       compiler_params=pltpu.CompilerParams(vmem_limit_bytes=60*2**20,collective_id=1,has_side_effects=True),name="finish_gradients")(*args)
 
-def widen_kernel(where,chunk,heads,mine,got,vec,tok,wup,wdown,wqkv,wout,blk,tok_o,bqv,*vectors):
+def widen_kernel(chunk,heads,mine,got,vec,tok,wup,wdown,wqkv,wout,blk,tok_o,bqv,*vectors):
     D=wup.shape[0]; q=wout.shape[0]; g=pl.program_id(0); HT=D//heads.shape[0]
     for i in range(FC//128):
         cols=slice(i*128,(i+1)*128)
@@ -546,24 +546,25 @@
             rr=slice(t*HT,(t+1)*HT)
             for c in range(3): wqkv[c,:,rr]=y[c*q:(c+1)*q,:]
             wout[:,rr]=y[3*q:,:]
-        blk[where[0]]=mine[...]; blk[1-where[0]]=got[...]
+        th,tw=lax.axis_index("th"),lax.axis_index("tw")
+        blk[tw]=mine[...]; blk[1-tw]=got[...]
         tok_o[...]=tok[...]
         at=sum(v.shape[0] for v in vectors)//128
         for i in range(2):
-            for z,w in ((0,128),(1,q-128)): bqv[i:i+1,z*128:z*128+w]=vec[pl.ds(at+4*where[1]+2*i+z,1),0:w]
+            for z,w in ((0,128),(1,q-128)): bqv[i:i+1,z*128:z*128+w]=vec[pl.ds(at+4*(2*th+tw)+2*i+z,1),0:w]
         at=0
         for v in vectors:
             for i in range(v.shape[0]//128):
                 v[i*128:(i+1)*128]=vec[at,:]; at+=1
 
-def widen(where,chunks,heads,mine,got,vec,tok):
+def widen(chunks,heads,mine,got,vec,tok):
     CH,_,R,_=chunks.shape; D=R*128//FC; FF=CH*FC; q=heads.shape[0]*heads.shape[1]*128//(4*D); T2=mine.shape[0]
     outs=[(D,FF),(FF,D),(3,q,D),(q,D)]; sizes=[D]*6+[FF]
     res=pl.pallas_call(widen_kernel,grid=(CH,),
-      in_specs=[pl.BlockSpec(memory_space=pltpu.SMEM),pl.BlockSpec((None,2,R,128),lambda g:(g,0,0,0))]+[pl.BlockSpec(a.shape,lambda g,n=a.ndim:(0,)*n) for a in (heads,mine,got,vec,tok)],
+      in_specs=[pl.BlockSpec((None,2,R,128),lambda g:(g,0,0,0))]+[pl.BlockSpec(a.shape,lambda g,n=a.ndim:(0,)*n) for a in (heads,mine,got,vec,tok)],
       out_specs=[pl.BlockSpec((D,FC),lambda g:(0,g)),pl.BlockSpec((FC,D),lambda g:(g,0))]+[pl.BlockSpec(memory_space=pltpu.VMEM)]*(5+len(sizes)),
       out_shape=[jax.ShapeDtypeStruct(o,F32) for o in outs]+[jax.ShapeDtypeStruct((2,T2,D),BF)]*2+[jax.ShapeDtypeStruct((2,q),F32)]+[jax.ShapeDtypeStruct((z,),F32) for z in sizes],
-      compiler_params=pltpu.CompilerParams(vmem_limit_bytes=63*2**20),name="widen")(where,chunks,heads,mine,got,vec,tok)
+      compiler_params=pltpu.CompilerParams(vmem_limit_bytes=63*2**20),name="widen")(chunks,heads,mine,got,vec,tok)
     return res[:7],res[7:]
 
 def front_kernel(tok,w,b,gain,shift,seg,x_o,normT_o,q_o,k_o,v_o,wh_o,mq_o,mk_o,x,norm,normT,qkv,wh,wgot,bgot,bias,mq,mk,tsem,bsem,csem,ysem,xsem,zsem,osem):
@@ -689,7 +690,7 @@
     b_down,
     cotangent,
 ):
-    th, tw = lax.axis_index("th"), lax.axis_index("tw")
+    tw = lax.axis_index("tw")
     x, normed_t, query, key, value, w_heads, mq, mk = front(
         tokens, w_qkv.transpose(0, 2, 1), b_qv, norm1_gain, norm1_shift, segment_ids
     )
@@ -706,9 +707,8 @@
     chunks, heads, small, grad_tokens = finish(
         dp_size, red, dq, dk, dv, normed_t, w_heads, grad_w_out, x, grad_middle, norm1_gain, sums, grad_b_up
     )
-    where = jnp.stack([tw, 2 * th + tw]).astype(jnp.int32)
     (up, down, w_qkv_grad, w_out_grad, block_out, grad_tokens, b_qv_grad), vecs = widen(
-        where, chunks, heads, out_mine, out_got, small, grad_tokens
+        chunks, heads, out_mine, out_got, small, grad_tokens
     )
     return (
         block_out,

time: 240 us -> 240 us (level)
  waiting for transfers between devices: 3.23 us -> 0.01 us
  Pallas kernels: 230 us -> 233 us
    pallas_call x1, Pallas kernels: 81.8 us -> 75.8 us  [finish(): pl.pallas_call(functools.partial(finish_kernel, dp), in_specs=[pl.BlockSp...]
    pallas_call x1, Pallas kernels: 23.4 us -> 28.4 us  [attn_bwd(): pl.pallas_call(bwd_kernel, grid_spec=pltpu.PrefetchScalarGridSpec(num_sca...]
    pallas_call x1, Pallas kernels: 16.1 us -> 19.9 us  [attn_fwd(): pl.pallas_call(fwd_kernel, grid_spec=pltpu.PrefetchScalarGridSpec(num_sca...]
    ppermute x3, waiting for transfers between devices: 3.23 us -> 0.01 us  [swap(): return lax.ppermute(value, axis, SWAP)]
  transfers between devices with their start and end apart: 3 -> 3, of which waited for: 1 -> 0; matrix products, arithmetic and copies ran while one was open for 1% -> 0% of each run, Pallas kernels for 50% -> 52%
where the time goes in v6:
time: 240 us
  Pallas kernels  233 us (97%)
  starting transfers between devices  3.56 us (1%)
    pallas_call x1, Pallas kernels, finish(): pl.pallas_call(functools.partial(finish_kernel, dp), in_specs=[pl.BlockSp...  75.8 us
    pallas_call x1, Pallas kernels, ffn(): pl.pallas_call(functools.partial(ffn_kernel, dp), in_specs=[whole(v.shape...  61.4 us
    pallas_call x1, Pallas kernels, front(): pl.pallas_call(front_kernel, in_specs=[pl.BlockSpec(memory_space=pltpu.VM...  33.1 us
    pallas_call x1, Pallas kernels, attn_bwd(): pl.pallas_call(bwd_kernel, grid_spec=pltpu.PrefetchScalarGridSpec(num_sca...  28.4 us
    pallas_call x1, Pallas kernels, attn_fwd(): pl.pallas_call(fwd_kernel, grid_spec=pltpu.PrefetchScalarGridSpec(num_sca...  19.9 us
    pallas_call x1, Pallas kernels, widen(): pl.pallas_call(widen_kernel, grid=(CH,), in_specs=[pl.BlockSpec((None, 2,...  14.6 us
  transfers between devices with their start and end apart: 3, of which 0 were waited for; matrix products, arithmetic and copies ran while one was open for 0% of the time, Pallas kernels for 52%

profile of v6, /device:TPU:0, one launch (start us, length us, event | category | flops | bytes accessed | tf_op | source)
XLA Modules:
  0.0 240.3 jit_solution(13640208947655813193)
XLA Ops:
  0.6 0.0 copy-start
  0.7 0.0 copy-start.2
  0.7 0.0 copy-start.4
  0.7 33.1 %front.1 = (bf16[768,768]{1,0:T(8,128)(2,1)}, bf16[768,1536]{1,0:T(8,128)(2,1)}, bf16[1536,384]{1,0:T(8,128)(2,1)}, bf16[1536,384]{1,0:T(8,128)(2,1)}, bf16[1536...) custom-call(bf16[2,384,768]{2,1,0:T(8,128)(2,1)} %tok.1, ...), custom_call_target="tpu_custom_call" | custom-call | tf_op jit(solution)/shard_map/front/pallas_call | solution.py:660
  33.8 0.0 copy-done
  33.9 0.7 collective-permute-start.1
  34.6 0.0 copy-done.2
  34.6 1.4 collective-permute-start
  36.0 0.1 slice.7
  36.1 0.1 slice.6
  36.2 0.2 convert_reduce_fusion
  36.4 0.5 and_select_fusion
  36.9 19.9 %attention_forward.1 = (bf16[1536,384]{1,0:T(8,128)(2,1)}, f32[8,1536]{1,0:T(8,128)}) custom-call(s32[6]{0:T(128)} %get-tuple-element.99.lo_ref, s32[6]{0:T(128)} %get-tuple-element.98.n_ref, bf16[1536,384]{1,0:T(8,128)(2,1)} %get-tuple-element.55.q_ref, bf16[1536,384]{1,0:T(8,128)(2,1)} %get-tuple-element.56.k_ref, ...), custom_call_target="tpu_custom_call" | custom-call | tf_op jit(solution)/shard_map/attention_forward/pallas_call | solution.py:64
  56.8 0.0 collective-permute-done.wo_got
  56.8 0.0 copy-start.3
  56.8 0.0 collective-permute-done.1.cot_got
  56.8 0.7 copy-done.3
  57.5 61.4 %feed_forward.1 = (bf16[384,768]{1,0:T(8,128)(2,1)}, bf16[384,768]{1,0:T(8,128)(2,1)}, f32[768,768]{1,0:T(8,128)}, f32[1,3072]{1,0:T(1,128)}, f32[8,768]{1,0:T(8...) custom-call(bf16[1536,384]{1,0:T(8,128)(2,1)} %get-tuple-element.60.att.o_ref, ...), custom_call_target="tpu_custom_call" | custom-call | tf_op jit(solution)/shard_map/feed_forward/pallas_call | solution.py:372
  119.0 1.5 collective-permute-start.2
  120.5 28.4 %attention_backward.1 = (bf16[1536,384]{1,0:T(8,128)(2,1)}, bf16[1536,384]{1,0:T(8,128)(2,1)}, bf16[1536,384]{1,0:T(8,128)(2,1)}) custom-call(s32[6]{0:T(128)} %get-tuple-element.99.lo_ref, s32[6]{0:T(128)} %get-tuple-element.98.n_ref, bf16[1536,384]{1,0:T(8,128)(2,1)} %get-tuple-element.55.q_ref, bf16[1536,384]{1,0:T(8,128)(2,1)} %get-tuple-element.56.k_ref, ...), custom_call_target="tpu_custom_call" | custom-call | tf_op jit(solution)/shard_map/attention_backward/pallas_call | solution.py:128
  148.9 75.8 %finish_gradients.1 = (bf16[6,2,3072,128]{3,2,1,0:T(8,128)(2,1)}, bf16[3,1536,128]{2,1,0:T(8,128)(2,1)}, f32[76,128]{1,0:T(8,128)}, bf16[2,384,768]{2,1,0:T(8,128)(2,1)}) custom-call(bf16[6,192,128]{2,1,0:T(8,128)(2,1)} %get-tuple-element.64.red, bf16[1536,384]{1,0:T(8,128)(2,1)} %get-tuple-element.67.dq_h, bf16[1536,384]{1,0:T(8,128)(2,1)} %get-tuple-element.68.dk_h, ...), custom_call_target="tpu_custom_call" | custom-call | tf_op jit(solution)/shard_map/finish_gradients/pallas_call | solution.py:528
  224.7 0.0 collective-permute-done.2.got
  224.7 0.8 copy-done.1
  225.5 14.6 %widen.1 = (f32[768,3072]{1,0:T(8,128)}, f32[3072,768]{1,0:T(8,128)}, f32[3,192,768]{2,1,0:T(8,128)}, f32[192,768]{1,0:T(8,128)}, bf16[2,384,768]{2,1,0:T(8,128)...) custom-call(bf16[6,2,3072,128]{3,2,1,0:T(8,128)(2,1)} %get-tuple-ele, ...), custom_call_target="tpu_custom_call" | custom-call | tf_op jit(solution)/shard_map/widen/pallas_call | solution.py:563
  (4 shorter events, 0.1 us)
Async XLA Ops:
  0.6 33.1 %copy-start = (bf16[2,384,768]{2,1,0:T(8,128)(2,1)S(1)}, bf16[2,384,768]{2,1,0:T(8,128)(2,1)}, u32[]{:S(2)}) copy-start(bf16[2,384,768]{2,1,0:T(8,128)(2,1)} %cot_h.1) | copy-start | bytes 3538948
  0.7 33.9 %copy-start.2 = (bf16[192,768]{1,0:T(8,128)(2,1)S(1)}, bf16[192,768]{1,0:T(8,128)(2,1)}, u32[]{:S(2)}) copy-start(bf16[192,768]{1,0:T(8,128)(2,1)} %wo_h.1) | copy-start | bytes 884740
  0.7 35.3 %copy-start.4 = (s32[2,1536]{1,0:T(2,128)S(1)}, s32[2,1536]{1,0:T(2,128)}, u32[]{:S(2)}) copy-start(s32[2,1536]{1,0:T(2,128)} %seg.1) | copy-start | bytes 36868
  33.9 23.0 %collective-permute-start.1 = (bf16[384,768]{1,0:T(8,128)(2,1)S(1)}, bf16[384,768]{1,0:T(8,128)(2,1)}, u32[]{:S(2)}, u32[]{:S(2)}) collective-permute-start(bf16[384,768]{1,0:T(8,128)(2,1)S(1)} %dynamic-slice_bitcast_fusion), channel_id=1, source_target_pairs={{0,1},{1,0},{2,3},{3,2},{4,5},{5,4},{6,7},{7,6},{8,9},{9,8},{10,11... | collective-permute-start | bytes 1769480 | tf_op jit(solution)/shard_map/ppermute | solution.py:672
  34.6 22.2 %collective-permute-start = (bf16[192,768]{1,0:T(8,128)(2,1)S(1)}, bf16[192,768]{1,0:T(8,128)(2,1)S(1)}, u32[]{:S(2)}, u32[]{:S(2)}) collective-permute-start(bf16[192,768]{1,0:T(8,128)(2,1)S(1)} %copy-done.2), channel_id=1, source_target_pairs={{0,1},{1,0},{2,3},{3,2},{4,5},{5,4},{6,7},{7,6},{8,9},{9,8},{10,11... | collective-permute-start | bytes 884744 | tf_op jit(solution)/shard_map/ppermute | solution.py:672
  56.8 0.7 copy-start.3
  119.0 105.7 %collective-permute-start.2 = (bf16[384,768]{1,0:T(8,128)(2,1)}, bf16[384,768]{1,0:T(8,128)(2,1)S(1)}, u32[]{:S(2)}, u32[]{:S(2)}) collective-permute-start(bf16[384,768]{1,0:T(8,128)(2,1)} %get-tuple-element.79), channel_id=1, source_target_pairs={{0,1},{1,0},{2,3},{3,2},{4,5},{5,4},{6,7},{7,6},{8,9},{9,8},{10,11... | collective-permute-start | bytes 1769480 | tf_op jit(solution)/shard_map/ppermute | solution.py:672
  224.7 0.8 copy-start.1

commit v7 on v6

--- a/solution.py
+++ b/solution.py
@@ -534,21 +534,21 @@
       compiler_params=pltpu.CompilerParams(vmem_limit_bytes=60*2**20,collective_id=1,has_side_effects=True),name="finish_gradients")(*args)
 
 def widen_kernel(chunk,heads,mine,got,vec,tok,wup,wdown,wqkv,wout,blk,tok_o,bqv,*vectors):
-    D=wup.shape[0]; q=wout.shape[0]; g=pl.program_id(0); HT=D//heads.shape[0]
+    D=wup.shape[0]; q=wout.shape[0]; g=pl.program_id(0); HT=wout.shape[1]
     for i in range(FC//128):
         cols=slice(i*128,(i+1)*128)
         wup[:,cols]=chunk[0,i*D:(i+1)*D,:].astype(F32)
         wdown[cols,:]=chunk[1,i*D:(i+1)*D,:].T.astype(F32)
+    @pl.when(g<D//HT)
+    def _():
+        y=jnp.concatenate([heads[i*HT:(i+1)*HT,:] for i in range(heads.shape[0]//HT)],1).T.astype(F32)
+        for c in range(3): wqkv[c]=y[c*q:(c+1)*q,:]
+        wout[...]=y[3*q:,:]
+    th,tw=lax.axis_index("th"),lax.axis_index("tw")
+    blk[tw]=mine[...]; blk[1-tw]=got[...]
+    tok_o[...]=tok[...]
     @pl.when(g==0)
     def _():
-        for t in range(heads.shape[0]):
-            y=jnp.concatenate([heads[t,i*HT:(i+1)*HT,:] for i in range(heads.shape[1]//HT)],1).T.astype(F32)
-            rr=slice(t*HT,(t+1)*HT)
-            for c in range(3): wqkv[c,:,rr]=y[c*q:(c+1)*q,:]
-            wout[:,rr]=y[3*q:,:]
-        th,tw=lax.axis_index("th"),lax.axis_index("tw")
-        blk[tw]=mine[...]; blk[1-tw]=got[...]
-        tok_o[...]=tok[...]
         at=sum(v.shape[0] for v in vectors)//128
         for i in range(2):
             for z,w in ((0,128),(1,q-128)): bqv[i:i+1,z*128:z*128+w]=vec[pl.ds(at+4*(2*th+tw)+2*i+z,1),0:w]
@@ -560,9 +560,12 @@
 def widen(chunks,heads,mine,got,vec,tok):
     CH,_,R,_=chunks.shape; D=R*128//FC; FF=CH*FC; q=heads.shape[0]*heads.shape[1]*128//(4*D); T2=mine.shape[0]
     outs=[(D,FF),(FF,D),(3,q,D),(q,D)]; sizes=[D]*6+[FF]
+    NH=heads.shape[0]; tile=lambda g: jnp.minimum(g,NH-1)
     res=pl.pallas_call(widen_kernel,grid=(CH,),
-      in_specs=[pl.BlockSpec((None,2,R,128),lambda g:(g,0,0,0))]+[pl.BlockSpec(a.shape,lambda g,n=a.ndim:(0,)*n) for a in (heads,mine,got,vec,tok)],
-      out_specs=[pl.BlockSpec((D,FC),lambda g:(0,g)),pl.BlockSpec((FC,D),lambda g:(g,0))]+[pl.BlockSpec(memory_space=pltpu.VMEM)]*(5+len(sizes)),
+      in_specs=[pl.BlockSpec((None,2,R,128),lambda g:(g,0,0,0))]+[pl.BlockSpec((None,)+heads.shape[1:],lambda g:(tile(g),0,0)),pl.BlockSpec((T2//CH,D),lambda g:(g,0)),pl.BlockSpec((T2//CH,D),lambda g:(g,0)),
+        pl.BlockSpec(vec.shape,lambda g:(0,0)),pl.BlockSpec((2,T2//CH,D),lambda g:(0,g,0))],
+      out_specs=[pl.BlockSpec((D,FC),lambda g:(0,g)),pl.BlockSpec((FC,D),lambda g:(g,0))]+[pl.BlockSpec((3,q,D//NH),lambda g:(0,0,tile(g))),pl.BlockSpec((q,D//NH),lambda g:(0,tile(g)))]
+        +[pl.BlockSpec((2,T2//CH,D),lambda g:(0,g,0))]*2+[pl.BlockSpec(memory_space=pltpu.VMEM)]*(1+len(sizes)),
       out_shape=[jax.ShapeDtypeStruct(o,F32) for o in outs]+[jax.ShapeDtypeStruct((2,T2,D),BF)]*2+[jax.ShapeDtypeStruct((2,q),F32)]+[jax.ShapeDtypeStruct((z,),F32) for z in sizes],
       compiler_params=pltpu.CompilerParams(vmem_limit_bytes=63*2**20),name="widen")(chunks,heads,mine,got,vec,tok)
     return res[:7],res[7:]

time: 240 us -> 239 us (level)
  no operation moved by 1% of the time
where the time goes in v7:
time: 239 us
  Pallas kernels  231 us (97%)
  starting transfers between devices  4.21 us (2%)
    pallas_call x1, Pallas kernels, finish(): pl.pallas_call(functools.partial(finish_kernel, dp), in_specs=[pl.BlockSp...  76.5 us
    pallas_call x1, Pallas kernels, ffn(): pl.pallas_call(functools.partial(ffn_kernel, dp), in_specs=[whole(v.shape...  60.4 us
    pallas_call x1, Pallas kernels, front(): pl.pallas_call(front_kernel, in_specs=[pl.BlockSpec(memory_space=pltpu.VM...  33.1 us
    pallas_call x1, Pallas kernels, attn_bwd(): pl.pallas_call(bwd_kernel, grid_spec=pltpu.PrefetchScalarGridSpec(num_sca...  28.2 us
    pallas_call x1, Pallas kernels, attn_fwd(): pl.pallas_call(fwd_kernel, grid_spec=pltpu.PrefetchScalarGridSpec(num_sca...  19.6 us
    pallas_call x1, Pallas kernels, widen(): pl.pallas_call(widen_kernel, grid=(CH,), in_specs=[pl.BlockSpec((None, 2,...  13.7 us
  transfers between devices with their start and end apart: 3, of which 0 were waited for; matrix products, arithmetic and copies ran while one was open for 0% of the time, Pallas kernels for 52%

profile of v7, /device:TPU:0, one launch (start us, length us, event | category | flops | bytes accessed | tf_op | source)
XLA Modules:
  0.0 239.1 jit_solution(9806560674217733138)
XLA Ops:
  0.6 0.0 copy-start
  0.7 0.0 copy-start.2
  0.7 0.0 copy-start.4
  0.7 33.1 %front.1 = (bf16[768,768]{1,0:T(8,128)(2,1)}, bf16[768,1536]{1,0:T(8,128)(2,1)}, bf16[1536,384]{1,0:T(8,128)(2,1)}, bf16[1536,384]{1,0:T(8,128)(2,1)}, bf16[1536...) custom-call(bf16[2,384,768]{2,1,0:T(8,128)(2,1)} %tok.1, ...), custom_call_target="tpu_custom_call" | custom-call | tf_op jit(solution)/shard_map/front/pallas_call | solution.py:663
  33.8 0.0 copy-done
  33.9 0.7 collective-permute-start.1
  34.6 0.0 copy-done.2
  34.6 1.4 collective-permute-start
  36.0 0.1 slice.7
  36.1 0.1 slice.6
  36.2 0.2 convert_reduce_fusion
  36.4 0.5 and_select_fusion
  36.9 19.6 %attention_forward.1 = (bf16[1536,384]{1,0:T(8,128)(2,1)}, f32[8,1536]{1,0:T(8,128)}) custom-call(s32[6]{0:T(128)} %get-tuple-element.99.lo_ref, s32[6]{0:T(128)} %get-tuple-element.98.n_ref, bf16[1536,384]{1,0:T(8,128)(2,1)} %get-tuple-element.55.q_ref, bf16[1536,384]{1,0:T(8,128)(2,1)} %get-tuple-element.56.k_ref, ...), custom_call_target="tpu_custom_call" | custom-call | tf_op jit(solution)/shard_map/attention_forward/pallas_call | solution.py:64
  56.5 0.0 collective-permute-done.wo_got
  56.5 0.0 copy-start.3
  56.6 0.0 collective-permute-done.1.cot_got
  56.6 0.7 copy-done.3
  57.3 60.4 %feed_forward.1 = (bf16[384,768]{1,0:T(8,128)(2,1)}, bf16[384,768]{1,0:T(8,128)(2,1)}, f32[768,768]{1,0:T(8,128)}, f32[1,3072]{1,0:T(1,128)}, f32[8,768]{1,0:T(8...) custom-call(bf16[1536,384]{1,0:T(8,128)(2,1)} %get-tuple-element.60.att.o_ref, ...), custom_call_target="tpu_custom_call" | custom-call | tf_op jit(solution)/shard_map/feed_forward/pallas_call | solution.py:372
  117.6 2.1 collective-permute-start.2
  119.8 28.2 %attention_backward.1 = (bf16[1536,384]{1,0:T(8,128)(2,1)}, bf16[1536,384]{1,0:T(8,128)(2,1)}, bf16[1536,384]{1,0:T(8,128)(2,1)}) custom-call(s32[6]{0:T(128)} %get-tuple-element.99.lo_ref, s32[6]{0:T(128)} %get-tuple-element.98.n_ref, bf16[1536,384]{1,0:T(8,128)(2,1)} %get-tuple-element.55.q_ref, bf16[1536,384]{1,0:T(8,128)(2,1)} %get-tuple-element.56.k_ref, ...), custom_call_target="tpu_custom_call" | custom-call | tf_op jit(solution)/shard_map/attention_backward/pallas_call | solution.py:128
  147.9 76.5 %finish_gradients.1 = (bf16[6,2,3072,128]{3,2,1,0:T(8,128)(2,1)}, bf16[3,1536,128]{2,1,0:T(8,128)(2,1)}, f32[76,128]{1,0:T(8,128)}, bf16[2,384,768]{2,1,0:T(8,128)(2,1)}) custom-call(bf16[6,192,128]{2,1,0:T(8,128)(2,1)} %get-tuple-element.64.red, bf16[1536,384]{1,0:T(8,128)(2,1)} %get-tuple-element.67.dq_h, bf16[1536,384]{1,0:T(8,128)(2,1)} %get-tuple-element.68.dk_h, ...), custom_call_target="tpu_custom_call" | custom-call | tf_op jit(solution)/shard_map/finish_gradients/pallas_call | solution.py:528
  224.4 0.0 collective-permute-done.2.got
  224.4 0.8 copy-done.1
  225.3 13.7 %widen.1 = (f32[768,3072]{1,0:T(8,128)}, f32[3072,768]{1,0:T(8,128)}, f32[3,192,768]{2,1,0:T(8,128)}, f32[192,768]{1,0:T(8,128)}, bf16[2,384,768]{2,1,0:T(8,128)...) custom-call(bf16[6,2,3072,128]{3,2,1,0:T(8,128)(2,1)} %get-tuple-ele, ...), custom_call_target="tpu_custom_call" | custom-call | tf_op jit(solution)/shard_map/widen/pallas_call | solution.py:564
  (4 shorter events, 0.1 us)
Async XLA Ops:
  0.6 33.1 %copy-start = (bf16[2,384,768]{2,1,0:T(8,128)(2,1)S(1)}, bf16[2,384,768]{2,1,0:T(8,128)(2,1)}, u32[]{:S(2)}) copy-start(bf16[2,384,768]{2,1,0:T(8,128)(2,1)} %cot_h.1) | copy-start | bytes 3538948
  0.7 33.9 %copy-start.2 = (bf16[192,768]{1,0:T(8,128)(2,1)S(1)}, bf16[192,768]{1,0:T(8,128)(2,1)}, u32[]{:S(2)}) copy-start(bf16[192,768]{1,0:T(8,128)(2,1)} %wo_h.1) | copy-start | bytes 884740
  0.7 35.3 %copy-start.4 = (s32[2,1536]{1,0:T(2,128)S(1)}, s32[2,1536]{1,0:T(2,128)}, u32[]{:S(2)}) copy-start(s32[2,1536]{1,0:T(2,128)} %seg.1) | copy-start | bytes 36868
  33.9 22.7 %collective-permute-start.1 = (bf16[384,768]{1,0:T(8,128)(2,1)S(1)}, bf16[384,768]{1,0:T(8,128)(2,1)}, u32[]{:S(2)}, u32[]{:S(2)}) collective-permute-start(bf16[384,768]{1,0:T(8,128)(2,1)S(1)} %dynamic-slice_bitcast_fusion), channel_id=1, source_target_pairs={{0,1},{1,0},{2,3},{3,2},{4,5},{5,4},{6,7},{7,6},{8,9},{9,8},{10,11... | collective-permute-start | bytes 1769480 | tf_op jit(solution)/shard_map/ppermute | solution.py:675
  34.6 22.0 %collective-permute-start = (bf16[192,768]{1,0:T(8,128)(2,1)S(1)}, bf16[192,768]{1,0:T(8,128)(2,1)S(1)}, u32[]{:S(2)}, u32[]{:S(2)}) collective-permute-start(bf16[192,768]{1,0:T(8,128)(2,1)S(1)} %copy-done.2), channel_id=1, source_target_pairs={{0,1},{1,0},{2,3},{3,2},{4,5},{5,4},{6,7},{7,6},{8,9},{9,8},{10,11... | collective-permute-start | bytes 884744 | tf_op jit(solution)/shard_map/ppermute | solution.py:675
  56.5 0.7 copy-start.3
  117.6 106.8 %collective-permute-start.2 = (bf16[384,768]{1,0:T(8,128)(2,1)}, bf16[384,768]{1,0:T(8,128)(2,1)S(1)}, u32[]{:S(2)}, u32[]{:S(2)}) collective-permute-start(bf16[384,768]{1,0:T(8,128)(2,1)} %get-tuple-element.79), channel_id=1, source_target_pairs={{0,1},{1,0},{2,3},{3,2},{4,5},{5,4},{6,7},{7,6},{8,9},{9,8},{10,11... | collective-permute-start | bytes 1769480 | tf_op jit(solution)/shard_map/ppermute | solution.py:675
  224.4 0.8 copy-start.1
